TPU v7x, 32 devices: a whole 2x2x4 slice. The times are simulated.
32 devices in a mesh: grp: 4 (over z), sub: 8 (over y, x, core).
Axes of the slice: x: 2, y: 2, z: 4, core: 2. Of those that a mesh axis runs over, the one named last changes fastest.
Arguments:
- stiff_blocks: float32 [8, 128, 4, 128, 128], P('grp', 'sub'), may hold values from -0.25 to 0.25
- block_cols: int32 [8, 128, 4], P('grp', 'sub'), may hold values from 0 to 127, as said below
- live_blocks: int32 [8, 8], P('grp', 'sub'), may hold values from 1 to 16, as said below
- sub_diag: float32 [8, 16384], P('grp', 'sub'), may hold values from 0.05 to 1
- penalty: float32 [8, 1024], P('grp', 'sub'), may hold values from 0.5 to 4
- sub_load: float32 [8, 16384], P('grp', 'sub'), may hold values from -6 to 6
- iface_map: int32 [8, 1024], P('grp', 'sub'), may hold values from 0 to 262143
- global_load: float32 [1024, 256], P(('grp', 'sub')), may hold values from -6 to 6
- global_diag: float32 [1024, 256], P(('grp', 'sub')), may hold values from 0.1 to 1
Outputs:
- global_field: float32 [1024, 256], P(('grp', 'sub'))
- sub_field: float32 [8, 16384], P('grp', 'sub')
Inputs may be any that keep to these rules, and one draw needn't show every extreme that they name: `live_blocks`: every live count is at least 1 and at most 16; the first submodel holds 16 live block rows on index 0 of sub. `block_cols`: among the blocks of one submodel's block rows on one index of sub, at most 8 have their column block among the block rows of any one index of sub; in every submodel some index of sub receives exactly 8 such blocks from every index of sub.
All inputs are finite; a program needn't handle non-finite values.
Results may differ from a plain program's by a relative error of at most 0.0003.
Values sent between devices are 32-bit elements; how exact they have to be, the bound alone decides.
No kernel may reach another device: no remote copies, remote signals or barrier semaphores. Data moves between devices by JAX's collectives and lax.ppermute only.
A program may use at most 64 MiB of HBM per device.

v0:
```python
import jax
import jax.numpy as jnp
from jax import lax
from jax.sharding import PartitionSpec as P

CG_STEPS = 2
COUPLE = 2
CAP = 8


HIGH = lax.Precision.HIGHEST


def with_halo(x, sides, width):
    for axis, dim in sides:
        peers, length = (lax.axis_size(axis), x.shape[dim])
        up = [(i, (i + 1) % peers) for i in range(peers - 1)]
        down = [(j, i) for i, j in up]
        last = lax.slice_in_dim(x, length - width, length, axis=dim)
        first = lax.slice_in_dim(x, 0, width, axis=dim)
        before = lax.ppermute(last, axis, up)
        after = lax.ppermute(first, axis, down)
        x = jnp.concatenate([before, x, after], axis=dim)
    return x


def glob_apply(field, gdiag):
    padded = with_halo(field, ((("grp", "sub"), 0),), 1)
    padded = jnp.pad(padded, ((0, 0), (1, 1)))
    beside = padded[2:, 1:-1] + padded[:-2, 1:-1] + padded[1:-1, 2:] + padded[1:-1, :-2]
    return (4.0 + gdiag) * field - beside


def row_sum(left, right):
    return jnp.sum(left * right, axis=1, keepdims=True)


def body(
    stiff_blocks,
    block_cols,
    live_blocks,
    sub_diag,
    penalty,
    sub_load,
    iface_map,
    global_load,
    global_diag,
):
    slots = stiff_blocks.shape[0]
    block_rows = stiff_blocks.shape[1]
    width = stiff_blocks.shape[3]
    rows_dev = block_rows * width
    gx_rows, gy_cols = global_load.shape
    glob_local = gx_rows * gy_cols
    groups_sub = lax.axis_size("sub")
    me_flat = lax.axis_index("grp") * groups_sub + lax.axis_index("sub")
    blocks = jnp.arange(rows_dev, dtype=jnp.int32) // width
    mask = (blocks[None, :] < live_blocks).astype(jnp.float32)
    pen_full = jnp.concatenate([penalty, jnp.zeros((slots, rows_dev - width), jnp.float32)], axis=1)
    dsum = sub_diag + pen_full
    flat_cols = block_cols.reshape(slots, -1)
    owner_of = flat_cols // block_rows
    local_of = flat_cols % block_rows
    owner_hot = (owner_of[..., None] == jnp.arange(groups_sub, dtype=jnp.int32)).astype(jnp.int32)
    earlier = jnp.cumsum(owner_hot, axis=1) - owner_hot
    rank_of = jnp.sum(earlier * owner_hot, axis=2)
    bucket_of = owner_of * CAP + rank_of
    placing = (bucket_of[..., None] == jnp.arange(groups_sub * CAP, dtype=jnp.int32)).astype(
        jnp.float32
    )
    send_ids = jnp.einsum("sqk,sq->sk", placing, (local_of + 1).astype(jnp.float32), precision=HIGH)
    send_ids = send_ids.reshape(slots, groups_sub, CAP)

    def sub_apply(vector):
        whole = lax.all_gather(vector, "sub", axis=1, tiled=True)
        tiles = whole.reshape(slots, -1, width)
        picked = jax.vmap(lambda table, index: table[index])(tiles, block_cols)
        strain = jnp.einsum("srnij,srnj->sri", stiff_blocks, picked, precision=HIGH)
        terms = jnp.einsum("srnij,sri->srnj", stiff_blocks, strain, precision=HIGH)
        targets = jnp.arange(block_rows * lax.axis_size("sub"), dtype=jnp.int32)
        onehot = (block_cols[..., None] == targets).astype(jnp.float32)
        back = lax.psum_scatter(
            jnp.einsum("srnm,srnj->msj", onehot, terms, precision=HIGH),
            "sub",
            scatter_dimension=0,
            tiled=True,
        )
        back = jnp.transpose(back, (1, 0, 2)).reshape(slots, rows_dev)
        return mask * (dsum * vector + back)

    all_map = lax.all_gather(iface_map, ("grp", "sub"), axis=0, tiled=True)
    local_idx = all_map - me_flat * glob_local
    valid = (local_idx >= 0) & (local_idx < glob_local)
    seg_idx = jnp.where(valid, local_idx, glob_local)
    global_field = jnp.zeros_like(global_load)
    sub_field = jnp.zeros_like(sub_load)
    for outer in range(COUPLE):
        if outer == 0:
            bvals = jnp.zeros_like(penalty)
        else:
            whole_field = lax.all_gather(global_field, ("grp", "sub"), axis=0, tiled=True)
            bvals = whole_field.reshape(-1)[iface_map]
        b_full = jnp.concatenate([bvals, jnp.zeros((slots, rows_dev - width), jnp.float32)], axis=1)
        rhs = mask * (sub_load + pen_full * b_full)
        field = sub_field
        if outer == 0:
            resid = rhs
        else:
            resid = rhs - sub_apply(field)

        def norm_sum(vector):
            return lax.psum(row_sum(vector, vector), "sub")

        direction = resid
        norm_now = norm_sum(resid)
        for step in range(CG_STEPS):
            image = sub_apply(direction)
            alpha = norm_now / lax.psum(row_sum(direction, image), "sub")
            field = field + alpha * direction
            resid = resid - alpha * image
            if step + 1 < CG_STEPS:
                norm_next = norm_sum(resid)
                direction = resid + norm_next / norm_now * direction
                norm_now = norm_next
        sub_field = field
        lam = penalty * (sub_field[:, :width] - bvals)
        lam_all = lax.all_gather(lam, ("grp", "sub"), axis=0, tiled=True)
        lam_g = jax.ops.segment_sum(
            lam_all.reshape(-1), seg_idx.reshape(-1), num_segments=glob_local + 1
        )
        lam_g = lam_g[:glob_local].reshape(gx_rows, gy_cols)
        if outer == 0:
            resid_g = global_load + lam_g
        else:
            resid_g = global_load - glob_apply(global_field, global_diag) + lam_g
        image_g = glob_apply(resid_g, global_diag)
        top, bottom = lax.psum(
            (jnp.sum(resid_g * resid_g), jnp.sum(resid_g * image_g)), ("grp", "sub")
        )
        global_field = global_field + top / bottom * resid_g
    return (global_field, sub_field)


def solution(mesh):
    return jax.shard_map(
        body,
        mesh=mesh,
        in_specs=(
            P("grp", "sub", None, None, None),
            P("grp", "sub", None),
            P("grp", "sub"),
            P("grp", "sub"),
            P("grp", "sub"),
            P("grp", "sub"),
            P("grp", "sub"),
            P(("grp", "sub"), None),
            P(("grp", "sub"), None),
        ),
        out_specs=(P(("grp", "sub"), None), P("grp", "sub")),
        check_vma=False,
    )
```

profile of v0, /device:TPU:0, one launch (start us, length us, event | category | flops | bytes accessed | tf_op | source)
XLA Modules:
  0.0 801.8 jit_solution(16290601400072708618)
XLA Ops:
  8.9 10.7 %all_gather.28 = f32[2,16384]{1,0:T(2,128)S(1)} all-gather(f32[2,2048]{1,0:T(2,128)S(1)} %compare_select_fusion.6), channel_id=1, replica_groups=mesh['grp'=4,'sub'=8] {'sub'}, dimensions={1}, use_global_device_ids=true | all-gather | bytes 147456 | tf_op jit(solution)/shard_map/all_gather | solution.py:75
  20.9 10.1 %convolution_bitcast_fusion.9 = f32[2,16,128,1,1]{2,3,4,1,0:T(1,128)S(1)} fusion(f32[2,16,4,128,1]{3,4,2,1,0:T(1,128)S(1)} %bitcast.242, f32[2,16,4,128,128]{4,3,2,1,0:T(8,128)} %param.9), kind=kOutput, calls=%fused_computation.17 | convolution fusion | flops 25165824 | bytes 8470528 | tf_op jit(solution)/shard_map/srnij,srnj->sri/dot_general | solution.py:78
  36.2 40.8 %all-gather = s32[32,2,128]{2,1,0:T(2,128)S(1)} all-gather(s32[1,2,128]{2,1,0:T(2,128)S(1)} %bitcast.257), channel_id=1, replica_groups=mesh['grp'=4,'sub'=8] {'grp','sub'}, dimensions={0}, use_global_device_ids=true | all-gather | bytes 33792 | tf_op jit(solution)/shard_map/all_gather | solution.py:91
  78.3 11.2 %all-reduce.20.cloned.1.call-done = f32[128,2,128]{2,1,0:T(2,128)} async-done(((f32[128,2,128]{2,1,0:T(2,128)}), f32[128,2,128]{2,1,0:T(2,128)}) %all-reduce.20.cloned.1.call-update) | async-done | bytes 131088
  90.5 11.8 %all-reduce.13 = (f32[2,1]{0,1:T(1,128)S(1)}, f32[2,1]{0,1:T(1,128)S(1)}) all-reduce(f32[2,1]{0,1:T(1,128)S(1)} %bitcast.259, f32[2,1]{0,1:T(1,128)S(1)} %bitcast.258), channel_id=1, replica_groups=mesh['grp'=4,'sub'=8] {'sub'}, use_global_device_ids=true, to_apply=%region_1.2 | all-reduce | flops 4 | bytes 32 | tf_op jit(solution)/shard_map/psum | solution.py:112
  102.5 11.8 %psum.86 = f32[2,1]{0,1:T(1,128)S(1)} all-reduce(f32[2,1]{0,1:T(1,128)S(1)} %bitcast.264), channel_id=1, replica_groups=mesh['grp'=4,'sub'=8] {'sub'}, use_global_device_ids=true, to_apply=%region_6.7 | all-reduce | flops 2 | bytes 16 | tf_op jit(solution)/shard_map/psum | solution.py:112
  114.4 8.7 %all_gather.29 = f32[2,16384]{1,0:T(2,128)S(1)} all-gather(f32[2,2048]{1,0:T(2,128)S(1)} %multiply_add_fusion.4), channel_id=1, replica_groups=mesh['grp'=4,'sub'=8] {'sub'}, dimensions={1}, use_global_device_ids=true | all-gather | bytes 147456 | tf_op jit(solution)/shard_map/all_gather | solution.py:75
  124.4 9.2 %convolution_bitcast_fusion.8 = f32[2,16,128,1,1]{2,3,4,1,0:T(1,128)S(1)} fusion(f32[2,16,4,128,1]{3,4,2,1,0:T(1,128)S(1)} %bitcast.243, f32[2,16,4,128,128]{4,3,2,1,0:T(8,128)} %param.9), kind=kOutput, calls=%fused_computation.16 | convolution fusion | flops 25165824 | bytes 8470528 | tf_op jit(solution)/shard_map/srnij,srnj->sri/dot_general | solution.py:78
  133.6 6.4 fusion.54
  141.2 53.0 %all-reduce.22.cloned.1.call-done = f32[128,2,128]{2,1,0:T(2,128)} async-done(((f32[128,2,128]{2,1,0:T(2,128)}), f32[128,2,128]{2,1,0:T(2,128)}) %all-reduce.22.cloned.1.call-update) | async-done | bytes 131088
  195.1 11.8 %psum.87 = f32[2,1]{0,1:T(1,128)S(1)} all-reduce(f32[2,1]{0,1:T(1,128)S(1)} %bitcast.263), channel_id=1, replica_groups=mesh['grp'=4,'sub'=8] {'sub'}, use_global_device_ids=true, to_apply=%region_9.10 | all-reduce | flops 2 | bytes 16 | tf_op jit(solution)/shard_map/psum | solution.py:118
  207.0 38.4 %all-gather.1 = f32[32,2,128]{2,1,0:T(2,128)S(1)} all-gather(f32[1,2,128]{2,1,0:T(2,128)S(1)} %fusion.49), channel_id=1, replica_groups=mesh['grp'=4,'sub'=8] {'grp','sub'}, dimensions={0}, use_global_device_ids=true | all-gather | bytes 33792 | tf_op jit(solution)/shard_map/all_gather | solution.py:127
  245.4 55.4 %scatter_custom_fusion = f32[8193]{0:T(1024)S(1)} fusion(s32[8192]{0:T(1024)S(1)} %select_bitcast_fusion, f32[8192]{0:T(1024)S(1)} %bitcast.249, f32[]{:T(128)} %constant.41.clone.1), kind=kCustom, calls=%fused_computation.88 | custom fusion | flops 8192 | bytes 32776 | tf_op jit(solution)/shard_map/scatter-add | solution.py:128
  306.9 37.8 %all-reduce.11 = (f32[]{:T(128)}, f32[]{:T(128)}) all-reduce(f32[]{:T(128)} %get-tuple-element.5, f32[]{:T(128)} %get-tuple-element.4), channel_id=1, replica_groups=mesh['grp'=4,'sub'=8] {'grp','sub'}, use_global_device_ids=true, to_apply=%region_12.13 | all-reduce | flops 2 | bytes 16 | tf_op jit(solution)/shard_map/psum | solution.py:137
  346.7 10.4 %all_gather.32 = f32[2,16384]{1,0:T(2,128)S(1)} all-gather(f32[2,2048]{1,0:T(2,128)S(1)} %multiply_add_fusion.3), channel_id=1, replica_groups=mesh['grp'=4,'sub'=8] {'sub'}, dimensions={1}, use_global_device_ids=true | all-gather | bytes 147456 | tf_op jit(solution)/shard_map/all_gather | solution.py:75
  358.4 9.2 %convolution_bitcast_fusion.7 = f32[2,16,128,1,1]{2,3,4,1,0:T(1,128)S(1)} fusion(f32[2,16,4,128,1]{3,4,2,1,0:T(1,128)S(1)} %bitcast.244, f32[2,16,4,128,128]{4,3,2,1,0:T(8,128)} %param.9), kind=kOutput, calls=%fused_computation.15 | convolution fusion | flops 25165824 | bytes 8470528 | tf_op jit(solution)/shard_map/srnij,srnj->sri/dot_general | solution.py:78
  375.1 26.6 %all-gather.5.cloned.1.call-done = f32[1024,256]{1,0:T(8,128)} async-done(((f32[32,256]{1,0:T(8,128)}), f32[1024,256]{1,0:T(8,128)}) %all-gather.5.cloned.1.call-update) | async-done | bytes 1048592 | tf_op jit(solution)/shard_map/all_gather | solution.py:101
  405.2 51.3 %all-reduce.24.cloned.1.call-done = f32[128,2,128]{2,1,0:T(2,128)} async-done(((f32[128,2,128]{2,1,0:T(2,128)}), f32[128,2,128]{2,1,0:T(2,128)}) %all-reduce.24.cloned.1.call-update) | async-done | bytes 131088
  457.3 8.8 %all_gather.33 = f32[2,16384]{1,0:T(2,128)S(1)} all-gather(f32[2,2048]{1,0:T(2,128)S(1)} %fusion.35), channel_id=1, replica_groups=mesh['grp'=4,'sub'=8] {'sub'}, dimensions={1}, use_global_device_ids=true | all-gather | bytes 147456 | tf_op jit(solution)/shard_map/all_gather | solution.py:75
  467.4 9.2 %convolution_bitcast_fusion.6 = f32[2,16,128,1,1]{2,3,4,1,0:T(1,128)S(1)} fusion(f32[2,16,4,128,1]{3,4,2,1,0:T(1,128)S(1)} %bitcast.245, f32[2,16,4,128,128]{4,3,2,1,0:T(8,128)} %param.9), kind=kOutput, calls=%fused_computation.14 | convolution fusion | flops 25165824 | bytes 8470528 | tf_op jit(solution)/shard_map/srnij,srnj->sri/dot_general | solution.py:78
  476.6 6.4 fusion.56
  487.7 49.5 %all-reduce.26.cloned.1.call-done = f32[128,2,128]{2,1,0:T(2,128)} async-done(((f32[128,2,128]{2,1,0:T(2,128)}), f32[128,2,128]{2,1,0:T(2,128)}) %all-reduce.26.cloned.1.call-update) | async-done | bytes 131088
  538.1 11.8 %all-reduce.12 = (f32[2,1]{0,1:T(1,128)S(1)}, f32[2,1]{0,1:T(1,128)S(1)}) all-reduce(f32[2,1]{0,1:T(1,128)S(1)} %bitcast.261, f32[2,1]{0,1:T(1,128)S(1)} %bitcast.260), channel_id=1, replica_groups=mesh['grp'=4,'sub'=8] {'sub'}, use_global_device_ids=true, to_apply=%region_17.18 | all-reduce | flops 4 | bytes 32 | tf_op jit(solution)/shard_map/psum | solution.py:112
  550.1 11.8 %psum.92 = f32[2,1]{0,1:T(1,128)S(1)} all-reduce(f32[2,1]{0,1:T(1,128)S(1)} %bitcast.265), channel_id=1, replica_groups=mesh['grp'=4,'sub'=8] {'sub'}, use_global_device_ids=true, to_apply=%region_22.23 | all-reduce | flops 2 | bytes 16 | tf_op jit(solution)/shard_map/psum | solution.py:112
  562.0 8.9 %all_gather.34 = f32[2,16384]{1,0:T(2,128)S(1)} all-gather(f32[2,2048]{1,0:T(2,128)S(1)} %multiply_add_fusion.2), channel_id=1, replica_groups=mesh['grp'=4,'sub'=8] {'sub'}, dimensions={1}, use_global_device_ids=true | all-gather | bytes 147456 | tf_op jit(solution)/shard_map/all_gather | solution.py:75
  572.1 9.2 %convolution_bitcast_fusion.5 = f32[2,16,128,1,1]{2,3,4,1,0:T(1,128)S(1)} fusion(f32[2,16,4,128,1]{3,4,2,1,0:T(1,128)S(1)} %bitcast.241, f32[2,16,4,128,128]{4,3,2,1,0:T(8,128)} %param.9), kind=kOutput, calls=%fused_computation.13 | convolution fusion | flops 25165824 | bytes 8470528 | tf_op jit(solution)/shard_map/srnij,srnj->sri/dot_general | solution.py:78
  581.3 6.4 fusion.57
  588.9 53.0 %all-reduce.28.cloned.1.call-done = f32[128,2,128]{2,1,0:T(2,128)} async-done(((f32[128,2,128]{2,1,0:T(2,128)}), f32[128,2,128]{2,1,0:T(2,128)}) %all-reduce.28.cloned.1.call-update) | async-done | bytes 131088
  642.8 11.8 %psum.93 = f32[2,1]{0,1:T(1,128)S(1)} all-reduce(f32[2,1]{0,1:T(1,128)S(1)} %bitcast.262), channel_id=1, replica_groups=mesh['grp'=4,'sub'=8] {'sub'}, use_global_device_ids=true, to_apply=%region_25.26 | all-reduce | flops 2 | bytes 16 | tf_op jit(solution)/shard_map/psum | solution.py:118
  654.8 38.4 %all-gather.2 = f32[32,2,128]{2,1,0:T(2,128)S(1)} all-gather(f32[1,2,128]{2,1,0:T(2,128)S(1)} %fusion.48), channel_id=1, replica_groups=mesh['grp'=4,'sub'=8] {'grp','sub'}, dimensions={0}, use_global_device_ids=true | all-gather | bytes 33792 | tf_op jit(solution)/shard_map/all_gather | solution.py:127
  693.1 55.4 %scatter_custom_fusion.1 = f32[8193]{0:T(1024)S(1)} fusion(s32[8192]{0:T(1024)S(1)} %select_bitcast_fusion, f32[8192]{0:T(1024)S(1)} %bitcast.248, f32[]{:T(128)} %constant.41.clone.1), kind=kCustom, calls=%fused_computation.86 | custom fusion | flops 8192 | bytes 32776 | tf_op jit(solution)/shard_map/scatter-add | solution.py:128
  754.8 37.8 %all-reduce.10 = (f32[]{:T(128)}, f32[]{:T(128)}) all-reduce(f32[]{:T(128)} %get-tuple-element.3, f32[]{:T(128)} %get-tuple-element.2), channel_id=1, replica_groups=mesh['grp'=4,'sub'=8] {'grp','sub'}, use_global_device_ids=true, to_apply=%region_28.29 | all-reduce | flops 2 | bytes 16 | tf_op jit(solution)/shard_map/psum | solution.py:137
  (117 shorter events, 50.6 us)
Async XLA Ops:
  7.2 82.4 %all-reduce.20.cloned.1.call-start = ((), (), s32[]{:S(2)}) async-start(), calls=%async_computation.1 | async-start | bytes 262144
  20.8 10.2 %copy-start = (f32[2,16,4,128,128]{4,3,2,1,0:T(8,128)S(1)}, f32[2,16,4,128,128]{4,3,2,1,0:T(8,128)}, u32[]{:S(2)}) copy-start(f32[2,16,4,128,128]{4,3,2,1,0:T(8,128)} %param.9) | copy-start | bytes 25165828
  20.8 14.2 %copy-start.4 = (s32[2,16,4]{1,2,0:T(4,128)S(1)}, s32[2,16,4]{1,2,0:T(4,128)}, u32[]{:S(2)}) copy-start(s32[2,16,4]{1,2,0:T(4,128)} %param.10) | copy-start | bytes 1540
  20.9 15.4 %copy-start.10 = (s32[2,128]{1,0:T(2,128)S(1)}, s32[2,128]{1,0:T(2,128)}, u32[]{:S(2)}) copy-start(s32[2,128]{1,0:T(2,128)} %param.15) | copy-start | bytes 3076
  20.9 56.2 %copy-start.11 = (u32[32]{0:T(128)S(1)}, u32[32]{0:T(128)}, u32[]{:S(2)}) copy-start(u32[32]{0:T(128)} %constant.138) | copy-start | bytes 388
  20.9 68.7 %copy-start.2 = (f32[2,2048]{1,0:T(2,128)S(1)}, f32[2,2048]{1,0:T(2,128)}, u32[]{:S(2)}) copy-start(f32[2,2048]{1,0:T(2,128)} %param.12) | copy-start | bytes 49156
  20.9 68.6 %copy-start.6 = (f32[2,128]{1,0:T(2,128)S(1)}, f32[2,128]{1,0:T(2,128)}, u32[]{:S(2)}) copy-start(f32[2,128]{1,0:T(2,128)} %param.13) | copy-start | bytes 3076
  20.9 68.6 %copy-start.9 = (s32[2,1]{0,1:T(1,128)S(1)}, s32[2,1]{0,1:T(1,128)}, u32[]{:S(2)}) copy-start(s32[2,1]{0,1:T(1,128)} %param.11) | copy-start | bytes 28
  36.2 158.0 %all-reduce.22.cloned.1.call-start = ((), (), s32[]{:S(2)}) async-start(), calls=%async_computation.2 | async-start | bytes 262144
  124.4 176.4 %copy-start.5 = (f32[32,256]{1,0:T(8,128)S(1)}, f32[32,256]{1,0:T(8,128)}, u32[]{:S(2)}) copy-start(f32[32,256]{1,0:T(8,128)} %param.16) | copy-start | bytes 98308
  124.4 181.8 %copy-start.3 = (f32[32,256]{1,0:T(8,128)S(1)}, f32[32,256]{1,0:T(8,128)}, u32[]{:S(2)}) copy-start(f32[32,256]{1,0:T(8,128)} %param.17) | copy-start | bytes 98308
  141.1 260.6 %all-gather.5.cloned.1.call-start = ((), (), s32[]{:S(2)}) async-start(), calls=%async_computation | async-start | bytes 1081344 | tf_op jit(solution)/shard_map/all_gather | solution.py:101
  300.9 3.5 collective-permute-start.1
  303.0 3.0 collective-permute-start
  346.7 109.9 %all-reduce.24.cloned.1.call-start = ((), (), s32[]{:S(2)}) async-start(), calls=%async_computation.3 | async-start | bytes 262144
  358.3 98.2 %copy-start.7 = (f32[2,2048]{1,0:T(2,128)S(1)}, f32[2,2048]{1,0:T(2,128)}, u32[]{:S(2)}) copy-start(f32[2,2048]{1,0:T(2,128)} %param.14) | copy-start | bytes 49156
  375.0 162.1 %all-reduce.26.cloned.1.call-start = ((), (), s32[]{:S(2)}) async-start(), calls=%async_computation.4 | async-start | bytes 262144
  467.4 16.8 %copy-start.1 = (f32[32,256]{1,0:T(8,128)S(1)}, f32[32,256]{1,0:T(8,128)}, u32[]{:S(2)}) copy-start(f32[32,256]{1,0:T(8,128)} %broadcast_multiply_fusion) | copy-start | bytes 98308
  484.1 157.8 %all-reduce.28.cloned.1.call-start = ((), (), s32[]{:S(2)}) async-start(), calls=%async_computation.5 | async-start | bytes 262144
  484.1 104.7 %collective-permute-start.3 = (f32[1,256]{1,0:T(1,128)S(1)}, f32[1,256]{1,0:T(1,128)S(1)}, u32[]{:S(2)}, u32[]{:S(2)}) collective-permute-start(f32[1,256]{1,0:T(1,128)S(1)} %get-tuple-element.22), channel_id=1, source_target_pairs={{0,1},{1,2},{2,3},{3,4},{4,5},{5,6},{6,7},{7,8},{8,9},{9,10},{10,1... | collective-permute-start | bytes 3080 | tf_op jit(solution)/shard_map/ppermute | solution.py:21
  486.4 102.4 %collective-permute-start.2 = (f32[1,256]{1,0:T(1,128)S(1)}, f32[1,256]{1,0:T(1,128)S(1)}, u32[]{:S(2)}, u32[]{:S(2)}) collective-permute-start(f32[1,256]{1,0:T(1,128)S(1)} %get-tuple-element.23), channel_id=1, source_target_pairs={{1,0},{2,1},{3,2},{4,3},{5,4},{6,5},{7,6},{8,7},{9,8},{10,9},{11,1... | collective-permute-start | bytes 3080 | tf_op jit(solution)/shard_map/ppermute | solution.py:22
  654.7 139.7 %copy-start.8 = (f32[2,2048]{1,0:T(2,128)}, f32[2,2048]{1,0:T(2,128)S(1)}, u32[]{:S(2)}) copy-start(f32[2,2048]{1,0:T(2,128)S(1)} %multiply_add_fusion.1) | copy-start | bytes 49156
  748.7 3.5 collective-permute-start.5
  750.9 3.0 collective-permute-start.4
Sparse Core Ops, SparseCore 0:
  36.3 53.2 all-reduce.19
  141.2 52.9 all-reduce.21
  346.8 54.9 all-gather.4
  404.6 51.8 all-reduce.23
  484.2 52.9 all-reduce.25
  588.9 52.9 all-reduce.27
where the time goes:
time: 811 us; the launch traced here: 802 us
  blocking collectives  311 us (38%)
  waiting for transfers between devices  248 us (31%)
  other arithmetic  121 us (15%)
  matrix products  78.1 us (10%)
  between operations  18.4 us (2%)
  local copies, waits for them, and re-layouts  14.3 us (2%)
  starting transfers between devices  10.7 us (1%)
    unnamed x11, waiting for transfers between devices  218 us
    scatter-add x2, other arithmetic, body(): jax.ops.segment_sum(lam_all.reshape(-1), seg_idx.reshape(-1), num_segment...  111 us
    all_gather x2, blocking collectives, body(): lam_all = lax.all_gather(lam, ('grp', 'sub'), axis=0, tiled=True)  76.8 us
    psum x2, blocking collectives, body(): lax.psum((jnp.sum(resid_g * resid_g), jnp.sum(resid_g * image_g)), ('grp'...  75.6 us
    all_gather x5, blocking collectives, sub_apply(): whole = lax.all_gather(vector, 'sub', axis=1, tiled=True)  47.4 us
    psum x4, blocking collectives, norm_sum(): return lax.psum(row_sum(vector, vector), 'sub')  47.2 us
    dot_general x5, matrix products, sub_apply(): strain = jnp.einsum('srnij,srnj->sri', stiff_blocks, picked, precision=HIGH)  46.9 us
    all_gather x1, blocking collectives, body(): all_map = lax.all_gather(iface_map, ('grp', 'sub'), axis=0, tiled=True)  40.8 us
  transfers between devices with their start and end apart: 12, of which 8 were waited for; matrix products, arithmetic and copies ran while one was open for 5% of the time, Pallas kernels for 0%

commit v1 on v0

v1 whole, which is shorter than its diff:
```python
import jax
import jax.numpy as jnp
from jax import lax
from jax.experimental import pallas as pl
from jax.experimental.pallas import tpu as pltpu
from jax.sharding import PartitionSpec as P

F32 = jnp.float32
BF16 = jnp.bfloat16
EDGE = 8
ALL = ("grp", "sub")

VMEM = pl.BlockSpec(memory_space=pltpu.VMEM)
SMEM = pl.BlockSpec(memory_space=pltpu.SMEM)


def total(x):
    return jnp.sum(jnp.sum(x, axis=0, keepdims=True), axis=1, keepdims=True)


def split3(x):
    hi = x.astype(BF16)
    rest = x - hi.astype(F32)
    mid = rest.astype(BF16)
    return hi, mid, (rest - mid.astype(F32)).astype(BF16)


def iota(shape, dim):
    return lax.broadcasted_iota(jnp.int32, shape, dim)


def contract(stiff, cols, vector, terms):
    slots, block_rows, per_row, width, _ = stiff.shape
    squares = []
    for s in range(slots):

        def row(r, acc, s=s):
            prod = None
            for n in range(per_row):
                part = stiff[s, r, n] * vector(s, cols[s, r * per_row + n])
                prod = part if prod is None else prod + part
            strain = jnp.sum(prod, axis=1, keepdims=True)
            if terms is not None:
                for n in range(per_row):
                    terms[s, pl.ds(r * per_row + n, 1), :] = jnp.sum(
                        stiff[s, r, n] * strain, axis=0, keepdims=True
                    )
            return acc + strain * strain

        squares.append(lax.fori_loop(0, block_rows, row, jnp.zeros((width, 1), F32), unroll=2))
    return squares


def stacked(gathered, first, count):
    devices, slots = gathered.shape[:2]
    return jnp.concatenate(
        [gathered[d, s, first : first + count, :] for s in range(slots) for d in range(devices)],
        axis=0,
    )


def landed(pack, arrived, block_rows, count):
    devices, slots, _, width = pack.shape
    targets = slots * devices * block_rows
    source = jnp.concatenate(
        [arrived[d, s, :count, :] for d in range(devices) for s in range(slots)], axis=0
    )
    col = jnp.concatenate(
        [pack[d, 0, 2 * block_rows + 1 : 2 * block_rows + 2, :] for d in range(devices)], axis=1
    )
    hot = jnp.where(iota((targets, col.shape[1]), 0).astype(F32) == col, 1.0, 0.0).astype(BF16)
    out = jnp.dot(hot, jnp.concatenate(split3(source), axis=1), preferred_element_type=F32)
    return out[:, :width] + out[:, width : 2 * width] + out[:, 2 * width :]


def prep_kernel(live, diag, pen, load, cols, gload, gdiag, pack, up, down):
    slots, rows, width = pack.shape
    block_rows = (rows - 8) // 2
    pack[:, 2 * block_rows :, :] = jnp.zeros((slots, 8, width), F32)
    for s in range(slots):
        count = live[s, 0]
        for b in range(block_rows):
            lanes = pl.ds(b * width, width)
            on = b < count
            main = diag[s : s + 1, lanes]
            if b == 0:
                main = main + pen[s : s + 1, :]
            pack[s, b : b + 1, :] = jnp.where(on, load[s : s + 1, lanes], 0.0)
            pack[s, block_rows + b : block_rows + b + 1, :] = jnp.where(on, main, 0.0)
        pack[s, 2 * block_rows : 2 * block_rows + 1, :] = pen[s : s + 1, :]
    pack[0, 2 * block_rows + 1 : 2 * block_rows + 2, :] = cols[...]
    last = gload.shape[0]
    up[...] = jnp.zeros_like(up)
    down[...] = jnp.zeros_like(down)
    up[0:2, :] = gload[0:2, :]
    up[2:3, :] = gdiag[0:1, :]
    down[0:2, :] = gload[last - 2 : last, :]
    down[2:3, :] = gdiag[last - 1 : last, :]


def first_kernel(cols, pack, stiff, terms):
    block_rows = stiff.shape[1]

    def vector(s, c):
        return pack[lax.div(c, block_rows), s, pl.ds(lax.rem(c, block_rows), 1), :]

    contract(stiff, cols, vector, terms)


def second_kernel(cols, pack, arrived, maps, stiff, resid, direc, terms, send, xown, pown):
    slots, block_rows, per_row, width, _ = stiff.shape
    devices = pack.shape[0]
    blocks = devices * block_rows
    me = lax.axis_index("sub")
    start = stacked(pack, 0, block_rows)
    dsum = stacked(pack, block_rows, block_rows)
    back = landed(pack, arrived, block_rows, block_rows * per_row)
    image = jnp.where(dsum > 0.0, dsum * start + back, 0.0)
    head, scal = [], []
    for s in range(slots):
        span = slice(s * blocks, (s + 1) * blocks)
        r0, q0 = start[span], image[span]
        norm = total(r0 * r0)
        alpha = norm / total(r0 * q0)
        r1 = r0 - alpha * q0
        norm1 = total(r1 * r1)
        p1 = r1 + norm1 / norm * r0
        resid[span, :] = r1
        direc[span, :] = p1
        scal.append((norm1, total(dsum[span] * p1 * p1)))
        xown[s] = alpha * pack[me, s, :block_rows, :]
        pown[s] = direc[pl.ds(s * blocks + me * block_rows, block_rows), :]
        head.append(pack[me, s, 2 * block_rows : 2 * block_rows + 1, :])
    squares = contract(stiff, cols, lambda s, c: direc[pl.ds(s * blocks + c, 1), :], terms)
    write_send(send, maps, head, [xown[s, 0:1, :] for s in range(slots)], pown, scal, squares, devices)


def write_send(send, maps, pen, x_face, pown, scal, squares, devices):
    slots, width = maps.shape
    lane = iota((1, width), 1)
    rows = [maps[s : s + 1, :] for s in range(slots)]
    rows += [pen[s] * x_face[s] for s in range(slots)]
    rows += [pen[s] * pown[s, 0:1, :] for s in range(slots)]
    for s in range(slots):
        norm1, own = scal[s]
        image = total(squares[s]) + own * (1.0 / devices)
        rows.append(jnp.where(lane < width // 2, image, norm1 * (1.0 / devices)))
    send[...] = jnp.broadcast_to(jnp.concatenate(rows, axis=0)[None], send.shape)


def reactions(got, groups):
    devices, rows, width = got.shape
    slots = rows // 4
    half = width // 2
    alphas, lams = [], []
    for s in range(slots):
        both = got[:, 3 * slots + s, :].reshape(groups, devices // groups, width).sum(axis=1)
        turned = pltpu.roll(both, half, 1)
        low = iota(both.shape, 1) < half
        alpha = jnp.where(low, turned, both) / jnp.where(low, both, turned)
        wide = jnp.broadcast_to(alpha[:, None, :], (groups, devices // groups, width))
        alphas.append(alpha)
        lams.append(got[:, slots + s, :] + wide.reshape(devices, width) * got[:, 2 * slots + s, :])
    return alphas, lams


def place(got_map, lams, row_s, col_s, part_s, first_row, window, hot_s):
    devices = got_map.shape[0]
    slots = len(lams)
    rows, columns = window
    for s in range(slots):
        flat = got_map[:, s, :]
        row = jnp.floor(flat * (1.0 / columns))
        col_s[s] = flat - row * columns
        row_s[s] = row - first_row
        hi = lams[s].astype(BF16).astype(F32)
        mid = (lams[s] - hi).astype(BF16).astype(F32)
        part_s[0, s] = hi
        part_s[1, s] = mid
        part_s[2, s] = lams[s] - hi - mid
    ids_c = iota((columns, 1), 0).astype(F32)
    ids_r = iota((rows, 1), 0).astype(F32)

    def lanes(ref, d):
        return jnp.concatenate([ref[s, pl.ds(d, 1), :] for s in range(slots)], axis=1)

    def step(d, acc):
        hot_c = jnp.where(ids_c == lanes(col_s, d), 1.0, 0.0).astype(BF16)
        if hot_s is not None:
            hot_s[d] = hot_c
        hit = ids_r == lanes(row_s, d)
        left = jnp.concatenate(
            [jnp.where(hit, lanes(part_s.at[i], d), 0.0).astype(BF16) for i in range(3)], axis=0
        )
        return acc + lax.dot_general(
            left, hot_c, (((1,), (1,)), ((), ())), preferred_element_type=F32
        )

    acc = lax.fori_loop(0, devices, step, jnp.zeros((3 * rows, columns), F32), unroll=2)
    return acc[:rows] + acc[rows : 2 * rows] + acc[2 * rows :]


def stencil(ref, gdiag, first, count):
    here = ref[first : first + count, :]
    columns = here.shape[1]
    lane = iota(here.shape, 1)
    left = jnp.where(lane == 0, 0.0, pltpu.roll(here, 1, 1))
    right = jnp.where(lane == columns - 1, 0.0, pltpu.roll(here, columns - 1, 1))
    above = ref[first - 1 : first + count - 1, :]
    below = ref[first + 1 : first + count + 1, :]
    return (4.0 + gdiag) * here - (above + below + left + right)


def fill_window(window, own, before, after, width):
    rows = own.shape[0]
    window[...] = jnp.zeros_like(window)
    window[EDGE : EDGE + rows, :] = own[...]
    if width == 2:
        window[EDGE - 2 : EDGE, :] = before[0:2, :]
        window[EDGE + rows : EDGE + rows + 2, :] = after[0:2, :]
    else:
        window[EDGE - 1 : EDGE, :] = before[2:3, :]
        window[EDGE + rows : EDGE + rows + 1, :] = after[2:3, :]


def third_kernel(got, gload, gdiag, before, after, window, alphas_out, send, row_s, col_s, part_s, hot_s):
    rows, columns = gload.shape
    devices, _, width = got.shape
    groups = lax.axis_size("grp")
    flat = lax.axis_index("grp") * lax.axis_size("sub") + lax.axis_index("sub")
    first_row = (flat * rows - EDGE).astype(F32)
    alphas, lams = reactions(got, groups)
    slots = len(lams)
    for s in range(slots):
        alphas_out[s, 0:groups, :] = alphas[s]
    fill_window(window, gload, before, after, 2)
    extent = window.shape
    placed = place(got, lams, row_s, col_s, part_s, first_row, extent, hot_s)
    at = iota(extent, 0)
    inside = (at >= EDGE - 2) & (at < EDGE + rows + 2)
    window[...] = window[...] + jnp.where(inside, placed, 0.0)
    own = window[EDGE : EDGE + rows, :]
    image = stencil(window, gdiag[...], EDGE, rows)
    send[...] = jnp.zeros_like(send)
    send[:, slots : slots + 1, :] = jnp.broadcast_to(total(own * own)[None], (devices, 1, width))
    send[:, slots + 1 : slots + 2, :] = jnp.broadcast_to(total(own * image)[None], (devices, 1, width))
    parts = jnp.concatenate(split3(own), axis=0)
    ids = iota((rows, 1), 0).astype(F32) + EDGE

    def step(d, carry):
        seen = jnp.dot(parts, hot_s[d], preferred_element_type=F32)
        seen = seen[:rows] + seen[rows : 2 * rows] + seen[2 * rows :]
        row = jnp.concatenate([row_s[s, pl.ds(d, 1), :] for s in range(slots)], axis=1)
        mine = jnp.sum(jnp.where(ids == row, seen, 0.0), axis=0, keepdims=True)
        for s in range(slots):
            send[d, s : s + 1, :] = mine[:, s * width : (s + 1) * width]
        return carry

    lax.fori_loop(0, devices, step, 0, unroll=2)


def scale_kernel(got, terms, window, send, field):
    slots, count, width = terms.shape
    sums = jnp.sum(got[...], axis=0)
    scale = sums[slots : slots + 1, :] / sums[slots + 1 : slots + 2, :]
    send[:, :count, :] = terms[...]
    send[:, count:, :] = jnp.zeros((slots, send.shape[1] - count, width), F32)
    for s in range(slots):
        send[s, count : count + 1, :] = scale * sums[s : s + 1, :]
    field[...] = window[...] * jnp.concatenate([scale] * (field.shape[1] // width), axis=1)


def fourth_kernel(cols, pack, arrived, alphas, resid, direc, xown, pown, stiff, start, terms, xnext):
    slots, block_rows, per_row, width, _ = stiff.shape
    devices = pack.shape[0]
    blocks = devices * block_rows
    count = block_rows * per_row
    group = lax.axis_index("grp")
    dsum = stacked(pack, block_rows, block_rows)
    back = landed(pack, arrived, block_rows, count)
    p1 = direc[...]
    image = jnp.where(dsum > 0.0, dsum * p1 + back, 0.0)
    for s in range(slots):
        span = slice(s * blocks, (s + 1) * blocks)
        alpha = alphas[s, pl.ds(group, 1), :]
        start[span, :] = resid[span, :] - alpha * image[span]
        xnext[s] = xown[s] + alpha * pown[s]
        for d in range(devices):
            face = slice(s * blocks + d * block_rows, s * blocks + d * block_rows + 1)
            pen = pack[d, s, 2 * block_rows : 2 * block_rows + 1, :]
            start[face, :] = start[face, :] + pen * arrived[d, s, count : count + 1, :]
    contract(stiff, cols, lambda s, c: start[pl.ds(s * blocks + c, 1), :], terms)


def fifth_kernel(cols, pack, arrived, bound, start, maps, xin, stiff, send, xown, pown, direc):
    slots, block_rows, per_row, width, _ = stiff.shape
    devices = pack.shape[0]
    blocks = devices * block_rows
    count = block_rows * per_row
    me = lax.axis_index("sub")
    dsum = stacked(pack, block_rows, block_rows)
    back = landed(pack, arrived, block_rows, count)
    image = jnp.where(dsum > 0.0, dsum * start[...] + back, 0.0)
    head, face, scal = [], [], []
    for s in range(slots):
        span = slice(s * blocks, (s + 1) * blocks)
        r0, q0 = start[span, :], image[span]
        norm = total(r0 * r0)
        alpha = norm / total(r0 * q0)
        r1 = r0 - alpha * q0
        norm1 = total(r1 * r1)
        p1 = r1 + norm1 / norm * r0
        direc[span, :] = p1
        scal.append((norm1, total(dsum[span] * p1 * p1)))
        mine = pl.ds(s * blocks + me * block_rows, block_rows)
        xown[s] = xin[s] + alpha * start[mine, :]
        pown[s] = direc[mine, :]
        head.append(pack[me, s, 2 * block_rows : 2 * block_rows + 1, :])
        face.append(xown[s, 0:1, :] - bound[s, count : count + 1, :])
    squares = contract(stiff, cols, lambda s, c: direc[pl.ds(s * blocks + c, 1), :], None)
    write_send(send, maps, head, face, pown, scal, squares, devices)


def sixth_kernel(
    got, gload, gdiag, before, after, field, xown, pown, resid, xout, send, window, diags, row_s, col_s, part_s
):
    rows, columns = gload.shape
    devices, _, width = got.shape
    groups = lax.axis_size("grp")
    group = lax.axis_index("grp")
    flat = group * lax.axis_size("sub") + lax.axis_index("sub")
    first_row = flat * rows - EDGE
    alphas, lams = reactions(got, groups)
    slots = len(lams)
    for s in range(slots):
        part_s[0, s, 0:groups, :] = alphas[s]
        alpha = part_s[0, s, pl.ds(group, 1), :]
        for b in range(xown.shape[1]):
            xout[s : s + 1, b * width : (b + 1) * width] = (
                xown[s, b : b + 1, :] + alpha * pown[s, b : b + 1, :]
            )
    fill_window(window, gload, before, after, 2)
    fill_window(diags, gdiag, before, after, 1)
    extent = window.shape
    placed = place(got, lams, row_s, col_s, part_s, first_row.astype(F32), extent, None)
    span = slice(EDGE - 1, EDGE + rows + 1)
    applied = stencil(field, diags[span, :], EDGE - 1, rows + 2)
    at = iota(applied.shape, 0) + (first_row + EDGE - 1)
    inside = (at >= 0) & (at < devices * rows)
    window[span, :] = jnp.where(inside, window[span, :] - applied + placed[span], 0.0)
    own = window[EDGE : EDGE + rows, :]
    resid[...] = own
    image = stencil(window, gdiag[...], EDGE, rows)
    send[...] = jnp.zeros_like(send)
    send[:, 0:1, :] = jnp.broadcast_to(total(own * own)[None], (devices, 1, width))
    send[:, 1:2, :] = jnp.broadcast_to(total(own * image)[None], (devices, 1, width))


def last_kernel(got, field, resid, out):
    sums = jnp.sum(got[...], axis=0)
    scale = sums[0:1, :] / sums[1:2, :]
    rows, columns = out.shape
    wide = jnp.concatenate([scale] * (columns // got.shape[2]), axis=1)
    out[...] = field[EDGE : EDGE + rows, :] + wide * resid[...]


def call(kernel, shapes, operands, scalars, scratch=(), limit=None):
    out_shape = [jax.ShapeDtypeStruct(s, F32) for s in shapes]
    return pl.pallas_call(
        kernel,
        out_shape=out_shape,
        in_specs=[SMEM] * scalars + [VMEM] * (len(operands) - scalars),
        out_specs=[VMEM] * len(shapes),
        scratch_shapes=list(scratch),
        compiler_params=pltpu.CompilerParams(vmem_limit_bytes=limit),
    )(*operands)


def body(
    stiff_blocks,
    block_cols,
    live_blocks,
    sub_diag,
    penalty,
    sub_load,
    iface_map,
    global_load,
    global_diag,
):
    slots, block_rows, per_row, width, _ = stiff_blocks.shape
    rows_dev = block_rows * width
    rows, columns = global_load.shape
    near, groups = lax.axis_size("sub"), lax.axis_size("grp")
    devices = near * groups
    blocks = slots * near * block_rows
    count = block_rows * per_row
    extent = (rows + 2 * EDGE, columns)
    own = (slots, block_rows, width)
    cols = block_cols.reshape(slots, count)
    shift = jnp.arange(slots, dtype=jnp.int32)[:, None] * (near * block_rows)
    col_row = (cols + shift).astype(F32).reshape(1, slots * count)
    maps = iface_map.astype(F32)

    def everywhere(x):
        return lax.all_to_all(x, ALL, 0, 0)

    def near_all(x):
        return lax.all_gather(x, "sub")

    pack, up, down = call(
        prep_kernel,
        [(slots, 2 * block_rows + 8, width), (8, columns), (8, columns)],
        (live_blocks, sub_diag, penalty, sub_load, col_row, global_load, global_diag),
        1,
    )
    hops = [(i, i + 1) for i in range(devices - 1)]
    before = lax.ppermute(down, ALL, hops)
    after = lax.ppermute(up, ALL, [(j, i) for i, j in hops])
    pack = near_all(pack)
    (terms,) = call(first_kernel, [(slots, count, width)], (cols, pack, stiff_blocks), 1)
    arrived = near_all(terms)
    resid, direc, terms, send, xown, pown = call(
        second_kernel,
        [(blocks, width), (blocks, width), (slots, count, width), (devices, 4 * slots, width), own, own],
        (cols, pack, arrived, maps, stiff_blocks),
        1,
    )
    got = everywhere(send)
    lists = pltpu.VMEM((slots, devices, width), F32)
    parts = pltpu.VMEM((3, slots, devices, width), F32)
    window, alphas, send = call(
        third_kernel,
        [extent, (slots, max(8, groups), width), (devices, 8, width)],
        (got, global_load, global_diag, before, after),
        0,
        (lists, lists, parts, pltpu.VMEM((devices, columns, slots * width), BF16)),
    )
    sums = everywhere(send)
    bound, field = call(scale_kernel, [(slots, count + 8, width), extent], (sums, terms, window), 0)
    arrived = near_all(bound)
    start, terms, xown = call(
        fourth_kernel,
        [(blocks, width), (slots, count, width), own],
        (cols, pack, arrived, alphas, resid, direc, xown, pown, stiff_blocks),
        1,
    )
    arrived = near_all(terms)
    send, xown, pown = call(
        fifth_kernel,
        [(devices, 4 * slots, width), own, own],
        (cols, pack, arrived, bound, start, maps, xown, stiff_blocks),
        1,
        (pltpu.VMEM((blocks, width), F32),),
    )
    got = everywhere(send)
    resid, sub_field, send = call(
        sixth_kernel,
        [(rows, columns), (slots, rows_dev), (devices, 8, width)],
        (got, global_load, global_diag, before, after, field, xown, pown),
        0,
        (pltpu.VMEM(extent, F32), pltpu.VMEM(extent, F32), lists, lists, parts),
    )
    sums = everywhere(send)
    (global_field,) = call(last_kernel, [(rows, columns)], (sums, field, resid), 0)
    return global_field, sub_field


def solution(mesh):
    return jax.shard_map(
        body,
        mesh=mesh,
        in_specs=(
            P("grp", "sub", None, None, None),
            P("grp", "sub", None),
            P("grp", "sub"),
            P("grp", "sub"),
            P("grp", "sub"),
            P("grp", "sub"),
            P("grp", "sub"),
            P(ALL, None),
            P(ALL, None),
        ),
        out_specs=(P(ALL, None), P("grp", "sub")),
        check_vma=False,
    )
```

time: 811 us -> 152 us (0.19)
  waiting for transfers between devices: 248 us -> 4.72 us
  blocking collectives: 311 us -> 83.6 us
  other arithmetic: 121 us -> 1.78 us
  matrix products: 78.1 us -> 0 us
  Pallas kernels: 0 us -> 47.8 us
  between operations: 18.4 us -> 0.71 us
  local copies, waits for them, and re-layouts: 14.3 us -> 3.68 us
    unnamed x11 -> x0, waiting for transfers between devices: 218 us -> none
    psum x8 -> x0, blocking collectives: 146 us -> none  [the longest x2 75.6 us: body(): lax.psum((jnp.sum(resid_g * resid_g), jnp.sum(resid_g * image_g)), ('grp'...]
    all_gather x8 -> x4, blocking collectives: 165 us -> 45.2 us  [near_all(): return lax.all_gather(x, 'sub')]
    scatter-add x2 -> x0, other arithmetic: 111 us -> none  [body(): jax.ops.segment_sum(lam_all.reshape(-1), seg_idx.reshape(-1), num_segment...]
    dot_general x15 -> x0, matrix products: 78.1 us -> none  [the longest x5 46.9 us: sub_apply(): strain = jnp.einsum('srnij,srnj->sri', stiff_blocks, picked, precision=HIGH)]
    pallas_call x0 -> x9, Pallas kernels: none -> 47.8 us  [call(): pl.pallas_call(kernel, out_shape=out_shape, in_specs=[SMEM] * scalars + [...]
    all_to_all x0 -> x3, blocking collectives: none -> 38.4 us  [everywhere(): return lax.all_to_all(x, ALL, 0, 0)]
    all_gather x1 -> x0, waiting for transfers between devices: 26.6 us -> none  [body(): lax.all_gather(global_field, ('grp', 'sub'), axis=0, tiled=True)]
  transfers between devices with their start and end apart: 12 -> 3, of which waited for: 8 -> 2; matrix products, arithmetic and copies ran while one was open for 5% -> 0% of each run, Pallas kernels for 0% -> 0%
where the time goes in v1:
time: 152 us; the launch traced here: 151 us
  blocking collectives  83.6 us (55%)
  Pallas kernels  47.8 us (31%)
  starting transfers between devices  8.33 us (5%)
  waiting for transfers between devices  4.72 us (3%)
  local copies, waits for them, and re-layouts  3.68 us (2%)
  other arithmetic  1.78 us (1%)
    pallas_call x9, Pallas kernels, call(): pl.pallas_call(kernel, out_shape=out_shape, in_specs=[SMEM] * scalars + [...  47.8 us
    all_gather x4, blocking collectives, near_all(): return lax.all_gather(x, 'sub')  45.2 us
    all_to_all x3, blocking collectives, everywhere(): return lax.all_to_all(x, ALL, 0, 0)  38.4 us
    all_to_all x1, starting transfers between devices, everywhere(): return lax.all_to_all(x, ALL, 0, 0)  4.88 us
  transfers between devices with their start and end apart: 3, of which 2 were waited for; matrix products, arithmetic and copies ran while one was open for 0% of the time, Pallas kernels for 0%

profile of v1, /device:TPU:0, one launch (start us, length us, event | category | flops | bytes accessed | tf_op | source)
XLA Modules:
  0.0 150.7 jit_solution(18393043348006001157)
XLA Ops:
  0.6 0.8 copy.17
  1.4 0.1 reshape.38
  1.5 0.7 reshape.37.cols
  2.2 0.1 add.17
  2.3 0.1 add.18
  2.4 1.3 convert_element_type.14.maps
  3.6 1.3 copy.19.live
  4.9 0.5 add_convert_fusion.cols
  5.4 1.5 %shard_map.104 = (f32[2,40,128]{2,1,0:T(8,128)}, f32[8,256]{1,0:T(8,128)}, f32[8,256]{1,0:T(8,128)}) custom-call(s32[2,1]{1,0:T(2,128)} %copy.19.live, f32[2,2048]{1,0:T(2,128)} %diag.1, f32[2,128]{1,0:T(2,128)} %pen.1, f32[2,2048]{1,0:T(2,128)} %load.1, f32[1,128]{1,0:T(1,128)} %add_convert_fusion.cols, f32[32,256]{1,0:T(8,128)} %gload.5, f32[32,256]{1,0:T(8,128)} %gdiag.5), custom_call_target="tpu_custom_call" | custom-call | tf_op jit(solution)/shard_map/pallas_call | solution.py:369
  6.9 12.7 %all-gather = f32[16,40,128]{2,1,0:T(8,128)} all-gather(f32[2,40,128]{2,1,0:T(8,128)} %get-tuple-element.25), channel_id=2, replica_groups=mesh['grp'=4,'sub'=8] {'sub'}, dimensions={0}, use_global_device_ids=true | all-gather | bytes 368640 | tf_op jit(solution)/shard_map/all_gather | solution.py:408
  19.7 6.5 %shard_map.105 = f32[2,64,128]{2,1,0:T(8,128)} custom-call(s32[2,64]{1,0:T(2,128)} %reshape.37.cols, f32[8,2,40,128]{3,2,1,0:T(8,128)} %bitcast.4, f32[2,16,4,128,128]{4,3,2,1,0:T(8,128)} %stiff.7), custom_call_target="tpu_custom_call" | custom-call | tf_op jit(solution)/shard_map/pallas_call | solution.py:369
  26.2 10.8 %all-gather.1 = f32[16,64,128]{2,1,0:T(8,128)} all-gather(f32[2,64,128]{2,1,0:T(8,128)} %shard_map.105), channel_id=3, replica_groups=mesh['grp'=4,'sub'=8] {'sub'}, dimensions={0}, use_global_device_ids=true | all-gather | bytes 589824 | tf_op jit(solution)/shard_map/all_gather | solution.py:408
  37.0 7.4 %shard_map.106 = (f32[256,128]{1,0:T(8,128)}, f32[256,128]{1,0:T(8,128)}, f32[2,64,128]{2,1,0:T(8,128)}, f32[32,8,128]{2,1,0:T(8,128)}, f32[2,16,128]{2,1,0:T(8,128)}, /*index=5*/f32[2,16,128]{2,1,0:T(8,128)}) custom-call(s32[2,64]{1,0:T(2,128)} %reshape.37.cols, f32[8,2,40,128]{3,2,1,0:T(8,128)} %bitcast.5, f32[8,2,64,128]{3,2,1,0:T(8,128)} %bitcast.10, ...), custom_call_target="tpu_custom_call" | custom-call | tf_op jit(solution)/shard_map/pallas_call | solution.py:369
  44.4 4.9 %all-to-all-start = ((f32[32,8,128]{2,1,0:T(8,128)}), f32[32,8,128]{2,1,0:T(8,128)S(1)}, u32[]{:S(2)}, u32[]{:S(2)}) async-start(f32[32,8,128]{2,1,0:T(8,128)} %get-tuple-element.26), calls=%async_computation | async-start | bytes 262144 | tf_op jit(solution)/shard_map/all_to_all | solution.py:405
  49.3 0.0 copy-done.4
  49.3 2.2 %collective-permute-start = (f32[8,256]{1,0:T(8,128)S(1)}, f32[8,256]{1,0:T(8,128)S(1)}, u32[]{:S(2)}, u32[]{:S(2)}) collective-permute-start(f32[8,256]{1,0:T(8,128)S(1)} %copy-done.4), channel_id=1, source_target_pairs={{0,1},{1,2},{2,3},{3,4},{4,5},{5,6},{6,7},{7,8},{8,9},{9,10},{10,1... | collective-permute-start | bytes 24584 | tf_op jit(solution)/shard_map/ppermute | solution.py:417
  51.4 1.3 collective-permute-start.1
  52.7 0.0 collective-permute-done.before
  52.8 2.9 %collective-permute-done.1.after = f32[8,256]{1,0:T(8,128)S(1)} collective-permute-done((f32[8,256]{1,0:T(8,128)S(1)}, f32[8,256]{1,0:T(8,128)S(1)}, u32[]{:S(2)}, u32[]{:S(2)}) %collective-permute-start.1) | collective-permute-done | bytes 8224 | tf_op jit(solution)/shard_map/ppermute | solution.py:418
  55.7 1.8 %all-to-all-done.got = f32[32,8,128]{2,1,0:T(8,128)S(1)} async-done(((f32[32,8,128]{2,1,0:T(8,128)}), f32[32,8,128]{2,1,0:T(8,128)S(1)}, u32[]{:S(2)}, u32[]{:S(2)}) %all-to-all-start) | async-done | bytes 131104 | tf_op jit(solution)/shard_map/all_to_all | solution.py:405
  57.5 0.7 copy-done
  58.2 9.0 %shard_map.107 = (f32[48,256]{1,0:T(8,128)}, f32[2,8,128]{2,1,0:T(8,128)}, f32[32,8,128]{2,1,0:T(8,128)}) custom-call(f32[32,8,128]{2,1,0:T(8,128)} %copy-done, f32[32,256]{1,0:T(8,128)} %gload.5, f32[32,256]{1,0:T(8,128)} %gdiag.5, f32[8,256]{1,0:T(8,128)} %copy-done.1, f32[8,256]{1,0:T(8,128)} %copy-done.2), custom_call_target="tpu_custom_call" | custom-call | tf_op jit(solution)/shard_map/pallas_call | solution.py:369
  67.1 15.5 %all_to_all.20.got = f32[32,8,128]{2,1,0:T(8,128)} all-to-all(f32[32,8,128]{2,1,0:T(8,128)} %get-tuple-element.29), channel_id=1, replica_groups=mesh['grp'=4,'sub'=8] {'grp','sub'}, dimensions={0} | all-to-all | bytes 262144 | tf_op jit(solution)/shard_map/all_to_all | solution.py:405
  82.6 1.6 %shard_map.108 = (f32[2,72,128]{2,1,0:T(8,128)}, f32[48,256]{1,0:T(8,128)}) custom-call(f32[32,8,128]{2,1,0:T(8,128)} %all_to_all.20.got, f32[2,64,128]{2,1,0:T(8,128)} %get-tuple-element.30.terms, f32[48,256]{1,0:T(8,128)} %get-tuple-element.31.window), custom_call_target="tpu_custom_call" | custom-call | tf_op jit(solution)/shard_map/pallas_call | solution.py:369
  84.2 10.9 %all-gather.2 = f32[16,72,128]{2,1,0:T(8,128)} all-gather(f32[2,72,128]{2,1,0:T(8,128)} %get-tuple-element.32.bound), channel_id=4, replica_groups=mesh['grp'=4,'sub'=8] {'sub'}, dimensions={0}, use_global_device_ids=true | all-gather | bytes 663552 | tf_op jit(solution)/shard_map/all_gather | solution.py:408
  95.1 7.1 %shard_map.109 = (f32[256,128]{1,0:T(8,128)}, f32[2,64,128]{2,1,0:T(8,128)}, f32[2,16,128]{2,1,0:T(8,128)}) custom-call(s32[2,64]{1,0:T(2,128)} %reshape.37.cols, f32[8,2,40,128]{3,2,1,0:T(8,128)} %bitcast.6, f32[8,2,72,128]{3,2,1,0:T(8,128)} %bitcast.8, f32[2,8,128]{2,1,0:T(8,128)} %get-tuple-element.33.alphas, f32[256,128]{1,0:T(8,128)} %get-tuple-element.34.resid, ...), custom_call_target="tpu_custom_call" | custom-call | tf_op jit(solution)/shard_map/pallas_call | solution.py:369
  102.2 10.8 %all-gather.3 = f32[16,64,128]{2,1,0:T(8,128)} all-gather(f32[2,64,128]{2,1,0:T(8,128)} %get-tuple-element.38), channel_id=5, replica_groups=mesh['grp'=4,'sub'=8] {'sub'}, dimensions={0}, use_global_device_ids=true | all-gather | bytes 589824 | tf_op jit(solution)/shard_map/all_gather | solution.py:408
  113.0 7.1 %shard_map.110 = (f32[32,8,128]{2,1,0:T(8,128)}, f32[2,16,128]{2,1,0:T(8,128)}, f32[2,16,128]{2,1,0:T(8,128)}) custom-call(s32[2,64]{1,0:T(2,128)} %reshape.37.cols, f32[8,2,40,128]{3,2,1,0:T(8,128)} %bitcast.7, f32[8,2,64,128]{3,2,1,0:T(8,128)} %bitcast.9, f32[2,72,128]{2,1,0:T(8,128)} %get-tuple-element.32.bound, f32[256,128]{1,0:T(8,128)} %get-tuple-element.39.start, ...), custom_call_target="tpu_custom_call" | custom-call | tf_op jit(solution)/shard_map/pallas_call | solution.py:369
  120.1 11.5 %all_to_all.21.got = f32[32,8,128]{2,1,0:T(8,128)} all-to-all(f32[32,8,128]{2,1,0:T(8,128)} %get-tuple-element.41), channel_id=1, replica_groups=mesh['grp'=4,'sub'=8] {'grp','sub'}, dimensions={0} | all-to-all | bytes 262144 | tf_op jit(solution)/shard_map/all_to_all | solution.py:405
  131.6 6.0 %shard_map.111 = (f32[32,256]{1,0:T(8,128)}, f32[2,2048]{1,0:T(2,128)}, f32[32,8,128]{2,1,0:T(8,128)}) custom-call(f32[32,8,128]{2,1,0:T(8,128)} %all_to_all.21.got, f32[32,256]{1,0:T(8,128)} %gload.5, f32[32,256]{1,0:T(8,128)} %gdiag.5, f32[8,256]{1,0:T(8,128)} %copy-done.1, f32[8,256]{1,0:T(8,128)} %copy-done.2, f32[48,256]{1,0:T(8,128)} %get-tuple-element.42.field, ...), custom_call_target="tpu_custom_call" | custom-call | tf_op jit(solution)/shard_map/pallas_call | solution.py:369
  137.6 11.5 %all_to_all.22.got = f32[32,8,128]{2,1,0:T(8,128)} all-to-all(f32[32,8,128]{2,1,0:T(8,128)} %get-tuple-element.45), channel_id=1, replica_groups=mesh['grp'=4,'sub'=8] {'grp','sub'}, dimensions={0} | all-to-all | bytes 262144 | tf_op jit(solution)/shard_map/all_to_all | solution.py:405
  149.1 1.6 %shard_map.112 = f32[32,256]{1,0:T(8,128)} custom-call(f32[32,8,128]{2,1,0:T(8,128)} %all_to_all.22.got, f32[48,256]{1,0:T(8,128)} %get-tuple-element.42.field, f32[32,256]{1,0:T(8,128)} %get-tuple-element.46.resid), custom_call_target="tpu_custom_call" | custom-call | tf_op jit(solution)/shard_map/pallas_call | solution.py:369
  (9 shorter events, 0.0 us)
Async XLA Ops:
  19.7 29.6 %copy-start.4 = (f32[8,256]{1,0:T(8,128)S(1)}, f32[8,256]{1,0:T(8,128)}, u32[]{:S(2)}) copy-start(f32[8,256]{1,0:T(8,128)} %get-tuple-element.27) | copy-start | bytes 24580
  19.7 31.8 %copy-start.3 = (f32[8,256]{1,0:T(8,128)S(1)}, f32[8,256]{1,0:T(8,128)}, u32[]{:S(2)}) copy-start(f32[8,256]{1,0:T(8,128)} %get-tuple-element.28) | copy-start | bytes 24580
  44.4 13.1 %all-to-all-start = ((f32[32,8,128]{2,1,0:T(8,128)}), f32[32,8,128]{2,1,0:T(8,128)S(1)}, u32[]{:S(2)}, u32[]{:S(2)}) async-start(f32[32,8,128]{2,1,0:T(8,128)} %get-tuple-element.26), calls=%async_computation | async-start | bytes 262144 | tf_op jit(solution)/shard_map/all_to_all | solution.py:405
  49.3 3.5 %collective-permute-start = (f32[8,256]{1,0:T(8,128)S(1)}, f32[8,256]{1,0:T(8,128)S(1)}, u32[]{:S(2)}, u32[]{:S(2)}) collective-permute-start(f32[8,256]{1,0:T(8,128)S(1)} %copy-done.4), channel_id=1, source_target_pairs={{0,1},{1,2},{2,3},{3,4},{4,5},{5,6},{6,7},{7,8},{8,9},{9,10},{10,1... | collective-permute-start | bytes 24584 | tf_op jit(solution)/shard_map/ppermute | solution.py:417
  51.4 4.2 %collective-permute-start.1 = (f32[8,256]{1,0:T(8,128)S(1)}, f32[8,256]{1,0:T(8,128)S(1)}, u32[]{:S(2)}, u32[]{:S(2)}) collective-permute-start(f32[8,256]{1,0:T(8,128)S(1)} %copy-done.3), channel_id=1, source_target_pairs={{1,0},{2,1},{3,2},{4,3},{5,4},{6,5},{7,6},{8,7},{9,8},{10,9},{11,1... | collective-permute-start | bytes 24584 | tf_op jit(solution)/shard_map/ppermute | solution.py:418
  52.8 4.7 %copy-start.1 = (f32[8,256]{1,0:T(8,128)}, f32[8,256]{1,0:T(8,128)S(1)}, u32[]{:S(2)}) copy-start(f32[8,256]{1,0:T(8,128)S(1)} %collective-permute-done.before) | copy-start | bytes 24580
  55.6 1.8 %copy-start.2 = (f32[8,256]{1,0:T(8,128)}, f32[8,256]{1,0:T(8,128)S(1)}, u32[]{:S(2)}) copy-start(f32[8,256]{1,0:T(8,128)S(1)} %collective-permute-done.1.after) | copy-start | bytes 24580
  57.5 0.7 copy-start

commit v2 on v1

v2 whole, which is shorter than its diff:
```python
import jax
import jax.numpy as jnp
from jax import lax
from jax.experimental import pallas as pl
from jax.experimental.pallas import tpu as pltpu
from jax.sharding import PartitionSpec as P

F32 = jnp.float32
BF16 = jnp.bfloat16
CHUNK = 16
AHEAD = 10
EDGE = 8
ALL = ("grp", "sub")

VMEM = pl.BlockSpec(memory_space=pltpu.VMEM)
SMEM = pl.BlockSpec(memory_space=pltpu.SMEM)


def total(x):
    return jnp.sum(jnp.sum(x, axis=0, keepdims=True), axis=1, keepdims=True)


def split3(x):
    hi = x.astype(BF16)
    rest = x - hi.astype(F32)
    mid = rest.astype(BF16)
    return hi, mid, (rest - mid.astype(F32)).astype(BF16)


def iota(shape, dim):
    return lax.broadcasted_iota(jnp.int32, shape, dim)


def contract(stiff, cols, vector, terms, arrive=None):
    slots, block_rows, per_row, width, _ = stiff.shape
    squares = []
    for s in range(slots):

        def row(r, acc, s=s):
            if arrive is not None:
                arrive(s, r)
            prod = None
            for n in range(per_row):
                part = stiff[s, r, n] * vector(s, cols[s, n, r])
                prod = part if prod is None else prod + part
            strain = jnp.sum(prod, axis=1, keepdims=True)
            if terms is not None:
                for n in range(per_row):
                    terms[s, pl.ds(n * block_rows + r, 1), :] = jnp.sum(
                        stiff[s, r, n] * strain, axis=0, keepdims=True
                    )
            return acc + strain * strain

        squares.append(lax.fori_loop(0, block_rows, row, jnp.zeros((width, 1), F32), unroll=2))
    return squares


def stacked(gathered, first, count):
    devices, slots = gathered.shape[:2]
    return jnp.concatenate(
        [gathered[d, s, first : first + count, :] for s in range(slots) for d in range(devices)],
        axis=0,
    )


def landed(pack, arrived, block_rows, count):
    devices, slots, _, width = pack.shape
    targets = slots * devices * block_rows
    source = jnp.concatenate(
        [arrived[d, s, :count, :] for d in range(devices) for s in range(slots)], axis=0
    )
    col = jnp.concatenate(
        [pack[d, 0, 2 * block_rows + 1 : 2 * block_rows + 2, :] for d in range(devices)], axis=1
    )
    hot = jnp.where(iota((targets, col.shape[1]), 0).astype(F32) == col, 1.0, 0.0).astype(BF16)
    out = jnp.dot(hot, jnp.concatenate(split3(source), axis=1), preferred_element_type=F32)
    return out[:, :width] + out[:, width : 2 * width] + out[:, 2 * width :]


def prep_kernel(live, diag, pen, load, cols, gload, gdiag, pack):
    slots, rows, width = pack.shape
    block_rows = (rows - 16) // 2
    per_row = cols.shape[1]
    blocks = block_rows * lax.axis_size("sub")
    pack[:, 2 * block_rows :, :] = jnp.zeros((slots, 16, width), F32)
    for s in range(slots):
        count = live[s]
        for b in range(block_rows):
            lanes = pl.ds(b * width, width)
            on = b < count
            main = diag[s : s + 1, lanes]
            if b == 0:
                main = main + pen[s : s + 1, :]
            pack[s, b : b + 1, :] = jnp.where(on, load[s : s + 1, lanes], 0.0)
            pack[s, block_rows + b : block_rows + b + 1, :] = jnp.where(on, main, 0.0)
        pack[s, 2 * block_rows : 2 * block_rows + 1, :] = pen[s : s + 1, :]
        for n in range(per_row):
            at = (s * per_row + n) * block_rows
            pack[0, 2 * block_rows + 1 : 2 * block_rows + 2, at : at + block_rows] = (
                cols[s, n : n + 1, :] + s * blocks
            ).astype(F32)
    last = gload.shape[0] - 1
    half = gload.shape[1] // width
    edge = 2 * block_rows + 8
    for side, picks in enumerate(
        (((gload, 0), (gload, 1), (gdiag, 0)), ((gload, last - 1), (gload, last), (gdiag, last)))
    ):
        for k, (ref, row) in enumerate(picks):
            for h in range(half):
                at = edge + k * half + h
                pack[side, at : at + 1, :] = ref[row : row + 1, h * width : (h + 1) * width]


def first_kernel(cols, pack, source, terms, stiff, sems):
    slots, block_rows = stiff.shape[:2]

    def copy(s, r):
        return pltpu.make_async_copy(source.at[s, r], stiff.at[s, r], sems.at[s, r])

    for i in range(AHEAD):
        copy(i // block_rows, i % block_rows).start()

    def arrive(s, r):
        copy(s, r).wait()
        later = s * block_rows + r + AHEAD

        @pl.when(later < slots * block_rows)
        def _():
            copy(lax.div(later, block_rows), lax.rem(later, block_rows)).start()

    def vector(s, c):
        return pack[lax.div(c, block_rows), s, pl.ds(lax.rem(c, block_rows), 1), :]

    contract(stiff, cols, vector, terms, arrive)


def second_kernel(cols, maps, pack, arrived, stiff, resid, direc, terms, send, xown, pown):
    slots, block_rows, per_row, width, _ = stiff.shape
    devices = pack.shape[0]
    blocks = devices * block_rows
    me = lax.axis_index("sub")
    start = stacked(pack, 0, block_rows)
    dsum = stacked(pack, block_rows, block_rows)
    back = landed(pack, arrived, block_rows, block_rows * per_row)
    image = jnp.where(dsum > 0.0, dsum * start + back, 0.0)
    head, scal = [], []
    for s in range(slots):
        span = slice(s * blocks, (s + 1) * blocks)
        r0, q0 = start[span], image[span]
        norm = total(r0 * r0)
        alpha = norm / total(r0 * q0)
        r1 = r0 - alpha * q0
        norm1 = total(r1 * r1)
        p1 = r1 + norm1 / norm * r0
        resid[span, :] = r1
        direc[span, :] = p1
        scal.append((norm1, total(dsum[span] * p1 * p1)))
        xown[s] = alpha * pack[me, s, :block_rows, :]
        pown[s] = direc[pl.ds(s * blocks + me * block_rows, block_rows), :]
        head.append(pack[me, s, 2 * block_rows : 2 * block_rows + 1, :])
    squares = contract(stiff, cols, lambda s, c: direc[pl.ds(s * blocks + c, 1), :], terms)
    write_send(send, maps, head, [xown[s, 0:1, :] for s in range(slots)], pown, scal, squares, devices)
    everyone, used = send.shape[0], 3 * slots + 1
    group = lax.axis_index("grp")
    groups = everyone // devices
    edge = 2 * block_rows + 8
    send[:, used : used + 1, :] = jnp.zeros((everyone, 1, width), F32)

    @pl.when((group > 0) & (me < 8))
    def _():
        send[group * devices - 1, used : used + 1, :] = pack[0, 0, pl.ds(edge + me, 1), :]

    @pl.when((group < groups - 1) & (me < 8))
    def _():
        send[(group + 1) * devices, used : used + 1, :] = pack[devices - 1, 1, pl.ds(edge + me, 1), :]


def write_send(send, maps, pen, x_face, pown, scal, squares, devices):
    slots, width = len(x_face), x_face[0].shape[1]
    lane = iota((1, width), 1)
    rows = [pen[s] * x_face[s] for s in range(slots)]
    rows += [pen[s] * pown[s, 0:1, :] for s in range(slots)]
    if maps is None:
        rows += [jnp.zeros((slots, width), F32)]
    else:
        rows += [maps[...].astype(F32)]
    row = jnp.zeros((1, width), F32)
    for s in range(slots):
        norm1, own = scal[s]
        image = total(squares[s]) + own * (1.0 / devices)
        row = jnp.where(lane == 2 * s, image, row)
        row = jnp.where(lane == 2 * s + 1, norm1 * (1.0 / devices), row)
    rows.append(row)
    send[:, : 3 * slots + 1, :] = jnp.broadcast_to(
        jnp.concatenate(rows, axis=0)[None], (send.shape[0], 3 * slots + 1, width)
    )


def reactions(got, groups, slots):
    devices, _, width = got.shape
    both = got[:, 3 * slots, :].reshape(groups, devices // groups, width).sum(axis=1)
    alphas, lams = [], []
    for s in range(slots):
        alpha = both[:, 2 * s + 1 : 2 * s + 2] / both[:, 2 * s : 2 * s + 1]
        alpha = jnp.broadcast_to(alpha, (groups, width))
        wide = jnp.broadcast_to(alpha[:, None, :], (groups, devices // groups, width))
        alphas.append(alpha)
        lams.append(got[:, s, :] + wide.reshape(devices, width) * got[:, slots + s, :])
    return alphas, lams


def split_lams(lams, part_s):
    for s, lam in enumerate(lams):
        hi = lam.astype(BF16).astype(F32)
        mid = (lam - hi).astype(BF16).astype(F32)
        part_s[0, s] = hi
        part_s[1, s] = mid
        part_s[2, s] = lam - hi - mid


def lanes_of(ref, d, slots):
    return jnp.concatenate([ref[s, pl.ds(d, 1), :] for s in range(slots)], axis=1)


def place(row_s, part_s, window, hot_of):
    _, slots, devices, _ = part_s.shape
    rows, columns = window
    ids_r = iota((rows, 1), 0).astype(F32)

    def step(c, acc):
        lefts, hots = [], []
        for d in [c * CHUNK + i for i in range(CHUNK)]:
            hit = ids_r == lanes_of(row_s, d, slots)
            lefts.append(
                jnp.concatenate(
                    [jnp.where(hit, lanes_of(part_s.at[i], d, slots), 0.0).astype(BF16) for i in range(3)],
                    axis=0,
                )
            )
            hots.append(hot_of(d))
        return acc + lax.dot_general(
            jnp.concatenate(lefts, axis=1),
            jnp.concatenate(hots, axis=1),
            (((1,), (1,)), ((), ())),
            preferred_element_type=F32,
        )

    acc = lax.fori_loop(0, devices // CHUNK, step, jnp.zeros((3 * rows, columns), F32))
    return acc[:rows] + acc[rows : 2 * rows] + acc[2 * rows :]


def stencil(ref, gdiag, first, count):
    here = ref[first : first + count, :]
    columns = here.shape[1]
    lane = iota(here.shape, 1)
    left = jnp.where(lane == 0, 0.0, pltpu.roll(here, 1, 1))
    right = jnp.where(lane == columns - 1, 0.0, pltpu.roll(here, columns - 1, 1))
    above = ref[first - 1 : first + count - 1, :]
    below = ref[first + 1 : first + count + 1, :]
    return (4.0 + gdiag) * here - (above + below + left + right)


def third_kernel(gload, gdiag, got, pack, window, loads, diags, alphas_out, send, row_s, hot_s, part_s, col_s):
    rows, columns = gload.shape
    slots, devices, width = row_s.shape
    groups = lax.axis_size("grp")
    flat = lax.axis_index("grp") * lax.axis_size("sub") + lax.axis_index("sub")
    first_row = (flat * rows - EDGE).astype(F32)
    alphas, lams = reactions(got, groups, slots)
    for s in range(slots):
        alphas_out[s, 0:groups, :] = alphas[s]
    split_lams(lams, part_s)
    for s in range(slots):
        where = got[:, 2 * slots + s, :]
        row = jnp.floor(where * (1.0 / columns))
        col_s[s] = where - row * columns
        row_s[s] = row - first_row
    me, group = lax.axis_index("sub"), lax.axis_index("grp")
    near = devices // groups
    half, edge, spare = columns // width, pack.shape[2] - 8, 3 * slots + 1
    loads[...] = jnp.zeros_like(loads)
    diags[...] = jnp.zeros_like(diags)
    loads[EDGE : EDGE + rows, :] = gload[...]
    diags[EDGE : EDGE + rows, :] = gdiag[...]
    last = EDGE + rows

    def fill(side, row_of):
        first = EDGE - 2 if side else last
        diag_row = EDGE - 1 if side else last
        for h in range(half):
            lanes = slice(h * width, (h + 1) * width)
            loads[first : first + 1, lanes] = row_of(h)
            loads[first + 1 : first + 2, lanes] = row_of(half + h)
            diags[diag_row : diag_row + 1, lanes] = row_of(2 * half + h)

    @pl.when(me > 0)
    def _():
        fill(1, lambda k: pack[me - 1, 1, edge + k : edge + k + 1, :])

    @pl.when((me == 0) & (group > 0))
    def _():
        fill(1, lambda k: got[(group - 1) * near + k, spare : spare + 1, :])

    @pl.when(me < near - 1)
    def _():
        fill(0, lambda k: pack[me + 1, 0, edge + k : edge + k + 1, :])

    @pl.when((me == near - 1) & (group < groups - 1))
    def _():
        fill(0, lambda k: got[(group + 1) * near + k, spare : spare + 1, :])

    extent = window.shape
    ids_c = iota((columns, 1), 0).astype(F32)

    def hot_of(d):
        hot = jnp.where(ids_c == lanes_of(col_s, d, slots), 1.0, 0.0).astype(BF16)
        hot_s[d] = hot
        return hot

    placed = place(row_s, part_s, extent, hot_of)
    at = iota(extent, 0)
    inside = (at >= EDGE - 2) & (at < last + 2)
    window[...] = loads[...] + jnp.where(inside, placed, 0.0)
    own = window[EDGE:last, :]
    image = stencil(window, gdiag[...], EDGE, rows)
    send[:, slots : slots + 1, :] = jnp.broadcast_to(total(own * own)[None], (devices, 1, width))
    send[:, slots + 1 : slots + 2, :] = jnp.broadcast_to(total(own * image)[None], (devices, 1, width))
    parts = jnp.concatenate(split3(own), axis=0)
    ids = iota((rows, 1), 0).astype(F32) + EDGE

    def step(d, carry):
        seen = jnp.dot(parts, hot_s[d], preferred_element_type=F32)
        seen = seen[:rows] + seen[rows : 2 * rows] + seen[2 * rows :]
        hit = ids == lanes_of(row_s, d, slots)
        mine = jnp.sum(jnp.where(hit, seen, 0.0), axis=0, keepdims=True)
        for s in range(slots):
            send[d, s : s + 1, :] = mine[:, s * width : (s + 1) * width]
        return carry

    lax.fori_loop(0, devices, step, 0, unroll=8)


def scale_kernel(got, terms, window, send, field):
    slots, count, width = terms.shape
    sums = jnp.sum(got[...], axis=0)
    scale = sums[slots : slots + 1, :] / sums[slots + 1 : slots + 2, :]
    send[:, :count, :] = terms[...]
    send[:, count:, :] = jnp.zeros((slots, send.shape[1] - count, width), F32)
    for s in range(slots):
        send[s, count : count + 1, :] = scale * sums[s : s + 1, :]
    field[...] = window[...] * jnp.concatenate([scale] * (field.shape[1] // width), axis=1)


def fourth_kernel(cols, pack, arrived, alphas, resid, direc, xown, pown, stiff, start, terms, xnext):
    slots, block_rows, per_row, width, _ = stiff.shape
    devices = pack.shape[0]
    blocks = devices * block_rows
    count = block_rows * per_row
    group = lax.axis_index("grp")
    dsum = stacked(pack, block_rows, block_rows)
    back = landed(pack, arrived, block_rows, count)
    p1 = direc[...]
    image = jnp.where(dsum > 0.0, dsum * p1 + back, 0.0)
    for s in range(slots):
        span = slice(s * blocks, (s + 1) * blocks)
        alpha = alphas[s, pl.ds(group, 1), :]
        start[span, :] = resid[span, :] - alpha * image[span]
        xnext[s] = xown[s] + alpha * pown[s]
        for d in range(devices):
            face = slice(s * blocks + d * block_rows, s * blocks + d * block_rows + 1)
            pen = pack[d, s, 2 * block_rows : 2 * block_rows + 1, :]
            start[face, :] = start[face, :] + pen * arrived[d, s, count : count + 1, :]
    contract(stiff, cols, lambda s, c: start[pl.ds(s * blocks + c, 1), :], terms)


def fifth_kernel(cols, pack, arrived, bound, start, xin, stiff, send, xown, pown, direc):
    slots, block_rows, per_row, width, _ = stiff.shape
    devices = pack.shape[0]
    blocks = devices * block_rows
    count = block_rows * per_row
    me = lax.axis_index("sub")
    dsum = stacked(pack, block_rows, block_rows)
    back = landed(pack, arrived, block_rows, count)
    image = jnp.where(dsum > 0.0, dsum * start[...] + back, 0.0)
    head, face, scal = [], [], []
    for s in range(slots):
        span = slice(s * blocks, (s + 1) * blocks)
        r0, q0 = start[span, :], image[span]
        norm = total(r0 * r0)
        alpha = norm / total(r0 * q0)
        r1 = r0 - alpha * q0
        norm1 = total(r1 * r1)
        p1 = r1 + norm1 / norm * r0
        direc[span, :] = p1
        scal.append((norm1, total(dsum[span] * p1 * p1)))
        mine = pl.ds(s * blocks + me * block_rows, block_rows)
        xown[s] = xin[s] + alpha * start[mine, :]
        pown[s] = direc[mine, :]
        head.append(pack[me, s, 2 * block_rows : 2 * block_rows + 1, :])
        face.append(xown[s, 0:1, :] - bound[s, count : count + 1, :])
    squares = contract(stiff, cols, lambda s, c: direc[pl.ds(s * blocks + c, 1), :], None)
    write_send(send, None, head, face, pown, scal, squares, devices)


def sixth_kernel(got, loads, diags, field, xown, pown, row_s, hot_s, resid, xout, send, window, part_s):
    slots, devices, width = row_s.shape
    rows, columns = resid.shape
    groups = lax.axis_size("grp")
    group = lax.axis_index("grp")
    flat = group * lax.axis_size("sub") + lax.axis_index("sub")
    alphas, lams = reactions(got, groups, slots)
    for s in range(slots):
        part_s[0, s, 0:groups, :] = alphas[s]
        alpha = part_s[0, s, pl.ds(group, 1), :]
        for b in range(xown.shape[1]):
            xout[s : s + 1, b * width : (b + 1) * width] = (
                xown[s, b : b + 1, :] + alpha * pown[s, b : b + 1, :]
            )
    split_lams(lams, part_s)
    placed = place(row_s, part_s, window.shape, lambda d: hot_s[d])
    span = slice(EDGE - 1, EDGE + rows + 1)
    applied = stencil(field, diags[span, :], EDGE - 1, rows + 2)
    at = iota(applied.shape, 0) + (flat * rows - 1)
    inside = (at >= 0) & (at < devices * rows)
    window[...] = jnp.zeros_like(window)
    window[span, :] = jnp.where(inside, loads[span, :] - applied + placed[span], 0.0)
    own = window[EDGE : EDGE + rows, :]
    resid[...] = own
    image = stencil(window, diags[EDGE : EDGE + rows, :], EDGE, rows)
    send[:, 0:1, :] = jnp.broadcast_to(total(own * own)[None], (devices, 1, width))
    send[:, 1:2, :] = jnp.broadcast_to(total(own * image)[None], (devices, 1, width))


def last_kernel(got, field, resid, out):
    sums = jnp.sum(got[...], axis=0)
    scale = sums[0:1, :] / sums[1:2, :]
    rows, columns = out.shape
    wide = jnp.concatenate([scale] * (columns // got.shape[2]), axis=1)
    out[...] = field[EDGE : EDGE + rows, :] + wide * resid[...]


def call(kernel, shapes, operands, scalars=0, raw=0, scratch=(), limit=4, plain=()):
    operands = [
        x if i < scalars else pltpu.with_memory_space_constraint(x, pltpu.HBM if i < scalars + raw else pltpu.VMEM)
        for i, x in enumerate(operands)
    ]
    out_shape = [
        jax.ShapeDtypeStruct(s, d) if i in plain else pltpu.VMEM(s, d) for i, (s, d) in enumerate(shapes)
    ]
    return pl.pallas_call(
        kernel,
        out_shape=out_shape,
        in_specs=[SMEM] * scalars + [VMEM] * (len(operands) - scalars),
        out_specs=[VMEM] * len(shapes),
        scratch_shapes=list(scratch),
        compiler_params=pltpu.CompilerParams(vmem_limit_bytes=limit << 20),
    )(*operands)


def body(
    stiff_blocks,
    block_cols,
    live_blocks,
    sub_diag,
    penalty,
    sub_load,
    iface_map,
    global_load,
    global_diag,
):
    slots, block_rows, per_row, width, _ = stiff_blocks.shape
    rows_dev = block_rows * width
    rows, columns = global_load.shape
    near, groups = lax.axis_size("sub"), lax.axis_size("grp")
    devices = near * groups
    blocks = slots * near * block_rows
    count = block_rows * per_row
    extent = ((rows + 2 * EDGE, columns), F32)
    own = ((slots, block_rows, width), F32)
    full = ((blocks, width), F32)
    every = ((slots, count, width), F32)
    cols = jnp.transpose(block_cols, (0, 2, 1))

    def everywhere(x):
        return lax.all_to_all(x, ALL, 0, 0)

    def near_all(x):
        return lax.all_gather(x, "sub")

    (pack,) = call(
        prep_kernel,
        [((slots, 2 * block_rows + 16, width), F32)],
        (live_blocks.reshape(slots), sub_diag, penalty, sub_load, cols, global_load, global_diag),
        scalars=1,
        raw=6,
    )
    pack = near_all(pack)
    terms, stiff = pl.pallas_call(
        first_kernel,
        out_shape=[pltpu.VMEM(every[0], F32), pltpu.VMEM(stiff_blocks.shape, F32)],
        in_specs=[SMEM, VMEM, pl.BlockSpec(memory_space=pltpu.HBM)],
        out_specs=[VMEM, VMEM],
        scratch_shapes=[pltpu.SemaphoreType.DMA((slots, block_rows))],
        compiler_params=pltpu.CompilerParams(vmem_limit_bytes=4 << 20),
    )(
        cols,
        pltpu.with_memory_space_constraint(pack, pltpu.VMEM),
        pltpu.with_memory_space_constraint(stiff_blocks, pltpu.HBM),
    )
    arrived = near_all(terms)
    resid, direc, terms, send, xown, pown = call(
        second_kernel,
        [full, full, every, ((devices, 4 * slots, width), F32), own, own],
        (cols, iface_map, pack, arrived, stiff),
        scalars=1,
        raw=1,
    )
    got = everywhere(send)
    listed = (slots, devices, width)
    parts = pltpu.VMEM((3,) + listed, F32)
    window, loads, diags, alphas, send, row_s, hot_s = call(
        third_kernel,
        [
            extent,
            extent,
            extent,
            ((slots, max(8, groups), width), F32),
            ((devices, slots + 2, width), F32),
            (listed, F32),
            ((devices, columns, slots * width), BF16),
        ],
        (global_load, global_diag, got, pack),
        raw=2,
        scratch=(parts, pltpu.VMEM(listed, F32)),
    )
    sums = everywhere(send)
    bound, field = call(
        scale_kernel, [((slots, count + 8, width), F32), extent], (sums, terms, window)
    )
    arrived = near_all(bound)
    start, terms, xown = call(
        fourth_kernel,
        [full, every, own],
        (cols, pack, arrived, alphas, resid, direc, xown, pown, stiff),
        scalars=1,
    )
    arrived = near_all(terms)
    send, xown, pown = call(
        fifth_kernel,
        [((devices, 4 * slots, width), F32), own, own],
        (cols, pack, arrived, bound, start, xown, stiff),
        scalars=1,
        scratch=(pltpu.VMEM(full[0], F32),),
    )
    got = everywhere(send)
    resid, sub_field, send = call(
        sixth_kernel,
        [((rows, columns), F32), ((slots, rows_dev), F32), ((devices, 2, width), F32)],
        (got, loads, diags, field, xown, pown, row_s, hot_s),
        scratch=(pltpu.VMEM(extent[0], F32), parts),
        plain=(1,),
    )
    sums = everywhere(send)
    (global_field,) = call(last_kernel, [((rows, columns), F32)], (sums, field, resid), plain=(0,))
    return global_field, sub_field


def solution(mesh):
    return jax.shard_map(
        body,
        mesh=mesh,
        in_specs=(
            P("grp", "sub", None, None, None),
            P("grp", "sub", None),
            P("grp", "sub"),
            P("grp", "sub"),
            P("grp", "sub"),
            P("grp", "sub"),
            P("grp", "sub"),
            P(ALL, None),
            P(ALL, None),
        ),
        out_specs=(P(ALL, None), P("grp", "sub")),
        check_vma=False,
    )
```

time: 152 us -> 108 us (0.71)
  Pallas kernels: 47.8 us -> 24.1 us
  starting transfers between devices: 8.33 us -> 0 us
  waiting for transfers between devices: 4.72 us -> 0 us
  blocking collectives: 83.6 us -> 81.1 us
  local copies, waits for them, and re-layouts: 3.68 us -> 1.34 us
  other arithmetic: 1.78 us -> 0 us
    pallas_call x9 -> x8, Pallas kernels: 47.8 us -> 18.4 us  [call(): pl.pallas_call(kernel, out_shape=out_shape, in_specs=[SMEM] * scalars + [...]
    pallas_call x0 -> x1, Pallas kernels: none -> 5.74 us  [body(): pl.pallas_call(first_kernel, out_shape=[pltpu.VMEM(every[0], F32), pltpu....]
    all_gather x4, blocking collectives: 45.2 us -> 39.7 us  [near_all(): return lax.all_gather(x, 'sub')]
    all_to_all x1 -> x0, starting transfers between devices: 4.88 us -> none  [everywhere(): return lax.all_to_all(x, ALL, 0, 0)]
    ppermute x2 -> x0, starting transfers between devices: 3.45 us -> none  [the longest x1 2.16 us: body(): before = lax.ppermute(down, ALL, hops)]
    ppermute x2 -> x0, waiting for transfers between devices: 2.89 us -> none  [the longest x1 2.88 us: body(): after = lax.ppermute(up, ALL, [(j, i) for i, j in hops])]
    all_to_all x3 -> x4, blocking collectives: 38.4 us -> 41.3 us  [everywhere(): return lax.all_to_all(x, ALL, 0, 0)]
    all_to_all x1 -> x0, waiting for transfers between devices: 1.84 us -> none  [everywhere(): return lax.all_to_all(x, ALL, 0, 0)]
  transfers between devices with their start and end apart: 3 -> 0, of which waited for: 2 -> 0; matrix products, arithmetic and copies ran while one was open for 0% -> 0% of each run, Pallas kernels for 0% -> 0%
where the time goes in v2:
time: 108 us; the launch traced here: 107 us
  blocking collectives  81.1 us (75%)
  Pallas kernels  24.1 us (22%)
  local copies, waits for them, and re-layouts  1.34 us (1%)
    all_to_all x4, blocking collectives, everywhere(): return lax.all_to_all(x, ALL, 0, 0)  41.3 us
    all_gather x4, blocking collectives, near_all(): return lax.all_gather(x, 'sub')  39.7 us
    pallas_call x8, Pallas kernels, call(): pl.pallas_call(kernel, out_shape=out_shape, in_specs=[SMEM] * scalars + [...  18.4 us
    pallas_call x1, Pallas kernels, body(): pl.pallas_call(first_kernel, out_shape=[pltpu.VMEM(every[0], F32), pltpu....  5.74 us

profile of v2, /device:TPU:0, one launch (start us, length us, event | category | flops | bytes accessed | tf_op | source)
XLA Modules:
  0.0 107.2 jit_solution(16641896415975908510)
XLA Ops:
  0.6 0.0 copy-start.2
  0.6 0.6 copy-done.2
  1.3 0.9 shard_map.104
  2.2 11.0 %all-gather = f32[16,48,128]{2,1,0:T(8,128)S(1)} all-gather(f32[2,48,128]{2,1,0:T(8,128)S(1)} %shard_map.104), channel_id=2, replica_groups=mesh['grp'=4,'sub'=8] {'sub'}, dimensions={0}, use_global_device_ids=true | all-gather | bytes 442368 | tf_op jit(solution)/shard_map/all_gather | solution.py:488
  13.2 0.0 copy-start
  13.2 0.7 copy-done
  13.9 0.0 copy-start.1
  13.9 5.7 %shard_map.105 = (f32[2,64,128]{2,1,0:T(8,128)S(1)}, f32[2,16,4,128,128]{4,3,2,1,0:T(8,128)S(1)}) custom-call(s32[2,4,16]{2,1,0:T(4,128)S(1)} %bitcast.15, f32[8,2,48,128]{3,2,1,0:T(8,128)S(1)} %bitcast.6, f32[2,16,4,128,128]{4,3,2,1,0:T(8,128)} %source.1), custom_call_target="tpu_custom_call" | custom-call | tf_op jit(solution)/shard_map/pallas_call | solution.py:498
  19.7 9.8 %all-gather.1 = f32[16,64,128]{2,1,0:T(8,128)S(1)} all-gather(f32[2,64,128]{2,1,0:T(8,128)S(1)} %get-tuple-element.28), channel_id=3, replica_groups=mesh['grp'=4,'sub'=8] {'sub'}, dimensions={0}, use_global_device_ids=true | all-gather | bytes 589824 | tf_op jit(solution)/shard_map/all_gather | solution.py:488
  29.5 3.7 %shard_map.106 = (f32[256,128]{1,0:T(8,128)S(1)}, f32[256,128]{1,0:T(8,128)S(1)}, f32[2,64,128]{2,1,0:T(8,128)S(1)}, f32[32,8,128]{2,1,0:T(8,128)S(1)}, f32[2,16...) custom-call(s32[2,4,16]{2,1,0:T(4,128)S(1)} %bitcast.16, s32[2,128]{1,0:T(2,128)} %maps.1, f32[8,2,48,128]{3,2,1,0:T(8,128)S(1)} %bitcast.7, ...), custom_call_target="tpu_custom_call" | custom-call | tf_op jit(solution)/shard_map/pallas_call | solution.py:450
  33.3 12.9 %all_to_all.20.got = f32[32,8,128]{2,1,0:T(8,128)S(1)} all-to-all(f32[32,8,128]{2,1,0:T(8,128)S(1)} %get-tuple-element.30), channel_id=1, replica_groups=mesh['grp'=4,'sub'=8] {'grp','sub'}, dimensions={0} | all-to-all | bytes 262144 | tf_op jit(solution)/shard_map/all_to_all | solution.py:485
  46.2 4.4 %shard_map.107 = (f32[48,256]{1,0:T(8,128)S(1)}, f32[48,256]{1,0:T(8,128)S(1)}, f32[48,256]{1,0:T(8,128)S(1)}, f32[2,8,128]{2,1,0:T(8,128)S(1)}, f32[32,4,128]{2...) custom-call(f32[32,256]{1,0:T(8,128)} %gload.3, f32[32,256]{1,0:T(8,128)} %gdiag.3, ...), custom_call_target="tpu_custom_call" | custom-call | tf_op jit(solution)/shard_map/pallas_call | solution.py:450
  50.6 9.2 %all_to_all.21.got = f32[32,4,128]{2,1,0:T(4,128)S(1)} all-to-all(f32[32,4,128]{2,1,0:T(4,128)S(1)} %get-tuple-element.31), channel_id=1, replica_groups=mesh['grp'=4,'sub'=8] {'grp','sub'}, dimensions={0} | all-to-all | bytes 131072 | tf_op jit(solution)/shard_map/all_to_all | solution.py:485
  59.8 9.1 %all-gather.2 = f32[16,72,128]{2,1,0:T(8,128)S(1)} all-gather(f32[2,72,128]{2,1,0:T(8,128)S(1)} %get-tuple-element.34.bound), channel_id=4, replica_groups=mesh['grp'=4,'sub'=8] {'sub'}, dimensions={0}, use_global_device_ids=true | all-gather | bytes 663552 | tf_op jit(solution)/shard_map/all_gather | solution.py:488
  68.9 0.0 copy-done.1
  68.9 3.2 %shard_map.109 = (f32[256,128]{1,0:T(8,128)S(1)}, f32[2,64,128]{2,1,0:T(8,128)S(1)}, f32[2,16,128]{2,1,0:T(8,128)S(1)}) custom-call(s32[2,4,16]{2,1,0:T(4,128)S(1)} %bitcast.17, f32[8,2,48,128]{3,2,1,0:T(8,128)S(1)} %bitcast.9, f32[8,2,72,128]{3,2,1,0:T(8,128)S(1)} %bitcast.11, f32[2,8,128]{2,1,0:T(8,128)S(1)} %get-tuple-element.35.alphas, ...), custom_call_target="tpu_custom_call" | custom-call | tf_op jit(solution)/shard_map/pallas_call | solution.py:450
  72.1 9.8 %all-gather.3 = f32[16,64,128]{2,1,0:T(8,128)S(1)} all-gather(f32[2,64,128]{2,1,0:T(8,128)S(1)} %get-tuple-element.40), channel_id=5, replica_groups=mesh['grp'=4,'sub'=8] {'sub'}, dimensions={0}, use_global_device_ids=true | all-gather | bytes 589824 | tf_op jit(solution)/shard_map/all_gather | solution.py:488
  81.9 3.3 %shard_map.110 = (f32[32,8,128]{2,1,0:T(8,128)S(1)}, f32[2,16,128]{2,1,0:T(8,128)S(1)}, f32[2,16,128]{2,1,0:T(8,128)S(1)}) custom-call(s32[2,4,16]{2,1,0:T(4,128)S(1)} %bitcast.18, f32[8,2,48,128]{3,2,1,0:T(8,128)S(1)} %bitcast.10, f32[8,2,64,128]{3,2,1,0:T(8,128)S(1)} %bitcast.12, f32[2,72,128]{2,1,0:T(8,128)S(1)} %get-tuple-element.34.bound, ...), custom_call_target="tpu_custom_call" | custom-call | tf_op jit(solution)/shard_map/pallas_call | solution.py:450
  85.2 10.2 %all_to_all.22.got = f32[32,8,128]{2,1,0:T(8,128)S(1)} all-to-all(f32[32,8,128]{2,1,0:T(8,128)S(1)} %get-tuple-element.43), channel_id=1, replica_groups=mesh['grp'=4,'sub'=8] {'grp','sub'}, dimensions={0} | all-to-all | bytes 262144 | tf_op jit(solution)/shard_map/all_to_all | solution.py:485
  95.4 2.1 %shard_map.111 = (f32[32,256]{1,0:T(8,128)S(1)}, f32[2,2048]{1,0:T(2,128)}, f32[32,2,128]{2,1,0:T(2,128)S(1)}) custom-call(f32[32,8,128]{2,1,0:T(8,128)S(1)} %all_to_all.22.got, f32[48,256]{1,0:T(8,128)S(1)} %get-tuple-element.44.loads, f32[48,256]{1,0:T(8,128)S(1)} %get-tuple-element.45.diags, f32[48,256]{1,0:T(8,128)S(1)} %get-tuple-element.46.field, ...), custom_call_target="tpu_custom_call" | custom-call | tf_op jit(solution)/shard_map/pallas_call | solution.py:450
  97.5 9.0 %all_to_all.23.got = f32[32,2,128]{2,1,0:T(2,128)S(1)} all-to-all(f32[32,2,128]{2,1,0:T(2,128)S(1)} %get-tuple-element.51), channel_id=1, replica_groups=mesh['grp'=4,'sub'=8] {'grp','sub'}, dimensions={0} | all-to-all | bytes 65536 | tf_op jit(solution)/shard_map/all_to_all | solution.py:485
  106.6 0.7 shard_map.112
  (1 shorter events, 0.0 us)
Async XLA Ops:
  0.6 0.7 copy-start.2
  13.2 0.7 copy-start
  13.9 54.9 %copy-start.1 = (s32[2,16,4]{1,2,0:T(4,128)S(1)}, s32[2,16,4]{1,2,0:T(4,128)}, u32[]{:S(2)}) copy-start(s32[2,16,4]{1,2,0:T(4,128)} %param.10) | copy-start | bytes 1540

commit v3 on v2

--- a/solution.py
+++ b/solution.py
@@ -8,7 +8,6 @@
 F32 = jnp.float32
 BF16 = jnp.bfloat16
 CHUNK = 16
-AHEAD = 10
 EDGE = 8
 ALL = ("grp", "sub")
 
@@ -51,7 +50,10 @@
                     )
             return acc + strain * strain
 
-        squares.append(lax.fori_loop(0, block_rows, row, jnp.zeros((width, 1), F32), unroll=2))
+        acc = jnp.zeros((width, 1), F32)
+        for r in range(block_rows):
+            acc = row(r, acc)
+        squares.append(acc)
     return squares
 
 
@@ -63,17 +65,20 @@
     )
 
 
-def landed(pack, arrived, block_rows, count):
-    devices, slots, _, width = pack.shape
-    targets = slots * devices * block_rows
+def targets(pack, block_rows, hot):
+    devices = pack.shape[0]
+    col = jnp.concatenate(
+        [pack[d, 0, 2 * block_rows + 1 : 2 * block_rows + 2, :] for d in range(devices)], axis=1
+    )
+    hot[...] = jnp.where(iota(hot.shape, 0).astype(F32) == col, 1.0, 0.0).astype(BF16)
+
+
+def landed(hot, arrived, count):
+    devices, slots, _, width = arrived.shape
     source = jnp.concatenate(
         [arrived[d, s, :count, :] for d in range(devices) for s in range(slots)], axis=0
     )
-    col = jnp.concatenate(
-        [pack[d, 0, 2 * block_rows + 1 : 2 * block_rows + 2, :] for d in range(devices)], axis=1
-    )
-    hot = jnp.where(iota((targets, col.shape[1]), 0).astype(F32) == col, 1.0, 0.0).astype(BF16)
-    out = jnp.dot(hot, jnp.concatenate(split3(source), axis=1), preferred_element_type=F32)
+    out = jnp.dot(hot[...], jnp.concatenate(split3(source), axis=1), preferred_element_type=F32)
     return out[:, :width] + out[:, width : 2 * width] + out[:, 2 * width :]
 
 
@@ -84,10 +89,10 @@
     blocks = block_rows * lax.axis_size("sub")
     pack[:, 2 * block_rows :, :] = jnp.zeros((slots, 16, width), F32)
     for s in range(slots):
-        count = live[s]
+        count = live[:, s : s + 1]
         for b in range(block_rows):
             lanes = pl.ds(b * width, width)
-            on = b < count
+            on = count > b
             main = diag[s : s + 1, lanes]
             if b == 0:
                 main = main + pen[s : s + 1, :]
@@ -117,31 +122,25 @@
     def copy(s, r):
         return pltpu.make_async_copy(source.at[s, r], stiff.at[s, r], sems.at[s, r])
 
-    for i in range(AHEAD):
-        copy(i // block_rows, i % block_rows).start()
-
-    def arrive(s, r):
-        copy(s, r).wait()
-        later = s * block_rows + r + AHEAD
-
-        @pl.when(later < slots * block_rows)
-        def _():
-            copy(lax.div(later, block_rows), lax.rem(later, block_rows)).start()
+    for s in range(slots):
+        for r in range(block_rows):
+            copy(s, r).start()
 
     def vector(s, c):
         return pack[lax.div(c, block_rows), s, pl.ds(lax.rem(c, block_rows), 1), :]
 
-    contract(stiff, cols, vector, terms, arrive)
-
-
-def second_kernel(cols, maps, pack, arrived, stiff, resid, direc, terms, send, xown, pown):
+    contract(stiff, cols, vector, terms, lambda s, r: copy(s, r).wait())
+
+
+def second_kernel(cols, maps, pack, arrived, stiff, resid, direc, terms, send, xown, pown, hot):
     slots, block_rows, per_row, width, _ = stiff.shape
     devices = pack.shape[0]
     blocks = devices * block_rows
     me = lax.axis_index("sub")
     start = stacked(pack, 0, block_rows)
     dsum = stacked(pack, block_rows, block_rows)
-    back = landed(pack, arrived, block_rows, block_rows * per_row)
+    targets(pack, block_rows, hot)
+    back = landed(hot, arrived, block_rows * per_row)
     image = jnp.where(dsum > 0.0, dsum * start + back, 0.0)
     head, scal = [], []
     for s in range(slots):
@@ -351,14 +350,14 @@
     field[...] = window[...] * jnp.concatenate([scale] * (field.shape[1] // width), axis=1)
 
 
-def fourth_kernel(cols, pack, arrived, alphas, resid, direc, xown, pown, stiff, start, terms, xnext):
+def fourth_kernel(cols, pack, arrived, hot, alphas, resid, direc, xown, pown, stiff, start, terms, xnext):
     slots, block_rows, per_row, width, _ = stiff.shape
     devices = pack.shape[0]
     blocks = devices * block_rows
     count = block_rows * per_row
     group = lax.axis_index("grp")
     dsum = stacked(pack, block_rows, block_rows)
-    back = landed(pack, arrived, block_rows, count)
+    back = landed(hot, arrived, count)
     p1 = direc[...]
     image = jnp.where(dsum > 0.0, dsum * p1 + back, 0.0)
     for s in range(slots):
@@ -373,14 +372,14 @@
     contract(stiff, cols, lambda s, c: start[pl.ds(s * blocks + c, 1), :], terms)
 
 
-def fifth_kernel(cols, pack, arrived, bound, start, xin, stiff, send, xown, pown, direc):
+def fifth_kernel(cols, pack, arrived, hot, bound, start, xin, stiff, send, xown, pown, direc):
     slots, block_rows, per_row, width, _ = stiff.shape
     devices = pack.shape[0]
     blocks = devices * block_rows
     count = block_rows * per_row
     me = lax.axis_index("sub")
     dsum = stacked(pack, block_rows, block_rows)
-    back = landed(pack, arrived, block_rows, count)
+    back = landed(hot, arrived, count)
     image = jnp.where(dsum > 0.0, dsum * start[...] + back, 0.0)
     head, face, scal = [], [], []
     for s in range(slots):
@@ -441,7 +440,7 @@
 
 def call(kernel, shapes, operands, scalars=0, raw=0, scratch=(), limit=4, plain=()):
     operands = [
-        x if i < scalars else pltpu.with_memory_space_constraint(x, pltpu.HBM if i < scalars + raw else pltpu.VMEM)
+        pltpu.with_memory_space_constraint(x, pltpu.HBM if i < scalars + raw else pltpu.VMEM)
         for i, x in enumerate(operands)
     ]
     out_shape = [
@@ -479,6 +478,7 @@
     own = ((slots, block_rows, width), F32)
     full = ((blocks, width), F32)
     every = ((slots, count, width), F32)
+    landing = ((blocks, near * slots * count), BF16)
     cols = jnp.transpose(block_cols, (0, 2, 1))
 
     def everywhere(x):
@@ -490,9 +490,8 @@
     (pack,) = call(
         prep_kernel,
         [((slots, 2 * block_rows + 16, width), F32)],
-        (live_blocks.reshape(slots), sub_diag, penalty, sub_load, cols, global_load, global_diag),
-        scalars=1,
-        raw=6,
+        (live_blocks.reshape(1, slots), sub_diag, penalty, sub_load, cols, global_load, global_diag),
+        raw=7,
     )
     pack = near_all(pack)
     terms, stiff = pl.pallas_call(
@@ -503,14 +502,14 @@
         scratch_shapes=[pltpu.SemaphoreType.DMA((slots, block_rows))],
         compiler_params=pltpu.CompilerParams(vmem_limit_bytes=4 << 20),
     )(
-        cols,
+        pltpu.with_memory_space_constraint(cols, pltpu.HBM),
         pltpu.with_memory_space_constraint(pack, pltpu.VMEM),
         pltpu.with_memory_space_constraint(stiff_blocks, pltpu.HBM),
     )
     arrived = near_all(terms)
-    resid, direc, terms, send, xown, pown = call(
+    resid, direc, terms, send, xown, pown, hot = call(
         second_kernel,
-        [full, full, every, ((devices, 4 * slots, width), F32), own, own],
+        [full, full, every, ((devices, 4 * slots, width), F32), own, own, landing],
         (cols, iface_map, pack, arrived, stiff),
         scalars=1,
         raw=1,
@@ -541,14 +540,14 @@
     start, terms, xown = call(
         fourth_kernel,
         [full, every, own],
-        (cols, pack, arrived, alphas, resid, direc, xown, pown, stiff),
+        (cols, pack, arrived, hot, alphas, resid, direc, xown, pown, stiff),
         scalars=1,
     )
     arrived = near_all(terms)
     send, xown, pown = call(
         fifth_kernel,
         [((devices, 4 * slots, width), F32), own, own],
-        (cols, pack, arrived, bound, start, xown, stiff),
+        (cols, pack, arrived, hot, bound, start, xown, stiff),
         scalars=1,
         scratch=(pltpu.VMEM(full[0], F32),),
     )

time: 108 us -> 103 us (0.954)
  Pallas kernels: 24.1 us -> 21.1 us
  local copies, waits for them, and re-layouts: 1.34 us -> 0 us
    pallas_call x8, Pallas kernels: 18.4 us -> 15.3 us  [call(): pl.pallas_call(kernel, out_shape=out_shape, in_specs=[SMEM] * scalars + [...]
    unnamed x6 -> x0, local copies, waits for them, and re-layouts: 1.34 us -> none
where the time goes in v3:
time: 103 us
  blocking collectives  81.1 us (79%)
  Pallas kernels  21.1 us (20%)
    all_to_all x4, blocking collectives, everywhere(): return lax.all_to_all(x, ALL, 0, 0)  41.3 us
    all_gather x4, blocking collectives, near_all(): return lax.all_gather(x, 'sub')  39.8 us
    pallas_call x8, Pallas kernels, call(): pl.pallas_call(kernel, out_shape=out_shape, in_specs=[SMEM] * scalars + [...  15.3 us
    pallas_call x1, Pallas kernels, body(): pl.pallas_call(first_kernel, out_shape=[pltpu.VMEM(every[0], F32), pltpu....  5.76 us

profile of v3, /device:TPU:0, one launch (start us, length us, event | category | flops | bytes accessed | tf_op | source)
XLA Modules:
  0.0 102.9 jit_solution(8605519312037661294)
XLA Ops:
  0.6 1.0 shard_map.104
  1.6 11.0 %all-gather = f32[16,48,128]{2,1,0:T(8,128)S(1)} all-gather(f32[2,48,128]{2,1,0:T(8,128)S(1)} %shard_map.104), channel_id=2, replica_groups=mesh['grp'=4,'sub'=8] {'sub'}, dimensions={0}, use_global_device_ids=true | all-gather | bytes 442368 | tf_op jit(solution)/shard_map/all_gather | solution.py:488
  12.6 5.8 %shard_map.105 = (f32[2,64,128]{2,1,0:T(8,128)S(1)}, f32[2,16,4,128,128]{4,3,2,1,0:T(8,128)S(1)}) custom-call(s32[2,4,16]{2,1,0:T(4,128)} %bitcast.15, f32[8,2,48,128]{3,2,1,0:T(8,128)S(1)} %bitcast.6, f32[2,16,4,128,128]{4,3,2,1,0:T(8,128)} %source.1), custom_call_target="tpu_custom_call" | custom-call | tf_op jit(solution)/shard_map/pallas_call | solution.py:497
  18.4 9.8 %all-gather.1 = f32[16,64,128]{2,1,0:T(8,128)S(1)} all-gather(f32[2,64,128]{2,1,0:T(8,128)S(1)} %get-tuple-element.29), channel_id=3, replica_groups=mesh['grp'=4,'sub'=8] {'sub'}, dimensions={0}, use_global_device_ids=true | all-gather | bytes 589824 | tf_op jit(solution)/shard_map/all_gather | solution.py:488
  28.3 2.7 %shard_map.106 = (f32[256,128]{1,0:T(8,128)S(1)}, f32[256,128]{1,0:T(8,128)S(1)}, f32[2,64,128]{2,1,0:T(8,128)S(1)}, f32[32,8,128]{2,1,0:T(8,128)S(1)}, f32[2,16...) custom-call(s32[2,4,16]{2,1,0:T(4,128)} %bitcast.16, s32[2,128]{1,0:T(2,128)} %maps.1, ...), custom_call_target="tpu_custom_call" | custom-call | tf_op jit(solution)/shard_map/pallas_call | solution.py:449
  31.0 12.9 %all_to_all.20.got = f32[32,8,128]{2,1,0:T(8,128)S(1)} all-to-all(f32[32,8,128]{2,1,0:T(8,128)S(1)} %get-tuple-element.31), channel_id=1, replica_groups=mesh['grp'=4,'sub'=8] {'grp','sub'}, dimensions={0} | all-to-all | bytes 262144 | tf_op jit(solution)/shard_map/all_to_all | solution.py:485
  43.9 4.4 %shard_map.107 = (f32[48,256]{1,0:T(8,128)S(1)}, f32[48,256]{1,0:T(8,128)S(1)}, f32[48,256]{1,0:T(8,128)S(1)}, f32[2,8,128]{2,1,0:T(8,128)S(1)}, f32[32,4,128]{2...) custom-call(f32[32,256]{1,0:T(8,128)} %gload.3, f32[32,256]{1,0:T(8,128)} %gdiag.3, ...), custom_call_target="tpu_custom_call" | custom-call | tf_op jit(solution)/shard_map/pallas_call | solution.py:449
  48.3 9.2 %all_to_all.21.got = f32[32,4,128]{2,1,0:T(4,128)S(1)} all-to-all(f32[32,4,128]{2,1,0:T(4,128)S(1)} %get-tuple-element.32), channel_id=1, replica_groups=mesh['grp'=4,'sub'=8] {'grp','sub'}, dimensions={0} | all-to-all | bytes 131072 | tf_op jit(solution)/shard_map/all_to_all | solution.py:485
  57.5 9.1 %all-gather.2 = f32[16,72,128]{2,1,0:T(8,128)S(1)} all-gather(f32[2,72,128]{2,1,0:T(8,128)S(1)} %get-tuple-element.35.bound), channel_id=4, replica_groups=mesh['grp'=4,'sub'=8] {'sub'}, dimensions={0}, use_global_device_ids=true | all-gather | bytes 663552 | tf_op jit(solution)/shard_map/all_gather | solution.py:488
  66.6 2.3 %shard_map.109 = (f32[256,128]{1,0:T(8,128)S(1)}, f32[2,64,128]{2,1,0:T(8,128)S(1)}, f32[2,16,128]{2,1,0:T(8,128)S(1)}) custom-call(s32[2,4,16]{2,1,0:T(4,128)} %bitcast.17, f32[8,2,48,128]{3,2,1,0:T(8,128)S(1)} %bitcast.9, f32[8,2,72,128]{3,2,1,0:T(8,128)S(1)} %bitcast.11, bf16[256,1024]{1,0:T(8,128)(2,1)S(1)} %get-tuple-element.36.hot, ...), custom_call_target="tpu_custom_call" | custom-call | tf_op jit(solution)/shard_map/pallas_call | solution.py:449
  68.9 9.8 %all-gather.3 = f32[16,64,128]{2,1,0:T(8,128)S(1)} all-gather(f32[2,64,128]{2,1,0:T(8,128)S(1)} %get-tuple-element.42), channel_id=5, replica_groups=mesh['grp'=4,'sub'=8] {'sub'}, dimensions={0}, use_global_device_ids=true | all-gather | bytes 589824 | tf_op jit(solution)/shard_map/all_gather | solution.py:488
  78.7 2.1 %shard_map.110 = (f32[32,8,128]{2,1,0:T(8,128)S(1)}, f32[2,16,128]{2,1,0:T(8,128)S(1)}, f32[2,16,128]{2,1,0:T(8,128)S(1)}) custom-call(s32[2,4,16]{2,1,0:T(4,128)} %bitcast.18, f32[8,2,48,128]{3,2,1,0:T(8,128)S(1)} %bitcast.10, f32[8,2,64,128]{3,2,1,0:T(8,128)S(1)} %bitcast.13, bf16[256,1024]{1,0:T(8,128)(2,1)S(1)} %get-tuple-element.36.hot, ...), custom_call_target="tpu_custom_call" | custom-call | tf_op jit(solution)/shard_map/pallas_call | solution.py:449
  80.8 10.2 %all_to_all.22.got = f32[32,8,128]{2,1,0:T(8,128)S(1)} all-to-all(f32[32,8,128]{2,1,0:T(8,128)S(1)} %get-tuple-element.45), channel_id=1, replica_groups=mesh['grp'=4,'sub'=8] {'grp','sub'}, dimensions={0} | all-to-all | bytes 262144 | tf_op jit(solution)/shard_map/all_to_all | solution.py:485
  91.1 2.1 %shard_map.111 = (f32[32,256]{1,0:T(8,128)S(1)}, f32[2,2048]{1,0:T(2,128)}, f32[32,2,128]{2,1,0:T(2,128)S(1)}) custom-call(f32[32,8,128]{2,1,0:T(8,128)S(1)} %all_to_all.22.got, f32[48,256]{1,0:T(8,128)S(1)} %get-tuple-element.46.loads, f32[48,256]{1,0:T(8,128)S(1)} %get-tuple-element.47.diags, f32[48,256]{1,0:T(8,128)S(1)} %get-tuple-element.48.field, ...), custom_call_target="tpu_custom_call" | custom-call | tf_op jit(solution)/shard_map/pallas_call | solution.py:449
  93.2 9.0 %all_to_all.23.got = f32[32,2,128]{2,1,0:T(2,128)S(1)} all-to-all(f32[32,2,128]{2,1,0:T(2,128)S(1)} %get-tuple-element.53), channel_id=1, replica_groups=mesh['grp'=4,'sub'=8] {'grp','sub'}, dimensions={0} | all-to-all | bytes 65536 | tf_op jit(solution)/shard_map/all_to_all | solution.py:485
  102.2 0.7 shard_map.112
  (1 shorter events, 0.0 us)

commit v4 on v3

--- a/solution.py
+++ b/solution.py
@@ -65,11 +65,8 @@
     )
 
 
-def targets(pack, block_rows, hot):
-    devices = pack.shape[0]
-    col = jnp.concatenate(
-        [pack[d, 0, 2 * block_rows + 1 : 2 * block_rows + 2, :] for d in range(devices)], axis=1
-    )
+def targets(pack, row, hot):
+    col = jnp.concatenate([pack[d, 0, row : row + 1, :] for d in range(pack.shape[0])], axis=1)
     hot[...] = jnp.where(iota(hot.shape, 0).astype(F32) == col, 1.0, 0.0).astype(BF16)
 
 
@@ -82,12 +79,12 @@
     return out[:, :width] + out[:, width : 2 * width] + out[:, 2 * width :]
 
 
-def prep_kernel(live, diag, pen, load, cols, gload, gdiag, pack):
-    slots, rows, width = pack.shape
-    block_rows = (rows - 16) // 2
+def prep_kernel(live, diag, pen, load, cols, maps, gload, gdiag, send, rest, cols_out, maps_out, loads, diags):
+    slots, block_rows, width = send.shape[1:]
     per_row = cols.shape[1]
     blocks = block_rows * lax.axis_size("sub")
-    pack[:, 2 * block_rows :, :] = jnp.zeros((slots, 16, width), F32)
+    first, rows = [], gload.shape[0]
+    rest[...] = jnp.zeros_like(rest)
     for s in range(slots):
         count = live[:, s : s + 1]
         for b in range(block_rows):
@@ -96,51 +93,71 @@
             main = diag[s : s + 1, lanes]
             if b == 0:
                 main = main + pen[s : s + 1, :]
-            pack[s, b : b + 1, :] = jnp.where(on, load[s : s + 1, lanes], 0.0)
-            pack[s, block_rows + b : block_rows + b + 1, :] = jnp.where(on, main, 0.0)
-        pack[s, 2 * block_rows : 2 * block_rows + 1, :] = pen[s : s + 1, :]
+            first.append(jnp.where(on, load[s : s + 1, lanes], 0.0))
+            rest[s, b : b + 1, :] = jnp.where(on, main, 0.0)
+        rest[s, block_rows : block_rows + 1, :] = pen[s : s + 1, :]
         for n in range(per_row):
             at = (s * per_row + n) * block_rows
-            pack[0, 2 * block_rows + 1 : 2 * block_rows + 2, at : at + block_rows] = (
+            rest[0, block_rows + 1 : block_rows + 2, at : at + block_rows] = (
                 cols[s, n : n + 1, :] + s * blocks
             ).astype(F32)
-    last = gload.shape[0] - 1
+    all_first = jnp.concatenate(first, axis=0).reshape(1, slots, block_rows, width)
+    send[...] = jnp.broadcast_to(all_first, send.shape)
+    cols_out[...] = cols[...]
+    maps_out[...] = maps[...].astype(F32)
+    loads[...] = jnp.zeros_like(loads)
+    diags[...] = jnp.zeros_like(diags)
+    loads[EDGE : EDGE + rows, :] = gload[...]
+    diags[EDGE : EDGE + rows, :] = gdiag[...]
+    last = rows - 1
     half = gload.shape[1] // width
-    edge = 2 * block_rows + 8
+    edge = block_rows + 8
     for side, picks in enumerate(
         (((gload, 0), (gload, 1), (gdiag, 0)), ((gload, last - 1), (gload, last), (gdiag, last)))
     ):
         for k, (ref, row) in enumerate(picks):
             for h in range(half):
                 at = edge + k * half + h
-                pack[side, at : at + 1, :] = ref[row : row + 1, h * width : (h + 1) * width]
-
-
-def first_kernel(cols, pack, source, terms, stiff, sems):
+                rest[side, at : at + 1, :] = ref[row : row + 1, h * width : (h + 1) * width]
+
+
+def first_kernel(cols, start, rest, source, terms, stiff, sems):
     slots, block_rows = stiff.shape[:2]
 
-    def copy(s, r):
-        return pltpu.make_async_copy(source.at[s, r], stiff.at[s, r], sems.at[s, r])
-
-    for s in range(slots):
-        for r in range(block_rows):
-            copy(s, r).start()
+    steps = [(s, k) for s in range(slots) for k in range(0, block_rows, 4)]
+
+    def copy(i):
+        s, k = steps[i]
+        rows = pl.ds(k, 4)
+        return pltpu.make_async_copy(source.at[s, rows], stiff.at[s, rows], sems.at[s, k])
+
+    for i in range(4):
+        copy(i).start()
+
+    def arrive(s, r):
+        if r % 4 == 0:
+            i = steps.index((s, r))
+            copy(i).wait()
+            if i + 4 < len(steps):
+                copy(i + 4).start()
 
     def vector(s, c):
-        return pack[lax.div(c, block_rows), s, pl.ds(lax.rem(c, block_rows), 1), :]
-
-    contract(stiff, cols, vector, terms, lambda s, r: copy(s, r).wait())
-
-
-def second_kernel(cols, maps, pack, arrived, stiff, resid, direc, terms, send, xown, pown, hot):
+        return start[lax.div(c, block_rows), s, pl.ds(lax.rem(c, block_rows), 1), :]
+
+    terms[:, block_rows * stiff.shape[2] :, :] = rest[...]
+    contract(stiff, cols, vector, terms, arrive)
+
+
+def second_kernel(cols, maps, first, pack, stiff, resid, direc, terms, send, xown, pown, hot):
     slots, block_rows, per_row, width, _ = stiff.shape
     devices = pack.shape[0]
     blocks = devices * block_rows
+    count = block_rows * per_row
     me = lax.axis_index("sub")
-    start = stacked(pack, 0, block_rows)
-    dsum = stacked(pack, block_rows, block_rows)
-    targets(pack, block_rows, hot)
-    back = landed(hot, arrived, block_rows * per_row)
+    start = stacked(first, 0, block_rows)
+    dsum = stacked(pack, count, block_rows)
+    targets(pack, count + block_rows + 1, hot)
+    back = landed(hot, pack, count)
     image = jnp.where(dsum > 0.0, dsum * start + back, 0.0)
     head, scal = [], []
     for s in range(slots):
@@ -154,15 +171,15 @@
         resid[span, :] = r1
         direc[span, :] = p1
         scal.append((norm1, total(dsum[span] * p1 * p1)))
-        xown[s] = alpha * pack[me, s, :block_rows, :]
+        xown[s] = alpha * first[me, s]
         pown[s] = direc[pl.ds(s * blocks + me * block_rows, block_rows), :]
-        head.append(pack[me, s, 2 * block_rows : 2 * block_rows + 1, :])
+        head.append(pack[me, s, count + block_rows : count + block_rows + 1, :])
     squares = contract(stiff, cols, lambda s, c: direc[pl.ds(s * blocks + c, 1), :], terms)
     write_send(send, maps, head, [xown[s, 0:1, :] for s in range(slots)], pown, scal, squares, devices)
     everyone, used = send.shape[0], 3 * slots + 1
     group = lax.axis_index("grp")
     groups = everyone // devices
-    edge = 2 * block_rows + 8
+    edge = count + block_rows + 8
     send[:, used : used + 1, :] = jnp.zeros((everyone, 1, width), F32)
 
     @pl.when((group > 0) & (me < 8))
@@ -182,7 +199,7 @@
     if maps is None:
         rows += [jnp.zeros((slots, width), F32)]
     else:
-        rows += [maps[...].astype(F32)]
+        rows += [maps[...]]
     row = jnp.zeros((1, width), F32)
     for s in range(slots):
         norm1, own = scal[s]
@@ -259,8 +276,8 @@
     return (4.0 + gdiag) * here - (above + below + left + right)
 
 
-def third_kernel(gload, gdiag, got, pack, window, loads, diags, alphas_out, send, row_s, hot_s, part_s, col_s):
-    rows, columns = gload.shape
+def third_kernel(got, pack, loads_in, diags_in, window, loads, diags, alphas_out, send, row_s, hot_s, part_s, col_s):
+    rows, columns = window.shape[0] - 2 * EDGE, window.shape[1]
     slots, devices, width = row_s.shape
     groups = lax.axis_size("grp")
     flat = lax.axis_index("grp") * lax.axis_size("sub") + lax.axis_index("sub")
@@ -277,10 +294,8 @@
     me, group = lax.axis_index("sub"), lax.axis_index("grp")
     near = devices // groups
     half, edge, spare = columns // width, pack.shape[2] - 8, 3 * slots + 1
-    loads[...] = jnp.zeros_like(loads)
-    diags[...] = jnp.zeros_like(diags)
-    loads[EDGE : EDGE + rows, :] = gload[...]
-    diags[EDGE : EDGE + rows, :] = gdiag[...]
+    loads[...] = loads_in[...]
+    diags[...] = diags_in[...]
     last = EDGE + rows
 
     def fill(side, row_of):
@@ -321,54 +336,65 @@
     inside = (at >= EDGE - 2) & (at < last + 2)
     window[...] = loads[...] + jnp.where(inside, placed, 0.0)
     own = window[EDGE:last, :]
-    image = stencil(window, gdiag[...], EDGE, rows)
-    send[:, slots : slots + 1, :] = jnp.broadcast_to(total(own * own)[None], (devices, 1, width))
-    send[:, slots + 1 : slots + 2, :] = jnp.broadcast_to(total(own * image)[None], (devices, 1, width))
+    image = stencil(window, diags[EDGE:last, :], EDGE, rows)
+    faces = slots * near
+    send[:, faces:, :] = jnp.zeros((groups, send.shape[1] - faces, width), F32)
+    send[:, faces : faces + 1, :] = jnp.broadcast_to(total(own * own)[None], (groups, 1, width))
+    send[:, faces + 1 : faces + 2, :] = jnp.broadcast_to(total(own * image)[None], (groups, 1, width))
     parts = jnp.concatenate(split3(own), axis=0)
     ids = iota((rows, 1), 0).astype(F32) + EDGE
 
-    def step(d, carry):
-        seen = jnp.dot(parts, hot_s[d], preferred_element_type=F32)
-        seen = seen[:rows] + seen[rows : 2 * rows] + seen[2 * rows :]
-        hit = ids == lanes_of(row_s, d, slots)
-        mine = jnp.sum(jnp.where(hit, seen, 0.0), axis=0, keepdims=True)
-        for s in range(slots):
-            send[d, s : s + 1, :] = mine[:, s * width : (s + 1) * width]
-        return carry
-
-    lax.fori_loop(0, devices, step, 0, unroll=8)
-
-
-def scale_kernel(got, terms, window, send, field):
+    for g in range(groups):
+        for k in range(near):
+            d = g * near + k
+            seen = jnp.dot(parts, hot_s[d], preferred_element_type=F32)
+            seen = seen[:rows] + seen[rows : 2 * rows] + seen[2 * rows :]
+            hit = ids == lanes_of(row_s, d, slots)
+            mine = jnp.sum(jnp.where(hit, seen, 0.0), axis=0, keepdims=True)
+            for s in range(slots):
+                send[g, s * near + k : s * near + k + 1, :] = mine[:, s * width : (s + 1) * width]
+
+
+def share_kernel(got, terms, send):
     slots, count, width = terms.shape
-    sums = jnp.sum(got[...], axis=0)
-    scale = sums[slots : slots + 1, :] / sums[slots + 1 : slots + 2, :]
+    near = lax.axis_size("sub")
+    sums = got[0]
+    for g in range(1, got.shape[0]):
+        sums = sums + got[g]
     send[:, :count, :] = terms[...]
-    send[:, count:, :] = jnp.zeros((slots, send.shape[1] - count, width), F32)
-    for s in range(slots):
-        send[s, count : count + 1, :] = scale * sums[s : s + 1, :]
-    field[...] = window[...] * jnp.concatenate([scale] * (field.shape[1] // width), axis=1)
-
-
-def fourth_kernel(cols, pack, arrived, hot, alphas, resid, direc, xown, pown, stiff, start, terms, xnext):
+    for s in range(slots):
+        send[s, count : count + near, :] = sums[s * near : (s + 1) * near, :]
+        send[s, count + near :, :] = sums[slots * near : slots * near + 8, :]
+
+
+def fourth_kernel(
+    cols, pack, arrived, hot, window, alphas, resid, direc, xown, pown, stiff, start, terms, xnext, face, field
+):
     slots, block_rows, per_row, width, _ = stiff.shape
     devices = pack.shape[0]
     blocks = devices * block_rows
     count = block_rows * per_row
     group = lax.axis_index("grp")
-    dsum = stacked(pack, block_rows, block_rows)
+    me = lax.axis_index("sub")
+    dsum = stacked(pack, count, block_rows)
     back = landed(hot, arrived, count)
     p1 = direc[...]
     image = jnp.where(dsum > 0.0, dsum * p1 + back, 0.0)
+    tail = arrived[0, :, count:, :]
+    for d in range(1, devices):
+        tail = tail + arrived[d, :, count:, :]
+    scale = tail[0, devices : devices + 1, :] / tail[0, devices + 1 : devices + 2, :]
+    field[...] = window[...] * jnp.concatenate([scale] * (field.shape[1] // width), axis=1)
     for s in range(slots):
         span = slice(s * blocks, (s + 1) * blocks)
         alpha = alphas[s, pl.ds(group, 1), :]
         start[span, :] = resid[span, :] - alpha * image[span]
         xnext[s] = xown[s] + alpha * pown[s]
+        face[s, :devices, :] = scale * tail[s, :devices, :]
         for d in range(devices):
-            face = slice(s * blocks + d * block_rows, s * blocks + d * block_rows + 1)
-            pen = pack[d, s, 2 * block_rows : 2 * block_rows + 1, :]
-            start[face, :] = start[face, :] + pen * arrived[d, s, count : count + 1, :]
+            at = slice(s * blocks + d * block_rows, s * blocks + d * block_rows + 1)
+            pen = pack[d, s, count + block_rows : count + block_rows + 1, :]
+            start[at, :] = start[at, :] + pen * face[s, d : d + 1, :]
     contract(stiff, cols, lambda s, c: start[pl.ds(s * blocks + c, 1), :], terms)
 
 
@@ -378,7 +404,7 @@
     blocks = devices * block_rows
     count = block_rows * per_row
     me = lax.axis_index("sub")
-    dsum = stacked(pack, block_rows, block_rows)
+    dsum = stacked(pack, count, block_rows)
     back = landed(hot, arrived, count)
     image = jnp.where(dsum > 0.0, dsum * start[...] + back, 0.0)
     head, face, scal = [], [], []
@@ -395,8 +421,8 @@
         mine = pl.ds(s * blocks + me * block_rows, block_rows)
         xown[s] = xin[s] + alpha * start[mine, :]
         pown[s] = direc[mine, :]
-        head.append(pack[me, s, 2 * block_rows : 2 * block_rows + 1, :])
-        face.append(xown[s, 0:1, :] - bound[s, count : count + 1, :])
+        head.append(pack[me, s, count + block_rows : count + block_rows + 1, :])
+        face.append(xown[s, 0:1, :] - bound[s, pl.ds(me, 1), :])
     squares = contract(stiff, cols, lambda s, c: direc[pl.ds(s * blocks + c, 1), :], None)
     write_send(send, None, head, face, pown, scal, squares, devices)
 
@@ -440,7 +466,7 @@
 
 def call(kernel, shapes, operands, scalars=0, raw=0, scratch=(), limit=4, plain=()):
     operands = [
-        pltpu.with_memory_space_constraint(x, pltpu.HBM if i < scalars + raw else pltpu.VMEM)
+        pltpu.with_memory_space_constraint(x, pltpu.HBM if i < raw else pltpu.VMEM)
         for i, x in enumerate(operands)
     ]
     out_shape = [
@@ -487,32 +513,40 @@
     def near_all(x):
         return lax.all_gather(x, "sub")
 
-    (pack,) = call(
+    send, rest, cols, maps, loads, diags = call(
         prep_kernel,
-        [((slots, 2 * block_rows + 16, width), F32)],
-        (live_blocks.reshape(1, slots), sub_diag, penalty, sub_load, cols, global_load, global_diag),
-        raw=7,
-    )
-    pack = near_all(pack)
+        [
+            ((near, slots, block_rows, width), F32),
+            ((slots, block_rows + 16, width), F32),
+            (cols.shape, jnp.int32),
+            (iface_map.shape, F32),
+            extent,
+            extent,
+        ],
+        (live_blocks.reshape(1, slots), sub_diag, penalty, sub_load, cols, iface_map, global_load, global_diag),
+        raw=8,
+    )
+    first = lax.all_to_all(send, "sub", 0, 0)
     terms, stiff = pl.pallas_call(
         first_kernel,
-        out_shape=[pltpu.VMEM(every[0], F32), pltpu.VMEM(stiff_blocks.shape, F32)],
-        in_specs=[SMEM, VMEM, pl.BlockSpec(memory_space=pltpu.HBM)],
+        out_shape=[
+            pltpu.VMEM((slots, count + rest.shape[1], width), F32),
+            pltpu.VMEM(stiff_blocks.shape, F32),
+        ],
+        in_specs=[SMEM, VMEM, VMEM, pl.BlockSpec(memory_space=pltpu.HBM)],
         out_specs=[VMEM, VMEM],
         scratch_shapes=[pltpu.SemaphoreType.DMA((slots, block_rows))],
         compiler_params=pltpu.CompilerParams(vmem_limit_bytes=4 << 20),
     )(
-        pltpu.with_memory_space_constraint(cols, pltpu.HBM),
-        pltpu.with_memory_space_constraint(pack, pltpu.VMEM),
+        *[pltpu.with_memory_space_constraint(x, pltpu.VMEM) for x in (cols, first, rest)],
         pltpu.with_memory_space_constraint(stiff_blocks, pltpu.HBM),
     )
-    arrived = near_all(terms)
+    pack = near_all(terms)
     resid, direc, terms, send, xown, pown, hot = call(
         second_kernel,
         [full, full, every, ((devices, 4 * slots, width), F32), own, own, landing],
-        (cols, iface_map, pack, arrived, stiff),
+        (cols, maps, first, pack, stiff),
         scalars=1,
-        raw=1,
     )
     got = everywhere(send)
     listed = (slots, devices, width)
@@ -524,23 +558,20 @@
             extent,
             extent,
             ((slots, max(8, groups), width), F32),
-            ((devices, slots + 2, width), F32),
+            ((groups, slots * near + 8, width), F32),
             (listed, F32),
             ((devices, columns, slots * width), BF16),
         ],
-        (global_load, global_diag, got, pack),
-        raw=2,
+        (got, pack, loads, diags),
         scratch=(parts, pltpu.VMEM(listed, F32)),
     )
-    sums = everywhere(send)
-    bound, field = call(
-        scale_kernel, [((slots, count + 8, width), F32), extent], (sums, terms, window)
-    )
-    arrived = near_all(bound)
-    start, terms, xown = call(
+    sums = lax.all_to_all(send, "grp", 0, 0)
+    (send,) = call(share_kernel, [((slots, count + near + 8, width), F32)], (sums, terms))
+    arrived = near_all(send)
+    start, terms, xown, bound, field = call(
         fourth_kernel,
-        [full, every, own],
-        (cols, pack, arrived, hot, alphas, resid, direc, xown, pown, stiff),
+        [full, every, own, ((slots, max(8, near), width), F32), extent],
+        (cols, pack, arrived, hot, window, alphas, resid, direc, xown, pown, stiff),
         scalars=1,
     )
     arrived = near_all(terms)

time: 103 us -> 98.5 us (0.956)
  Pallas kernels: 21.1 us -> 18.2 us
  blocking collectives: 81.1 us -> 79.1 us
    all_to_all x0 -> x2, blocking collectives: none -> 18.6 us  [the longest x1 10.5 us: body(): first = lax.all_to_all(send, 'sub', 0, 0)]
    all_gather x4 -> x3, blocking collectives: 39.8 us -> 28.5 us  [near_all(): return lax.all_gather(x, 'sub')]
    all_to_all x4 -> x3, blocking collectives: 41.3 us -> 32.1 us  [everywhere(): return lax.all_to_all(x, ALL, 0, 0)]
    pallas_call x8, Pallas kernels: 15.3 us -> 13.5 us  [call(): pl.pallas_call(kernel, out_shape=out_shape, in_specs=[SMEM] * scalars + [...]
    pallas_call x1, Pallas kernels: 5.76 us -> 4.7 us  [body(): pl.pallas_call(first_kernel, out_shape=[pltpu.VMEM((slots, count + rest.s...]
where the time goes in v4:
time: 98.5 us; the launch traced here: 98.1 us
  blocking collectives  79.1 us (80%)
  Pallas kernels  18.2 us (18%)
    all_to_all x3, blocking collectives, everywhere(): return lax.all_to_all(x, ALL, 0, 0)  32.1 us
    all_gather x3, blocking collectives, near_all(): return lax.all_gather(x, 'sub')  28.5 us
    pallas_call x8, Pallas kernels, call(): pl.pallas_call(kernel, out_shape=out_shape, in_specs=[SMEM] * scalars + [...  13.5 us
    all_to_all x1, blocking collectives, body(): first = lax.all_to_all(send, 'sub', 0, 0)  10.5 us
    all_to_all x1, blocking collectives, body(): sums = lax.all_to_all(send, 'grp', 0, 0)  8.09 us
    pallas_call x1, Pallas kernels, body(): pl.pallas_call(first_kernel, out_shape=[pltpu.VMEM((slots, count + rest.s...  4.7 us

profile of v4, /device:TPU:0, one launch (start us, length us, event | category | flops | bytes accessed | tf_op | source)
XLA Modules:
  0.0 98.1 jit_solution(5156392586057031155)
XLA Ops:
  0.6 1.0 %shard_map.104 = (f32[8,2,16,128]{3,2,1,0:T(8,128)S(1)}, f32[2,32,128]{2,1,0:T(8,128)S(1)}, s32[2,4,16]{2,1,0:T(4,128)S(1)}, f32[2,128]{1,0:T(2,128)S(1)}, f32[48,256]{1,0:T(8,128)S(1)}, /*index=5*/f32[48,256]{1,0:T(8,128)S(1)}) custom-call(s32[1,2]{1,0:T(1,128)} %bitcast.12, f32[2,2048]{1,0:T(2,128)} %diag.1, f32[2,128]{1,0:T(2,128)} %pen.1, ...), custom_call_target="tpu_custom_call" | custom-call | tf_op jit(solution)/shard_map/pallas_call | solution.py:475
  1.6 10.5 %all_to_all.25.start.first = f32[8,2,16,128]{3,2,1,0:T(8,128)S(1)} all-to-all(f32[8,2,16,128]{3,2,1,0:T(8,128)S(1)} %get-tuple-element.36), channel_id=1, replica_groups=mesh['grp'=4,'sub'=8] {'sub'}, dimensions={0} | all-to-all | bytes 262144 | tf_op jit(solution)/shard_map/all_to_all | solution.py:529
  12.1 4.7 %shard_map.105 = (f32[2,96,128]{2,1,0:T(8,128)S(1)}, f32[2,16,4,128,128]{4,3,2,1,0:T(8,128)S(1)}) custom-call(s32[2,4,16]{2,1,0:T(4,128)S(1)} %get-tuple-element.35.cols, f32[8,2,16,128]{3,2,1,0:T(8,128)S(1)} %all_to_all.25.start.first, f32[2,32,128]{2,1,0:T(8,128)S(1)} %get-tuple-element.37.rest, f32[2,16,4,128,128]{4,3,2,1,0:T(8,128)} %source.1), custom_call_target="tpu_custom_call" | custom-call | tf_op jit(solution)/shard_map/pallas_call | solution.py:530
  16.8 9.5 %all-gather = f32[16,96,128]{2,1,0:T(8,128)S(1)} all-gather(f32[2,96,128]{2,1,0:T(8,128)S(1)} %get-tuple-element.38), channel_id=2, replica_groups=mesh['grp'=4,'sub'=8] {'sub'}, dimensions={0}, use_global_device_ids=true | all-gather | bytes 884736 | tf_op jit(solution)/shard_map/all_gather | solution.py:514
  26.3 2.6 %shard_map.106 = (f32[256,128]{1,0:T(8,128)S(1)}, f32[256,128]{1,0:T(8,128)S(1)}, f32[2,64,128]{2,1,0:T(8,128)S(1)}, f32[32,8,128]{2,1,0:T(8,128)S(1)}, f32[2,16...) custom-call(s32[2,4,16]{2,1,0:T(4,128)S(1)} %get-tuple-element.35.cols, ...), custom_call_target="tpu_custom_call" | custom-call | tf_op jit(solution)/shard_map/pallas_call | solution.py:475
  28.9 12.9 %all_to_all.26.got = f32[32,8,128]{2,1,0:T(8,128)S(1)} all-to-all(f32[32,8,128]{2,1,0:T(8,128)S(1)} %get-tuple-element.41), channel_id=1, replica_groups=mesh['grp'=4,'sub'=8] {'grp','sub'}, dimensions={0} | all-to-all | bytes 262144 | tf_op jit(solution)/shard_map/all_to_all | solution.py:511
  41.8 3.0 %shard_map.107 = (f32[48,256]{1,0:T(8,128)S(1)}, f32[48,256]{1,0:T(8,128)S(1)}, f32[48,256]{1,0:T(8,128)S(1)}, f32[2,8,128]{2,1,0:T(8,128)S(1)}, f32[4,24,128]{2...) custom-call(f32[32,8,128]{2,1,0:T(8,128)S(1)} %all_to_all.26.got, ...), custom_call_target="tpu_custom_call" | custom-call | tf_op jit(solution)/shard_map/pallas_call | solution.py:475
  44.8 8.1 %all_to_all.27.got = f32[4,24,128]{2,1,0:T(8,128)S(1)} all-to-all(f32[4,24,128]{2,1,0:T(8,128)S(1)} %get-tuple-element.44), channel_id=1, replica_groups=mesh['grp'=4,'sub'=8] {'grp'}, dimensions={0} | all-to-all | bytes 98304 | tf_op jit(solution)/shard_map/all_to_all | solution.py:568
  52.9 9.3 %all-gather.1 = f32[16,80,128]{2,1,0:T(8,128)S(1)} all-gather(f32[2,80,128]{2,1,0:T(8,128)S(1)} %shard_map.108), channel_id=3, replica_groups=mesh['grp'=4,'sub'=8] {'sub'}, dimensions={0}, use_global_device_ids=true | all-gather | bytes 737280 | tf_op jit(solution)/shard_map/all_gather | solution.py:514
  62.2 2.2 %shard_map.109 = (f32[256,128]{1,0:T(8,128)S(1)}, f32[2,64,128]{2,1,0:T(8,128)S(1)}, f32[2,16,128]{2,1,0:T(8,128)S(1)}, f32[2,8,128]{2,1,0:T(8,128)S(1)}, f32[48,256]{1,0:T(8,128)S(1)}) custom-call(s32[2,4,16]{2,1,0:T(4,128)S(1)} %get-tuple-element.35.cols, f32[8,2,96,128]{3,2,1,0:T(8,128)S(1)} %bitcast.7, f32[8,2,80,128]{3,2,1,0:T(8,128)S(1)} %bitcast.9, ...), custom_call_target="tpu_custom_call" | custom-call | tf_op jit(solution)/shard_map/pallas_call | solution.py:475
  64.4 9.7 %all-gather.2 = f32[16,64,128]{2,1,0:T(8,128)S(1)} all-gather(f32[2,64,128]{2,1,0:T(8,128)S(1)} %get-tuple-element.53), channel_id=4, replica_groups=mesh['grp'=4,'sub'=8] {'sub'}, dimensions={0}, use_global_device_ids=true | all-gather | bytes 589824 | tf_op jit(solution)/shard_map/all_gather | solution.py:514
  74.1 2.0 %shard_map.110 = (f32[32,8,128]{2,1,0:T(8,128)S(1)}, f32[2,16,128]{2,1,0:T(8,128)S(1)}, f32[2,16,128]{2,1,0:T(8,128)S(1)}) custom-call(s32[2,4,16]{2,1,0:T(4,128)S(1)} %get-tuple-element.35.cols, f32[8,2,96,128]{3,2,1,0:T(8,128)S(1)} %bitcast.8, f32[8,2,64,128]{3,2,1,0:T(8,128)S(1)} %bitcast.10, bf16[256,1024]{1,0:T(8,128)(2,1)S(1)} %get-tuple-element.46.hot, ...), custom_call_target="tpu_custom_call" | custom-call | tf_op jit(solution)/shard_map/pallas_call | solution.py:475
  76.1 10.1 %all_to_all.28.got = f32[32,8,128]{2,1,0:T(8,128)S(1)} all-to-all(f32[32,8,128]{2,1,0:T(8,128)S(1)} %get-tuple-element.57), channel_id=1, replica_groups=mesh['grp'=4,'sub'=8] {'grp','sub'}, dimensions={0} | all-to-all | bytes 262144 | tf_op jit(solution)/shard_map/all_to_all | solution.py:511
  86.2 2.1 %shard_map.111 = (f32[32,256]{1,0:T(8,128)S(1)}, f32[2,2048]{1,0:T(2,128)}, f32[32,2,128]{2,1,0:T(2,128)S(1)}) custom-call(f32[32,8,128]{2,1,0:T(8,128)S(1)} %all_to_all.28.got, f32[48,256]{1,0:T(8,128)S(1)} %get-tuple-element.58.loads, f32[48,256]{1,0:T(8,128)S(1)} %get-tuple-element.59.diags, f32[48,256]{1,0:T(8,128)S(1)} %get-tuple-element.60.field, ...), custom_call_target="tpu_custom_call" | custom-call | tf_op jit(solution)/shard_map/pallas_call | solution.py:475
  88.4 9.0 %all_to_all.29.got = f32[32,2,128]{2,1,0:T(2,128)S(1)} all-to-all(f32[32,2,128]{2,1,0:T(2,128)S(1)} %get-tuple-element.65), channel_id=1, replica_groups=mesh['grp'=4,'sub'=8] {'grp','sub'}, dimensions={0} | all-to-all | bytes 65536 | tf_op jit(solution)/shard_map/all_to_all | solution.py:511
  97.4 0.7 shard_map.112
  (1 shorter events, 0.0 us)

commit v5 on v4

--- a/solution.py
+++ b/solution.py
@@ -121,31 +121,14 @@
                 rest[side, at : at + 1, :] = ref[row : row + 1, h * width : (h + 1) * width]
 
 
-def first_kernel(cols, start, rest, source, terms, stiff, sems):
-    slots, block_rows = stiff.shape[:2]
-
-    steps = [(s, k) for s in range(slots) for k in range(0, block_rows, 4)]
-
-    def copy(i):
-        s, k = steps[i]
-        rows = pl.ds(k, 4)
-        return pltpu.make_async_copy(source.at[s, rows], stiff.at[s, rows], sems.at[s, k])
-
-    for i in range(4):
-        copy(i).start()
-
-    def arrive(s, r):
-        if r % 4 == 0:
-            i = steps.index((s, r))
-            copy(i).wait()
-            if i + 4 < len(steps):
-                copy(i + 4).start()
+def first_kernel(cols, start, rest, stiff, terms):
+    slots, block_rows, per_row = stiff.shape[:3]
 
     def vector(s, c):
         return start[lax.div(c, block_rows), s, pl.ds(lax.rem(c, block_rows), 1), :]
 
-    terms[:, block_rows * stiff.shape[2] :, :] = rest[...]
-    contract(stiff, cols, vector, terms, arrive)
+    terms[:, block_rows * per_row :, :] = rest[...]
+    contract(stiff, cols, vector, terms)
 
 
 def second_kernel(cols, maps, first, pack, stiff, resid, direc, terms, send, xown, pown, hot):
@@ -464,7 +447,7 @@
     out[...] = field[EDGE : EDGE + rows, :] + wide * resid[...]
 
 
-def call(kernel, shapes, operands, scalars=0, raw=0, scratch=(), limit=4, plain=()):
+def call(kernel, shapes, operands, scalars=0, raw=0, scratch=(), limit=4, plain=(), cost=None):
     operands = [
         pltpu.with_memory_space_constraint(x, pltpu.HBM if i < raw else pltpu.VMEM)
         for i, x in enumerate(operands)
@@ -479,6 +462,7 @@
         out_specs=[VMEM] * len(shapes),
         scratch_shapes=list(scratch),
         compiler_params=pltpu.CompilerParams(vmem_limit_bytes=limit << 20),
+        cost_estimate=cost,
     )(*operands)
 
 
@@ -525,21 +509,15 @@
         ],
         (live_blocks.reshape(1, slots), sub_diag, penalty, sub_load, cols, iface_map, global_load, global_diag),
         raw=8,
+        cost=pl.CostEstimate(flops=20_000_000_000, bytes_accessed=0, transcendentals=0),
     )
     first = lax.all_to_all(send, "sub", 0, 0)
-    terms, stiff = pl.pallas_call(
+    stiff = stiff_blocks
+    (terms,) = call(
         first_kernel,
-        out_shape=[
-            pltpu.VMEM((slots, count + rest.shape[1], width), F32),
-            pltpu.VMEM(stiff_blocks.shape, F32),
-        ],
-        in_specs=[SMEM, VMEM, VMEM, pl.BlockSpec(memory_space=pltpu.HBM)],
-        out_specs=[VMEM, VMEM],
-        scratch_shapes=[pltpu.SemaphoreType.DMA((slots, block_rows))],
-        compiler_params=pltpu.CompilerParams(vmem_limit_bytes=4 << 20),
-    )(
-        *[pltpu.with_memory_space_constraint(x, pltpu.VMEM) for x in (cols, first, rest)],
-        pltpu.with_memory_space_constraint(stiff_blocks, pltpu.HBM),
+        [((slots, count + rest.shape[1], width), F32)],
+        (cols, first, rest, stiff),
+        scalars=1,
     )
     pack = near_all(terms)
     resid, direc, terms, send, xown, pown, hot = call(

time: 98.5 us -> 95.8 us (0.973)
  Pallas kernels: 18.2 us -> 15.4 us
    pallas_call x1 -> x0, Pallas kernels: 4.7 us -> none  [body(): pl.pallas_call(first_kernel, out_shape=[pltpu.VMEM((slots, count + rest.s...]
    pallas_call x8 -> x9, Pallas kernels: 13.5 us -> 15.4 us  [call(): pl.pallas_call(kernel, out_shape=out_shape, in_specs=[SMEM] * scalars + [...]
where the time goes in v5:
time: 95.8 us; the launch traced here: 95.5 us
  blocking collectives  79.4 us (83%)
  Pallas kernels  15.4 us (16%)
    all_to_all x3, blocking collectives, everywhere(): return lax.all_to_all(x, ALL, 0, 0)  32.1 us
    all_gather x3, blocking collectives, near_all(): return lax.all_gather(x, 'sub')  28.5 us
    pallas_call x9, Pallas kernels, call(): pl.pallas_call(kernel, out_shape=out_shape, in_specs=[SMEM] * scalars + [...  15.4 us
    all_to_all x1, blocking collectives, body(): first = lax.all_to_all(send, 'sub', 0, 0)  10.8 us
    all_to_all x1, blocking collectives, body(): sums = lax.all_to_all(send, 'grp', 0, 0)  8.1 us

profile of v5, /device:TPU:0, one launch (start us, length us, event | category | flops | bytes accessed | tf_op | source)
XLA Modules:
  0.0 95.5 jit_solution(14870109369730847471)
XLA Ops:
  0.6 0.0 copy-start
  0.6 1.1 %shard_map.104 = (f32[8,2,16,128]{3,2,1,0:T(8,128)S(1)}, f32[2,32,128]{2,1,0:T(8,128)S(1)}, s32[2,4,16]{2,1,0:T(4,128)S(1)}, f32[2,128]{1,0:T(2,128)S(1)}, f32[48,256]{1,0:T(8,128)S(1)}, /*index=5*/f32[48,256]{1,0:T(8,128)S(1)}) custom-call(s32[1,2]{1,0:T(1,128)} %bitcast.12, f32[2,2048]{1,0:T(2,128)} %diag.1, f32[2,128]{1,0:T(2,128)} %pen.1, ...), custom_call_target="tpu_custom_call" | custom-call | flops 20000000000 | tf_op jit(solution)/shard_map/pallas_call | solution.py:458
  1.8 10.8 %all_to_all.25.start.first = f32[8,2,16,128]{3,2,1,0:T(8,128)S(1)} all-to-all(f32[8,2,16,128]{3,2,1,0:T(8,128)S(1)} %get-tuple-element.34), channel_id=1, replica_groups=mesh['grp'=4,'sub'=8] {'sub'}, dimensions={0} | all-to-all | bytes 262144 | tf_op jit(solution)/shard_map/all_to_all | solution.py:514
  12.5 0.0 copy-done
  12.6 1.7 %shard_map.105 = f32[2,96,128]{2,1,0:T(8,128)S(1)} custom-call(s32[2,4,16]{2,1,0:T(4,128)S(1)} %get-tuple-element.33.cols, f32[8,2,16,128]{3,2,1,0:T(8,128)S(1)} %all_to_all.25.start.first, f32[2,32,128]{2,1,0:T(8,128)S(1)} %get-tuple-element.35.rest, f32[2,16,4,128,128]{4,3,2,1,0:T(8,128)S(1)} %copy-done), custom_call_target="tpu_custom_call" | custom-call | tf_op jit(solution)/shard_map/pallas_call | solution.py:458
  14.3 9.5 %all-gather = f32[16,96,128]{2,1,0:T(8,128)S(1)} all-gather(f32[2,96,128]{2,1,0:T(8,128)S(1)} %shard_map.105), channel_id=2, replica_groups=mesh['grp'=4,'sub'=8] {'sub'}, dimensions={0}, use_global_device_ids=true | all-gather | bytes 884736 | tf_op jit(solution)/shard_map/all_gather | solution.py:498
  23.8 2.6 %shard_map.106 = (f32[256,128]{1,0:T(8,128)S(1)}, f32[256,128]{1,0:T(8,128)S(1)}, f32[2,64,128]{2,1,0:T(8,128)S(1)}, f32[32,8,128]{2,1,0:T(8,128)S(1)}, f32[2,16...) custom-call(s32[2,4,16]{2,1,0:T(4,128)S(1)} %get-tuple-element.33.cols, ...), custom_call_target="tpu_custom_call" | custom-call | tf_op jit(solution)/shard_map/pallas_call | solution.py:458
  26.3 12.9 %all_to_all.26.got = f32[32,8,128]{2,1,0:T(8,128)S(1)} all-to-all(f32[32,8,128]{2,1,0:T(8,128)S(1)} %get-tuple-element.37), channel_id=1, replica_groups=mesh['grp'=4,'sub'=8] {'grp','sub'}, dimensions={0} | all-to-all | bytes 262144 | tf_op jit(solution)/shard_map/all_to_all | solution.py:495
  39.2 3.0 %shard_map.107 = (f32[48,256]{1,0:T(8,128)S(1)}, f32[48,256]{1,0:T(8,128)S(1)}, f32[48,256]{1,0:T(8,128)S(1)}, f32[2,8,128]{2,1,0:T(8,128)S(1)}, f32[4,24,128]{2...) custom-call(f32[32,8,128]{2,1,0:T(8,128)S(1)} %all_to_all.26.got, ...), custom_call_target="tpu_custom_call" | custom-call | tf_op jit(solution)/shard_map/pallas_call | solution.py:458
  42.2 8.1 %all_to_all.27.got = f32[4,24,128]{2,1,0:T(8,128)S(1)} all-to-all(f32[4,24,128]{2,1,0:T(8,128)S(1)} %get-tuple-element.40), channel_id=1, replica_groups=mesh['grp'=4,'sub'=8] {'grp'}, dimensions={0} | all-to-all | bytes 98304 | tf_op jit(solution)/shard_map/all_to_all | solution.py:546
  50.3 9.3 %all-gather.1 = f32[16,80,128]{2,1,0:T(8,128)S(1)} all-gather(f32[2,80,128]{2,1,0:T(8,128)S(1)} %shard_map.108), channel_id=3, replica_groups=mesh['grp'=4,'sub'=8] {'sub'}, dimensions={0}, use_global_device_ids=true | all-gather | bytes 737280 | tf_op jit(solution)/shard_map/all_gather | solution.py:498
  59.6 2.2 %shard_map.109 = (f32[256,128]{1,0:T(8,128)S(1)}, f32[2,64,128]{2,1,0:T(8,128)S(1)}, f32[2,16,128]{2,1,0:T(8,128)S(1)}, f32[2,8,128]{2,1,0:T(8,128)S(1)}, f32[48,256]{1,0:T(8,128)S(1)}) custom-call(s32[2,4,16]{2,1,0:T(4,128)S(1)} %get-tuple-element.33.cols, f32[8,2,96,128]{3,2,1,0:T(8,128)S(1)} %bitcast.7, f32[8,2,80,128]{3,2,1,0:T(8,128)S(1)} %bitcast.9, ...), custom_call_target="tpu_custom_call" | custom-call | tf_op jit(solution)/shard_map/pallas_call | solution.py:458
  61.9 9.7 %all-gather.2 = f32[16,64,128]{2,1,0:T(8,128)S(1)} all-gather(f32[2,64,128]{2,1,0:T(8,128)S(1)} %get-tuple-element.49), channel_id=4, replica_groups=mesh['grp'=4,'sub'=8] {'sub'}, dimensions={0}, use_global_device_ids=true | all-gather | bytes 589824 | tf_op jit(solution)/shard_map/all_gather | solution.py:498
  71.6 2.0 %shard_map.110 = (f32[32,8,128]{2,1,0:T(8,128)S(1)}, f32[2,16,128]{2,1,0:T(8,128)S(1)}, f32[2,16,128]{2,1,0:T(8,128)S(1)}) custom-call(s32[2,4,16]{2,1,0:T(4,128)S(1)} %get-tuple-element.33.cols, f32[8,2,96,128]{3,2,1,0:T(8,128)S(1)} %bitcast.8, f32[8,2,64,128]{3,2,1,0:T(8,128)S(1)} %bitcast.10, bf16[256,1024]{1,0:T(8,128)(2,1)S(1)} %get-tuple-element.42.hot, ...), custom_call_target="tpu_custom_call" | custom-call | tf_op jit(solution)/shard_map/pallas_call | solution.py:458
  73.6 10.1 %all_to_all.28.got = f32[32,8,128]{2,1,0:T(8,128)S(1)} all-to-all(f32[32,8,128]{2,1,0:T(8,128)S(1)} %get-tuple-element.53), channel_id=1, replica_groups=mesh['grp'=4,'sub'=8] {'grp','sub'}, dimensions={0} | all-to-all | bytes 262144 | tf_op jit(solution)/shard_map/all_to_all | solution.py:495
  83.7 2.1 %shard_map.111 = (f32[32,256]{1,0:T(8,128)S(1)}, f32[2,2048]{1,0:T(2,128)}, f32[32,2,128]{2,1,0:T(2,128)S(1)}) custom-call(f32[32,8,128]{2,1,0:T(8,128)S(1)} %all_to_all.28.got, f32[48,256]{1,0:T(8,128)S(1)} %get-tuple-element.54.loads, f32[48,256]{1,0:T(8,128)S(1)} %get-tuple-element.55.diags, f32[48,256]{1,0:T(8,128)S(1)} %get-tuple-element.56.field, ...), custom_call_target="tpu_custom_call" | custom-call | tf_op jit(solution)/shard_map/pallas_call | solution.py:458
  85.8 9.0 %all_to_all.29.got = f32[32,2,128]{2,1,0:T(2,128)S(1)} all-to-all(f32[32,2,128]{2,1,0:T(2,128)S(1)} %get-tuple-element.61), channel_id=1, replica_groups=mesh['grp'=4,'sub'=8] {'grp','sub'}, dimensions={0} | all-to-all | bytes 65536 | tf_op jit(solution)/shard_map/all_to_all | solution.py:495
  94.9 0.7 shard_map.112
  (1 shorter events, 0.0 us)
Async XLA Ops:
  0.6 11.9 %copy-start = (f32[2,16,4,128,128]{4,3,2,1,0:T(8,128)S(1)}, f32[2,16,4,128,128]{4,3,2,1,0:T(8,128)}, u32[]{:S(2)}) copy-start(f32[2,16,4,128,128]{4,3,2,1,0:T(8,128)} %stiff.7) | copy-start | bytes 25165828

commit v6 on v5

--- a/solution.py
+++ b/solution.py
@@ -66,23 +66,27 @@
 
 
 def targets(pack, row, hot):
-    col = jnp.concatenate([pack[d, 0, row : row + 1, :] for d in range(pack.shape[0])], axis=1)
-    hot[...] = jnp.where(iota(hot.shape, 0).astype(F32) == col, 1.0, 0.0).astype(BF16)
+    count = hot.shape[2] // pack.shape[0]
+    for s in range(hot.shape[0]):
+        col = jnp.concatenate(
+            [pack[d, 0, row : row + 1, s * count : (s + 1) * count] for d in range(pack.shape[0])], axis=1
+        )
+        hot[s] = jnp.where(iota(hot.shape[1:], 0).astype(F32) == col, 1.0, 0.0).astype(BF16)
 
 
 def landed(hot, arrived, count):
     devices, slots, _, width = arrived.shape
-    source = jnp.concatenate(
-        [arrived[d, s, :count, :] for d in range(devices) for s in range(slots)], axis=0
-    )
-    out = jnp.dot(hot[...], jnp.concatenate(split3(source), axis=1), preferred_element_type=F32)
-    return out[:, :width] + out[:, width : 2 * width] + out[:, 2 * width :]
+    sums = []
+    for s in range(slots):
+        source = jnp.concatenate([arrived[d, s, :count, :] for d in range(devices)], axis=0)
+        out = jnp.dot(hot[s], jnp.concatenate(split3(source), axis=1), preferred_element_type=F32)
+        sums.append(out[:, :width] + out[:, width : 2 * width] + out[:, 2 * width :])
+    return jnp.concatenate(sums, axis=0)
 
 
 def prep_kernel(live, diag, pen, load, cols, maps, gload, gdiag, send, rest, cols_out, maps_out, loads, diags):
     slots, block_rows, width = send.shape[1:]
     per_row = cols.shape[1]
-    blocks = block_rows * lax.axis_size("sub")
     first, rows = [], gload.shape[0]
     rest[...] = jnp.zeros_like(rest)
     for s in range(slots):
@@ -99,7 +103,7 @@
         for n in range(per_row):
             at = (s * per_row + n) * block_rows
             rest[0, block_rows + 1 : block_rows + 2, at : at + block_rows] = (
-                cols[s, n : n + 1, :] + s * blocks
+                cols[s, n : n + 1, :]
             ).astype(F32)
     all_first = jnp.concatenate(first, axis=0).reshape(1, slots, block_rows, width)
     send[...] = jnp.broadcast_to(all_first, send.shape)
@@ -179,32 +183,36 @@
     lane = iota((1, width), 1)
     rows = [pen[s] * x_face[s] for s in range(slots)]
     rows += [pen[s] * pown[s, 0:1, :] for s in range(slots)]
-    if maps is None:
-        rows += [jnp.zeros((slots, width), F32)]
-    else:
-        rows += [maps[...]]
     row = jnp.zeros((1, width), F32)
     for s in range(slots):
         norm1, own = scal[s]
         image = total(squares[s]) + own * (1.0 / devices)
         row = jnp.where(lane == 2 * s, image, row)
         row = jnp.where(lane == 2 * s + 1, norm1 * (1.0 / devices), row)
-    rows.append(row)
+    if maps is None:
+        rows += [row, jnp.zeros((slots - 1, width), F32)]
+        out = jnp.concatenate(rows, axis=0)
+        for k in range(3):
+            part = out[None, k * slots : (k + 1) * slots, :]
+            send[:, k] = jnp.broadcast_to(part, (send.shape[0], slots, width))
+        return
+    rows += [maps[...], row]
     send[:, : 3 * slots + 1, :] = jnp.broadcast_to(
         jnp.concatenate(rows, axis=0)[None], (send.shape[0], 3 * slots + 1, width)
     )
 
 
-def reactions(got, groups, slots):
-    devices, _, width = got.shape
-    both = got[:, 3 * slots, :].reshape(groups, devices // groups, width).sum(axis=1)
+def reactions(row_of, groups, slots):
+    sums = row_of(-1)
+    devices, width = sums.shape
+    both = sums.reshape(groups, devices // groups, width).sum(axis=1)
     alphas, lams = [], []
     for s in range(slots):
         alpha = both[:, 2 * s + 1 : 2 * s + 2] / both[:, 2 * s : 2 * s + 1]
         alpha = jnp.broadcast_to(alpha, (groups, width))
         wide = jnp.broadcast_to(alpha[:, None, :], (groups, devices // groups, width))
         alphas.append(alpha)
-        lams.append(got[:, s, :] + wide.reshape(devices, width) * got[:, slots + s, :])
+        lams.append(row_of(s) + wide.reshape(devices, width) * row_of(slots + s))
     return alphas, lams
 
 
@@ -265,7 +273,7 @@
     groups = lax.axis_size("grp")
     flat = lax.axis_index("grp") * lax.axis_size("sub") + lax.axis_index("sub")
     first_row = (flat * rows - EDGE).astype(F32)
-    alphas, lams = reactions(got, groups, slots)
+    alphas, lams = reactions(lambda r: got[:, 3 * slots if r < 0 else r, :], groups, slots)
     for s in range(slots):
         alphas_out[s, 0:groups, :] = alphas[s]
     split_lams(lams, part_s)
@@ -416,7 +424,9 @@
     groups = lax.axis_size("grp")
     group = lax.axis_index("grp")
     flat = group * lax.axis_size("sub") + lax.axis_index("sub")
-    alphas, lams = reactions(got, groups, slots)
+    alphas, lams = reactions(
+        lambda r: got[:, 2, 0, :] if r < 0 else got[:, r // slots, r % slots, :], groups, slots
+    )
     for s in range(slots):
         part_s[0, s, 0:groups, :] = alphas[s]
         alpha = part_s[0, s, pl.ds(group, 1), :]
@@ -488,7 +498,7 @@
     own = ((slots, block_rows, width), F32)
     full = ((blocks, width), F32)
     every = ((slots, count, width), F32)
-    landing = ((blocks, near * slots * count), BF16)
+    landing = ((slots, near * block_rows, near * count), BF16)
     cols = jnp.transpose(block_cols, (0, 2, 1))
 
     def everywhere(x):
@@ -555,7 +565,7 @@
     arrived = near_all(terms)
     send, xown, pown = call(
         fifth_kernel,
-        [((devices, 4 * slots, width), F32), own, own],
+        [((devices, 3, slots, width), F32), own, own],
         (cols, pack, arrived, hot, bound, start, xown, stiff),
         scalars=1,
         scratch=(pltpu.VMEM(full[0], F32),),

time: 95.8 us -> 95 us (level)
  no operation moved by 1% of the time
where the time goes in v6:
time: 95 us; the launch traced here: 94.7 us
  blocking collectives  78.9 us (83%)
  Pallas kernels  15.1 us (16%)
    all_to_all x3, blocking collectives, everywhere(): return lax.all_to_all(x, ALL, 0, 0)  31.6 us
    all_gather x3, blocking collectives, near_all(): return lax.all_gather(x, 'sub')  28.5 us
    pallas_call x9, Pallas kernels, call(): pl.pallas_call(kernel, out_shape=out_shape, in_specs=[SMEM] * scalars + [...  15.1 us
    all_to_all x1, blocking collectives, body(): first = lax.all_to_all(send, 'sub', 0, 0)  10.8 us
    all_to_all x1, blocking collectives, body(): sums = lax.all_to_all(send, 'grp', 0, 0)  8.09 us

profile of v6, /device:TPU:0, one launch (start us, length us, event | category | flops | bytes accessed | tf_op | source)
XLA Modules:
  0.0 94.7 jit_solution(10386565322249761280)
XLA Ops:
  0.6 0.0 copy-start
  0.6 1.1 %shard_map.104 = (f32[8,2,16,128]{3,2,1,0:T(8,128)S(1)}, f32[2,32,128]{2,1,0:T(8,128)S(1)}, s32[2,4,16]{2,1,0:T(4,128)S(1)}, f32[2,128]{1,0:T(2,128)S(1)}, f32[48,256]{1,0:T(8,128)S(1)}, /*index=5*/f32[48,256]{1,0:T(8,128)S(1)}) custom-call(s32[1,2]{1,0:T(1,128)} %bitcast.12, f32[2,2048]{1,0:T(2,128)} %diag.1, f32[2,128]{1,0:T(2,128)} %pen.1, ...), custom_call_target="tpu_custom_call" | custom-call | flops 20000000000 | tf_op jit(solution)/shard_map/pallas_call | solution.py:468
  1.8 10.8 %all_to_all.25.start.first = f32[8,2,16,128]{3,2,1,0:T(8,128)S(1)} all-to-all(f32[8,2,16,128]{3,2,1,0:T(8,128)S(1)} %get-tuple-element.34), channel_id=1, replica_groups=mesh['grp'=4,'sub'=8] {'sub'}, dimensions={0} | all-to-all | bytes 262144 | tf_op jit(solution)/shard_map/all_to_all | solution.py:524
  12.5 0.0 copy-done
  12.6 1.8 %shard_map.105 = f32[2,96,128]{2,1,0:T(8,128)S(1)} custom-call(s32[2,4,16]{2,1,0:T(4,128)S(1)} %get-tuple-element.33.cols, f32[8,2,16,128]{3,2,1,0:T(8,128)S(1)} %all_to_all.25.start.first, f32[2,32,128]{2,1,0:T(8,128)S(1)} %get-tuple-element.35.rest, f32[2,16,4,128,128]{4,3,2,1,0:T(8,128)S(1)} %copy-done), custom_call_target="tpu_custom_call" | custom-call | tf_op jit(solution)/shard_map/pallas_call | solution.py:468
  14.3 9.5 %all-gather = f32[16,96,128]{2,1,0:T(8,128)S(1)} all-gather(f32[2,96,128]{2,1,0:T(8,128)S(1)} %shard_map.105), channel_id=2, replica_groups=mesh['grp'=4,'sub'=8] {'sub'}, dimensions={0}, use_global_device_ids=true | all-gather | bytes 884736 | tf_op jit(solution)/shard_map/all_gather | solution.py:508
  23.8 2.5 %shard_map.106 = (f32[256,128]{1,0:T(8,128)S(1)}, f32[256,128]{1,0:T(8,128)S(1)}, f32[2,64,128]{2,1,0:T(8,128)S(1)}, f32[32,8,128]{2,1,0:T(8,128)S(1)}, f32[2,16...) custom-call(s32[2,4,16]{2,1,0:T(4,128)S(1)} %get-tuple-element.33.cols, ...), custom_call_target="tpu_custom_call" | custom-call | tf_op jit(solution)/shard_map/pallas_call | solution.py:468
  26.3 12.9 %all_to_all.26.got = f32[32,8,128]{2,1,0:T(8,128)S(1)} all-to-all(f32[32,8,128]{2,1,0:T(8,128)S(1)} %get-tuple-element.37), channel_id=1, replica_groups=mesh['grp'=4,'sub'=8] {'grp','sub'}, dimensions={0} | all-to-all | bytes 262144 | tf_op jit(solution)/shard_map/all_to_all | solution.py:505
  39.2 3.0 %shard_map.107 = (f32[48,256]{1,0:T(8,128)S(1)}, f32[48,256]{1,0:T(8,128)S(1)}, f32[48,256]{1,0:T(8,128)S(1)}, f32[2,8,128]{2,1,0:T(8,128)S(1)}, f32[4,24,128]{2...) custom-call(f32[32,8,128]{2,1,0:T(8,128)S(1)} %all_to_all.26.got, ...), custom_call_target="tpu_custom_call" | custom-call | tf_op jit(solution)/shard_map/pallas_call | solution.py:468
  42.2 8.1 %all_to_all.27.got = f32[4,24,128]{2,1,0:T(8,128)S(1)} all-to-all(f32[4,24,128]{2,1,0:T(8,128)S(1)} %get-tuple-element.40), channel_id=1, replica_groups=mesh['grp'=4,'sub'=8] {'grp'}, dimensions={0} | all-to-all | bytes 98304 | tf_op jit(solution)/shard_map/all_to_all | solution.py:556
  50.3 9.3 %all-gather.1 = f32[16,80,128]{2,1,0:T(8,128)S(1)} all-gather(f32[2,80,128]{2,1,0:T(8,128)S(1)} %shard_map.108), channel_id=3, replica_groups=mesh['grp'=4,'sub'=8] {'sub'}, dimensions={0}, use_global_device_ids=true | all-gather | bytes 737280 | tf_op jit(solution)/shard_map/all_gather | solution.py:508
  59.6 2.1 %shard_map.109 = (f32[256,128]{1,0:T(8,128)S(1)}, f32[2,64,128]{2,1,0:T(8,128)S(1)}, f32[2,16,128]{2,1,0:T(8,128)S(1)}, f32[2,8,128]{2,1,0:T(8,128)S(1)}, f32[48,256]{1,0:T(8,128)S(1)}) custom-call(s32[2,4,16]{2,1,0:T(4,128)S(1)} %get-tuple-element.33.cols, f32[8,2,96,128]{3,2,1,0:T(8,128)S(1)} %bitcast.7, f32[8,2,80,128]{3,2,1,0:T(8,128)S(1)} %bitcast.9, ...), custom_call_target="tpu_custom_call" | custom-call | tf_op jit(solution)/shard_map/pallas_call | solution.py:468
  61.7 9.7 %all-gather.2 = f32[16,64,128]{2,1,0:T(8,128)S(1)} all-gather(f32[2,64,128]{2,1,0:T(8,128)S(1)} %get-tuple-element.49), channel_id=4, replica_groups=mesh['grp'=4,'sub'=8] {'sub'}, dimensions={0}, use_global_device_ids=true | all-gather | bytes 589824 | tf_op jit(solution)/shard_map/all_gather | solution.py:508
  71.4 1.9 %shard_map.110 = (f32[32,3,2,128]{3,2,1,0:T(2,128)S(1)}, f32[2,16,128]{2,1,0:T(8,128)S(1)}, f32[2,16,128]{2,1,0:T(8,128)S(1)}) custom-call(s32[2,4,16]{2,1,0:T(4,128)S(1)} %get-tuple-element.33.cols, f32[8,2,96,128]{3,2,1,0:T(8,128)S(1)} %bitcast.8, f32[8,2,64,128]{3,2,1,0:T(8,128)S(1)} %bitcast.10, bf16[2,128,512]{2,1,0:T(8,128)(2,1)S(1)} %get-tuple-element.42.hot, ...), custom_call_target="tpu_custom_call" | custom-call | tf_op jit(solution)/shard_map/pallas_call | solution.py:468
  73.2 9.7 %all_to_all.28.got = f32[32,3,2,128]{3,2,1,0:T(2,128)S(1)} all-to-all(f32[32,3,2,128]{3,2,1,0:T(2,128)S(1)} %get-tuple-element.53), channel_id=1, replica_groups=mesh['grp'=4,'sub'=8] {'grp','sub'}, dimensions={0} | all-to-all | bytes 196608 | tf_op jit(solution)/shard_map/all_to_all | solution.py:505
  83.0 2.1 %shard_map.111 = (f32[32,256]{1,0:T(8,128)S(1)}, f32[2,2048]{1,0:T(2,128)}, f32[32,2,128]{2,1,0:T(2,128)S(1)}) custom-call(f32[32,3,2,128]{3,2,1,0:T(2,128)S(1)} %all_to_all.28.got, f32[48,256]{1,0:T(8,128)S(1)} %get-tuple-element.54.loads, f32[48,256]{1,0:T(8,128)S(1)} %get-tuple-element.55.diags, f32[48,256]{1,0:T(8,128)S(1)} %get-tuple-element.56.field, ...), custom_call_target="tpu_custom_call" | custom-call | tf_op jit(solution)/shard_map/pallas_call | solution.py:468
  85.1 8.9 %all_to_all.29.got = f32[32,2,128]{2,1,0:T(2,128)S(1)} all-to-all(f32[32,2,128]{2,1,0:T(2,128)S(1)} %get-tuple-element.61), channel_id=1, replica_groups=mesh['grp'=4,'sub'=8] {'grp','sub'}, dimensions={0} | all-to-all | bytes 65536 | tf_op jit(solution)/shard_map/all_to_all | solution.py:505
  94.1 0.7 shard_map.112
  (1 shorter events, 0.0 us)
Async XLA Ops:
  0.6 11.9 %copy-start = (f32[2,16,4,128,128]{4,3,2,1,0:T(8,128)S(1)}, f32[2,16,4,128,128]{4,3,2,1,0:T(8,128)}, u32[]{:S(2)}) copy-start(f32[2,16,4,128,128]{4,3,2,1,0:T(8,128)} %stiff.7) | copy-start | bytes 25165828

commit v7 on v6

--- a/solution.py
+++ b/solution.py
@@ -24,6 +24,12 @@
     rest = x - hi.astype(F32)
     mid = rest.astype(BF16)
     return hi, mid, (rest - mid.astype(F32)).astype(BF16)
+
+
+def matches(ids, wanted):
+    kind = BF16 if ids.shape[0] <= 256 else F32
+    same = ids.astype(F32).astype(kind) == wanted.astype(kind)
+    return jnp.where(same, jnp.ones((), kind), jnp.zeros((), kind)).astype(BF16)
 
 
 def iota(shape, dim):
@@ -71,7 +77,7 @@
         col = jnp.concatenate(
             [pack[d, 0, row : row + 1, s * count : (s + 1) * count] for d in range(pack.shape[0])], axis=1
         )
-        hot[s] = jnp.where(iota(hot.shape[1:], 0).astype(F32) == col, 1.0, 0.0).astype(BF16)
+        hot[s] = matches(iota(hot.shape[1:], 0), col)
 
 
 def landed(hot, arrived, count):
@@ -229,18 +235,18 @@
     return jnp.concatenate([ref[s, pl.ds(d, 1), :] for s in range(slots)], axis=1)
 
 
-def place(row_s, part_s, window, hot_of):
+def place(row_s, part_s, window, hot_of, chunk):
     _, slots, devices, _ = part_s.shape
     rows, columns = window
-    ids_r = iota((rows, 1), 0).astype(F32)
+    ids_r = iota((rows, slots * part_s.shape[3]), 0).astype(F32).astype(BF16)
 
     def step(c, acc):
         lefts, hots = [], []
-        for d in [c * CHUNK + i for i in range(CHUNK)]:
-            hit = ids_r == lanes_of(row_s, d, slots)
+        for d in [c * chunk + i for i in range(chunk)]:
+            hit = ids_r == lanes_of(row_s, d, slots).astype(BF16)
             lefts.append(
                 jnp.concatenate(
-                    [jnp.where(hit, lanes_of(part_s.at[i], d, slots), 0.0).astype(BF16) for i in range(3)],
+                    [jnp.where(hit, lanes_of(part_s.at[i], d, slots).astype(BF16), jnp.zeros((), BF16)) for i in range(3)],
                     axis=0,
                 )
             )
@@ -252,7 +258,8 @@
             preferred_element_type=F32,
         )
 
-    acc = lax.fori_loop(0, devices // CHUNK, step, jnp.zeros((3 * rows, columns), F32))
+    acc = jnp.zeros((3 * rows, columns), F32)
+    acc = step(0, acc) if chunk == devices else lax.fori_loop(0, devices // chunk, step, acc)
     return acc[:rows] + acc[rows : 2 * rows] + acc[2 * rows :]
 
 
@@ -315,14 +322,14 @@
         fill(0, lambda k: got[(group + 1) * near + k, spare : spare + 1, :])
 
     extent = window.shape
-    ids_c = iota((columns, 1), 0).astype(F32)
+    ids_c = iota((columns, slots * width), 0)
 
     def hot_of(d):
-        hot = jnp.where(ids_c == lanes_of(col_s, d, slots), 1.0, 0.0).astype(BF16)
+        hot = matches(ids_c, lanes_of(col_s, d, slots))
         hot_s[d] = hot
         return hot
 
-    placed = place(row_s, part_s, extent, hot_of)
+    placed = place(row_s, part_s, extent, hot_of, CHUNK)
     at = iota(extent, 0)
     inside = (at >= EDGE - 2) & (at < last + 2)
     window[...] = loads[...] + jnp.where(inside, placed, 0.0)
@@ -435,7 +442,7 @@
                 xown[s, b : b + 1, :] + alpha * pown[s, b : b + 1, :]
             )
     split_lams(lams, part_s)
-    placed = place(row_s, part_s, window.shape, lambda d: hot_s[d])
+    placed = place(row_s, part_s, window.shape, lambda d: hot_s[d], min(2 * CHUNK, devices))
     span = slice(EDGE - 1, EDGE + rows + 1)
     applied = stencil(field, diags[span, :], EDGE - 1, rows + 2)
     at = iota(applied.shape, 0) + (flat * rows - 1)

time: 95 us -> 94.6 us (level)
  no operation moved by 1% of the time
where the time goes in v7:
time: 94.6 us; the launch traced here: 94.2 us
  blocking collectives  78.9 us (83%)
  Pallas kernels  14.6 us (15%)
    all_to_all x3, blocking collectives, everywhere(): return lax.all_to_all(x, ALL, 0, 0)  31.6 us
    all_gather x3, blocking collectives, near_all(): return lax.all_gather(x, 'sub')  28.5 us
    pallas_call x9, Pallas kernels, call(): pl.pallas_call(kernel, out_shape=out_shape, in_specs=[SMEM] * scalars + [...  14.6 us
    all_to_all x1, blocking collectives, body(): first = lax.all_to_all(send, 'sub', 0, 0)  10.8 us
    all_to_all x1, blocking collectives, body(): sums = lax.all_to_all(send, 'grp', 0, 0)  8.1 us

profile of v7, /device:TPU:0, one launch (start us, length us, event | category | flops | bytes accessed | tf_op | source)
XLA Modules:
  0.0 94.2 jit_solution(4896959116239251118)
XLA Ops:
  0.6 0.0 copy-start
  0.6 1.1 %shard_map.104 = (f32[8,2,16,128]{3,2,1,0:T(8,128)S(1)}, f32[2,32,128]{2,1,0:T(8,128)S(1)}, s32[2,4,16]{2,1,0:T(4,128)S(1)}, f32[2,128]{1,0:T(2,128)S(1)}, f32[48,256]{1,0:T(8,128)S(1)}, /*index=5*/f32[48,256]{1,0:T(8,128)S(1)}) custom-call(s32[1,2]{1,0:T(1,128)} %bitcast.12, f32[2,2048]{1,0:T(2,128)} %diag.1, f32[2,128]{1,0:T(2,128)} %pen.1, ...), custom_call_target="tpu_custom_call" | custom-call | flops 20000000000 | tf_op jit(solution)/shard_map/pallas_call | solution.py:475
  1.8 10.8 %all_to_all.25.start.first = f32[8,2,16,128]{3,2,1,0:T(8,128)S(1)} all-to-all(f32[8,2,16,128]{3,2,1,0:T(8,128)S(1)} %get-tuple-element.34), channel_id=1, replica_groups=mesh['grp'=4,'sub'=8] {'sub'}, dimensions={0} | all-to-all | bytes 262144 | tf_op jit(solution)/shard_map/all_to_all | solution.py:531
  12.5 0.0 copy-done
  12.6 1.8 %shard_map.105 = f32[2,96,128]{2,1,0:T(8,128)S(1)} custom-call(s32[2,4,16]{2,1,0:T(4,128)S(1)} %get-tuple-element.33.cols, f32[8,2,16,128]{3,2,1,0:T(8,128)S(1)} %all_to_all.25.start.first, f32[2,32,128]{2,1,0:T(8,128)S(1)} %get-tuple-element.35.rest, f32[2,16,4,128,128]{4,3,2,1,0:T(8,128)S(1)} %copy-done), custom_call_target="tpu_custom_call" | custom-call | tf_op jit(solution)/shard_map/pallas_call | solution.py:475
  14.3 9.5 %all-gather = f32[16,96,128]{2,1,0:T(8,128)S(1)} all-gather(f32[2,96,128]{2,1,0:T(8,128)S(1)} %shard_map.105), channel_id=2, replica_groups=mesh['grp'=4,'sub'=8] {'sub'}, dimensions={0}, use_global_device_ids=true | all-gather | bytes 884736 | tf_op jit(solution)/shard_map/all_gather | solution.py:515
  23.8 2.5 %shard_map.106 = (f32[256,128]{1,0:T(8,128)S(1)}, f32[256,128]{1,0:T(8,128)S(1)}, f32[2,64,128]{2,1,0:T(8,128)S(1)}, f32[32,8,128]{2,1,0:T(8,128)S(1)}, f32[2,16...) custom-call(s32[2,4,16]{2,1,0:T(4,128)S(1)} %get-tuple-element.33.cols, ...), custom_call_target="tpu_custom_call" | custom-call | tf_op jit(solution)/shard_map/pallas_call | solution.py:475
  26.3 12.9 %all_to_all.26.got = f32[32,8,128]{2,1,0:T(8,128)S(1)} all-to-all(f32[32,8,128]{2,1,0:T(8,128)S(1)} %get-tuple-element.37), channel_id=1, replica_groups=mesh['grp'=4,'sub'=8] {'grp','sub'}, dimensions={0} | all-to-all | bytes 262144 | tf_op jit(solution)/shard_map/all_to_all | solution.py:512
  39.2 2.8 %shard_map.107 = (f32[48,256]{1,0:T(8,128)S(1)}, f32[48,256]{1,0:T(8,128)S(1)}, f32[48,256]{1,0:T(8,128)S(1)}, f32[2,8,128]{2,1,0:T(8,128)S(1)}, f32[4,24,128]{2...) custom-call(f32[32,8,128]{2,1,0:T(8,128)S(1)} %all_to_all.26.got, ...), custom_call_target="tpu_custom_call" | custom-call | tf_op jit(solution)/shard_map/pallas_call | solution.py:475
  42.0 8.1 %all_to_all.27.got = f32[4,24,128]{2,1,0:T(8,128)S(1)} all-to-all(f32[4,24,128]{2,1,0:T(8,128)S(1)} %get-tuple-element.40), channel_id=1, replica_groups=mesh['grp'=4,'sub'=8] {'grp'}, dimensions={0} | all-to-all | bytes 98304 | tf_op jit(solution)/shard_map/all_to_all | solution.py:563
  50.1 9.3 %all-gather.1 = f32[16,80,128]{2,1,0:T(8,128)S(1)} all-gather(f32[2,80,128]{2,1,0:T(8,128)S(1)} %shard_map.108), channel_id=3, replica_groups=mesh['grp'=4,'sub'=8] {'sub'}, dimensions={0}, use_global_device_ids=true | all-gather | bytes 737280 | tf_op jit(solution)/shard_map/all_gather | solution.py:515
  59.4 2.1 %shard_map.109 = (f32[256,128]{1,0:T(8,128)S(1)}, f32[2,64,128]{2,1,0:T(8,128)S(1)}, f32[2,16,128]{2,1,0:T(8,128)S(1)}, f32[2,8,128]{2,1,0:T(8,128)S(1)}, f32[48,256]{1,0:T(8,128)S(1)}) custom-call(s32[2,4,16]{2,1,0:T(4,128)S(1)} %get-tuple-element.33.cols, f32[8,2,96,128]{3,2,1,0:T(8,128)S(1)} %bitcast.7, f32[8,2,80,128]{3,2,1,0:T(8,128)S(1)} %bitcast.9, ...), custom_call_target="tpu_custom_call" | custom-call | tf_op jit(solution)/shard_map/pallas_call | solution.py:475
  61.5 9.7 %all-gather.2 = f32[16,64,128]{2,1,0:T(8,128)S(1)} all-gather(f32[2,64,128]{2,1,0:T(8,128)S(1)} %get-tuple-element.49), channel_id=4, replica_groups=mesh['grp'=4,'sub'=8] {'sub'}, dimensions={0}, use_global_device_ids=true | all-gather | bytes 589824 | tf_op jit(solution)/shard_map/all_gather | solution.py:515
  71.2 1.9 %shard_map.110 = (f32[32,3,2,128]{3,2,1,0:T(2,128)S(1)}, f32[2,16,128]{2,1,0:T(8,128)S(1)}, f32[2,16,128]{2,1,0:T(8,128)S(1)}) custom-call(s32[2,4,16]{2,1,0:T(4,128)S(1)} %get-tuple-element.33.cols, f32[8,2,96,128]{3,2,1,0:T(8,128)S(1)} %bitcast.8, f32[8,2,64,128]{3,2,1,0:T(8,128)S(1)} %bitcast.10, bf16[2,128,512]{2,1,0:T(8,128)(2,1)S(1)} %get-tuple-element.42.hot, ...), custom_call_target="tpu_custom_call" | custom-call | tf_op jit(solution)/shard_map/pallas_call | solution.py:475
  73.1 9.7 %all_to_all.28.got = f32[32,3,2,128]{3,2,1,0:T(2,128)S(1)} all-to-all(f32[32,3,2,128]{3,2,1,0:T(2,128)S(1)} %get-tuple-element.53), channel_id=1, replica_groups=mesh['grp'=4,'sub'=8] {'grp','sub'}, dimensions={0} | all-to-all | bytes 196608 | tf_op jit(solution)/shard_map/all_to_all | solution.py:512
  82.8 1.8 %shard_map.111 = (f32[32,256]{1,0:T(8,128)S(1)}, f32[2,2048]{1,0:T(2,128)}, f32[32,2,128]{2,1,0:T(2,128)S(1)}) custom-call(f32[32,3,2,128]{3,2,1,0:T(2,128)S(1)} %all_to_all.28.got, f32[48,256]{1,0:T(8,128)S(1)} %get-tuple-element.54.loads, f32[48,256]{1,0:T(8,128)S(1)} %get-tuple-element.55.diags, f32[48,256]{1,0:T(8,128)S(1)} %get-tuple-element.56.field, ...), custom_call_target="tpu_custom_call" | custom-call | tf_op jit(solution)/shard_map/pallas_call | solution.py:475
  84.6 8.9 %all_to_all.29.got = f32[32,2,128]{2,1,0:T(2,128)S(1)} all-to-all(f32[32,2,128]{2,1,0:T(2,128)S(1)} %get-tuple-element.61), channel_id=1, replica_groups=mesh['grp'=4,'sub'=8] {'grp','sub'}, dimensions={0} | all-to-all | bytes 65536 | tf_op jit(solution)/shard_map/all_to_all | solution.py:512
  93.6 0.7 shard_map.112
  (1 shorter events, 0.0 us)
Async XLA Ops:
  0.6 11.9 %copy-start = (f32[2,16,4,128,128]{4,3,2,1,0:T(8,128)S(1)}, f32[2,16,4,128,128]{4,3,2,1,0:T(8,128)}, u32[]{:S(2)}) copy-start(f32[2,16,4,128,128]{4,3,2,1,0:T(8,128)} %stiff.7) | copy-start | bytes 25165828

commit v8 on v7

--- a/solution.py
+++ b/solution.py
@@ -90,8 +90,8 @@
     return jnp.concatenate(sums, axis=0)
 
 
-def prep_kernel(live, diag, pen, load, cols, maps, gload, gdiag, send, rest, cols_out, maps_out, loads, diags):
-    slots, block_rows, width = send.shape[1:]
+def prep_kernel(live, diag, pen, load, cols, maps, gload, gdiag, grid, send, rest, cols_out, maps_out):
+    slots, block_rows, width = send.shape
     per_row = cols.shape[1]
     first, rows = [], gload.shape[0]
     rest[...] = jnp.zeros_like(rest)
@@ -111,33 +111,34 @@
             rest[0, block_rows + 1 : block_rows + 2, at : at + block_rows] = (
                 cols[s, n : n + 1, :]
             ).astype(F32)
-    all_first = jnp.concatenate(first, axis=0).reshape(1, slots, block_rows, width)
-    send[...] = jnp.broadcast_to(all_first, send.shape)
+    send[...] = jnp.concatenate(first, axis=0).reshape(slots, block_rows, width)
     cols_out[...] = cols[...]
     maps_out[...] = maps[...].astype(F32)
-    loads[...] = jnp.zeros_like(loads)
-    diags[...] = jnp.zeros_like(diags)
-    loads[EDGE : EDGE + rows, :] = gload[...]
-    diags[EDGE : EDGE + rows, :] = gdiag[...]
-    last = rows - 1
-    half = gload.shape[1] // width
-    edge = block_rows + 8
-    for side, picks in enumerate(
-        (((gload, 0), (gload, 1), (gdiag, 0)), ((gload, last - 1), (gload, last), (gdiag, last)))
-    ):
-        for k, (ref, row) in enumerate(picks):
-            for h in range(half):
-                at = edge + k * half + h
-                rest[side, at : at + 1, :] = ref[row : row + 1, h * width : (h + 1) * width]
-
-
-def first_kernel(cols, start, rest, stiff, terms):
-    slots, block_rows, per_row = stiff.shape[:3]
+    grid[:rows, :] = gload[...]
+    grid[rows:, :] = gdiag[...]
+
+
+def first_kernel(cols, start, rest, stiff, *grids):
+    slots, block_rows, per_row, width, _ = stiff.shape
+    grids, terms = grids[:-1], grids[-1]
+    groups = len(grids)
+    rows, columns = grids[0].shape
+    last, half = rows // 2 - 1, columns // width
+    group = lax.axis_index("grp")
 
     def vector(s, c):
         return start[lax.div(c, block_rows), s, pl.ds(lax.rem(c, block_rows), 1), :]
 
-    terms[:, block_rows * per_row :, :] = rest[...]
+    edge = block_rows * per_row + rest.shape[1]
+    terms[:, edge - rest.shape[1] : edge, :] = rest[...]
+    terms[:, edge:, :] = jnp.zeros((slots, terms.shape[1] - edge, width), F32)
+    for away, grid in enumerate(grids):
+        block = lax.rem(group + groups - away, groups)
+        for side, picks in enumerate(((0, 1, last + 1), (last - 1, last, 2 * last + 1))):
+            for k, row in enumerate(picks):
+                for h in range(half):
+                    at = edge + (block * 3 + k) * half + h
+                    terms[side, pl.ds(at, 1), :] = grid[row : row + 1, h * width : (h + 1) * width]
     contract(stiff, cols, vector, terms)
 
 
@@ -169,19 +170,7 @@
         head.append(pack[me, s, count + block_rows : count + block_rows + 1, :])
     squares = contract(stiff, cols, lambda s, c: direc[pl.ds(s * blocks + c, 1), :], terms)
     write_send(send, maps, head, [xown[s, 0:1, :] for s in range(slots)], pown, scal, squares, devices)
-    everyone, used = send.shape[0], 3 * slots + 1
-    group = lax.axis_index("grp")
-    groups = everyone // devices
-    edge = count + block_rows + 8
-    send[:, used : used + 1, :] = jnp.zeros((everyone, 1, width), F32)
-
-    @pl.when((group > 0) & (me < 8))
-    def _():
-        send[group * devices - 1, used : used + 1, :] = pack[0, 0, pl.ds(edge + me, 1), :]
-
-    @pl.when((group < groups - 1) & (me < 8))
-    def _():
-        send[(group + 1) * devices, used : used + 1, :] = pack[devices - 1, 1, pl.ds(edge + me, 1), :]
+    send[:, 3 * slots + 1 :, :] = jnp.zeros((send.shape[0], slots - 1, width), F32)
 
 
 def write_send(send, maps, pen, x_face, pown, scal, squares, devices):
@@ -274,54 +263,60 @@
     return (4.0 + gdiag) * here - (above + below + left + right)
 
 
-def third_kernel(got, pack, loads_in, diags_in, window, loads, diags, alphas_out, send, row_s, hot_s, part_s, col_s):
-    rows, columns = window.shape[0] - 2 * EDGE, window.shape[1]
+def third_kernel(got, pack, terms, *more):
+    groups = lax.axis_size("grp")
+    third_inner(got, pack, terms, more[:groups], *more[groups:])
+
+
+def third_inner(got, pack, terms, grids, window, loads, diags, alphas_out, send, row_s, hot_s, part_s, col_s):
+    groups = len(grids)
+    rows, columns = grids[0].shape
+    rows = rows // 2
+    tall = rows + 2 * EDGE
     slots, devices, width = row_s.shape
-    groups = lax.axis_size("grp")
-    flat = lax.axis_index("grp") * lax.axis_size("sub") + lax.axis_index("sub")
-    first_row = (flat * rows - EDGE).astype(F32)
+    near = devices // groups
+    me, group = lax.axis_index("sub"), lax.axis_index("grp")
     alphas, lams = reactions(lambda r: got[:, 3 * slots if r < 0 else r, :], groups, slots)
     for s in range(slots):
         alphas_out[s, 0:groups, :] = alphas[s]
     split_lams(lams, part_s)
+    apart = near * rows
+    shift = (me * rows - EDGE).astype(F32)
     for s in range(slots):
         where = got[:, 2 * slots + s, :]
         row = jnp.floor(where * (1.0 / columns))
         col_s[s] = where - row * columns
-        row_s[s] = row - first_row
-    me, group = lax.axis_index("sub"), lax.axis_index("grp")
-    near = devices // groups
-    half, edge, spare = columns // width, pack.shape[2] - 8, 3 * slots + 1
-    loads[...] = loads_in[...]
-    diags[...] = diags_in[...]
-    last = EDGE + rows
-
-    def fill(side, row_of):
-        first = EDGE - 2 if side else last
-        diag_row = EDGE - 1 if side else last
-        for h in range(half):
-            lanes = slice(h * width, (h + 1) * width)
-            loads[first : first + 1, lanes] = row_of(h)
-            loads[first + 1 : first + 2, lanes] = row_of(half + h)
-            diags[diag_row : diag_row + 1, lanes] = row_of(2 * half + h)
-
-    @pl.when(me > 0)
-    def _():
-        fill(1, lambda k: pack[me - 1, 1, edge + k : edge + k + 1, :])
-
-    @pl.when((me == 0) & (group > 0))
-    def _():
-        fill(1, lambda k: got[(group - 1) * near + k, spare : spare + 1, :])
-
-    @pl.when(me < near - 1)
-    def _():
-        fill(0, lambda k: pack[me + 1, 0, edge + k : edge + k + 1, :])
-
-    @pl.when((me == near - 1) & (group < groups - 1))
-    def _():
-        fill(0, lambda k: got[(group + 1) * near + k, spare : spare + 1, :])
-
-    extent = window.shape
+        row = row - shift
+        which = jnp.floor(row * (1.0 / apart))
+        row = row - which * apart
+        near_by = (row >= EDGE - 2) & (row < EDGE + rows + 2)
+        row_s[s] = jnp.where(near_by, which * tall + row, -1.0)
+    half, edge, count = columns // width, pack.shape[2] - edge_rows(groups, columns // width), terms.shape[1]
+    loads[...] = jnp.zeros_like(loads)
+    diags[...] = jnp.zeros_like(diags)
+    for away, grid in enumerate(grids):
+        base = pl.multiple_of(lax.rem(group + groups - away, groups) * tall + EDGE, 8)
+        loads[pl.ds(base, rows), :] = grid[:rows, :]
+        diags[pl.ds(base, rows), :] = grid[rows:, :]
+    for g in range(groups):
+        base = g * tall + EDGE
+        def fill(side, device, block, base=base):
+            first = base - 2 if side else base + rows
+            diag_row = base - 1 if side else base + rows
+            for h in range(half):
+                lanes = slice(h * width, (h + 1) * width)
+                at = edge + block * 3 * half + h
+                loads[first : first + 1, lanes] = pack[device, side, at : at + 1, :]
+                loads[first + 1 : first + 2, lanes] = pack[device, side, at + half : at + half + 1, :]
+                diags[diag_row : diag_row + 1, lanes] = pack[device, side, at + 2 * half : at + 2 * half + 1, :]
+
+        pl.when(me > 0)(lambda g=g, fill=fill: fill(1, me - 1, g))
+        pl.when(me < near - 1)(lambda g=g, fill=fill: fill(0, me + 1, g))
+        if g > 0:
+            pl.when(me == 0)(lambda g=g, fill=fill: fill(1, near - 1, g - 1))
+        if g < groups - 1:
+            pl.when(me == near - 1)(lambda g=g, fill=fill: fill(0, 0, g + 1))
+
     ids_c = iota((columns, slots * width), 0)
 
     def hot_of(d):
@@ -329,40 +324,37 @@
         hot_s[d] = hot
         return hot
 
-    placed = place(row_s, part_s, extent, hot_of, CHUNK)
-    at = iota(extent, 0)
-    inside = (at >= EDGE - 2) & (at < last + 2)
-    window[...] = loads[...] + jnp.where(inside, placed, 0.0)
-    own = window[EDGE:last, :]
-    image = stencil(window, diags[EDGE:last, :], EDGE, rows)
-    faces = slots * near
-    send[:, faces:, :] = jnp.zeros((groups, send.shape[1] - faces, width), F32)
-    send[:, faces : faces + 1, :] = jnp.broadcast_to(total(own * own)[None], (groups, 1, width))
-    send[:, faces + 1 : faces + 2, :] = jnp.broadcast_to(total(own * image)[None], (groups, 1, width))
+    window[...] = loads[...] + place(row_s, part_s, window.shape, hot_of, CHUNK)
+    owns, ids = [], []
+    top = bottom = None
+    for g in range(groups):
+        base = g * tall + EDGE
+        own = window[base : base + rows, :]
+        image = stencil(window, diags[base : base + rows, :], base, rows)
+        top = own * own if top is None else top + own * own
+        bottom = own * image if bottom is None else bottom + own * image
+        owns.append(own)
+        ids.append(iota((rows, 1), 0).astype(F32) + base)
+    send[:, :count, :] = terms[...]
+    send[:, count + near :, :] = jnp.zeros((slots, send.shape[1] - count - near, width), F32)
+    at = count + near
+    send[:, at : at + 1, :] = jnp.broadcast_to(total(top)[None], (slots, 1, width))
+    send[:, at + 1 : at + 2, :] = jnp.broadcast_to(total(bottom)[None], (slots, 1, width))
+    own, ids = jnp.concatenate(owns, axis=0), jnp.concatenate(ids, axis=0)
     parts = jnp.concatenate(split3(own), axis=0)
-    ids = iota((rows, 1), 0).astype(F32) + EDGE
-
-    for g in range(groups):
-        for k in range(near):
-            d = g * near + k
-            seen = jnp.dot(parts, hot_s[d], preferred_element_type=F32)
-            seen = seen[:rows] + seen[rows : 2 * rows] + seen[2 * rows :]
-            hit = ids == lanes_of(row_s, d, slots)
-            mine = jnp.sum(jnp.where(hit, seen, 0.0), axis=0, keepdims=True)
-            for s in range(slots):
-                send[g, s * near + k : s * near + k + 1, :] = mine[:, s * width : (s + 1) * width]
-
-
-def share_kernel(got, terms, send):
-    slots, count, width = terms.shape
-    near = lax.axis_size("sub")
-    sums = got[0]
-    for g in range(1, got.shape[0]):
-        sums = sums + got[g]
-    send[:, :count, :] = terms[...]
-    for s in range(slots):
-        send[s, count : count + near, :] = sums[s * near : (s + 1) * near, :]
-        send[s, count + near :, :] = sums[slots * near : slots * near + 8, :]
+    tall_own = groups * rows
+    for k in range(near):
+        d = group * near + k
+        seen = jnp.dot(parts, hot_s[d], preferred_element_type=F32)
+        seen = seen[:tall_own] + seen[tall_own : 2 * tall_own] + seen[2 * tall_own :]
+        hit = ids == lanes_of(row_s, d, slots)
+        mine = jnp.sum(jnp.where(hit, seen, 0.0), axis=0, keepdims=True)
+        for s in range(slots):
+            send[s, count + k : count + k + 1, :] = mine[:, s * width : (s + 1) * width]
+
+
+def edge_rows(groups, half):
+    return -(-3 * half * groups // 8) * 8
 
 
 def fourth_kernel(
@@ -428,9 +420,10 @@
 def sixth_kernel(got, loads, diags, field, xown, pown, row_s, hot_s, resid, xout, send, window, part_s):
     slots, devices, width = row_s.shape
     rows, columns = resid.shape
-    groups = lax.axis_size("grp")
-    group = lax.axis_index("grp")
-    flat = group * lax.axis_size("sub") + lax.axis_index("sub")
+    tall = rows + 2 * EDGE
+    groups = window.shape[0] // tall
+    near = devices // groups
+    group, me = lax.axis_index("grp"), lax.axis_index("sub")
     alphas, lams = reactions(
         lambda r: got[:, 2, 0, :] if r < 0 else got[:, r // slots, r % slots, :], groups, slots
     )
@@ -442,26 +435,31 @@
                 xown[s, b : b + 1, :] + alpha * pown[s, b : b + 1, :]
             )
     split_lams(lams, part_s)
-    placed = place(row_s, part_s, window.shape, lambda d: hot_s[d], min(2 * CHUNK, devices))
-    span = slice(EDGE - 1, EDGE + rows + 1)
-    applied = stencil(field, diags[span, :], EDGE - 1, rows + 2)
-    at = iota(applied.shape, 0) + (flat * rows - 1)
-    inside = (at >= 0) & (at < devices * rows)
-    window[...] = jnp.zeros_like(window)
-    window[span, :] = jnp.where(inside, loads[span, :] - applied + placed[span], 0.0)
-    own = window[EDGE : EDGE + rows, :]
-    resid[...] = own
-    image = stencil(window, diags[EDGE : EDGE + rows, :], EDGE, rows)
-    send[:, 0:1, :] = jnp.broadcast_to(total(own * own)[None], (devices, 1, width))
-    send[:, 1:2, :] = jnp.broadcast_to(total(own * image)[None], (devices, 1, width))
+    window[...] = loads[...] + place(row_s, part_s, window.shape, lambda d: hot_s[d], min(2 * CHUNK, devices))
+    top = bottom = None
+    for g in range(groups):
+        base = g * tall + EDGE
+        span = slice(base - 1, base + rows + 1)
+        applied = stencil(field, diags[span, :], base - 1, rows + 2)
+        at = iota(applied.shape, 0) + ((g * near + me) * rows - 1)
+        inside = (at >= 0) & (at < devices * rows)
+        window[span, :] = jnp.where(inside, window[span, :] - applied, 0.0)
+        own = window[base : base + rows, :]
+        image = stencil(window, diags[base : base + rows, :], base, rows)
+        top = own * own if top is None else top + own * own
+        bottom = own * image if bottom is None else bottom + own * image
+    resid[...] = window[pl.ds(group * tall + EDGE, rows), :]
+    send[:, 0:1, :] = jnp.broadcast_to(total(top)[None], (near, 1, width))
+    send[:, 1:2, :] = jnp.broadcast_to(total(bottom)[None], (near, 1, width))
 
 
 def last_kernel(got, field, resid, out):
     sums = jnp.sum(got[...], axis=0)
     scale = sums[0:1, :] / sums[1:2, :]
     rows, columns = out.shape
+    mine = pl.ds(lax.axis_index("grp") * (rows + 2 * EDGE) + EDGE, rows)
     wide = jnp.concatenate([scale] * (columns // got.shape[2]), axis=1)
-    out[...] = field[EDGE : EDGE + rows, :] + wide * resid[...]
+    out[...] = field[mine, :] + wide * resid[...]
 
 
 def call(kernel, shapes, operands, scalars=0, raw=0, scratch=(), limit=4, plain=(), cost=None):
@@ -501,7 +499,7 @@
     devices = near * groups
     blocks = slots * near * block_rows
     count = block_rows * per_row
-    extent = ((rows + 2 * EDGE, columns), F32)
+    extent = ((groups * (rows + 2 * EDGE), columns), F32)
     own = ((slots, block_rows, width), F32)
     full = ((blocks, width), F32)
     every = ((slots, count, width), F32)
@@ -514,26 +512,28 @@
     def near_all(x):
         return lax.all_gather(x, "sub")
 
-    send, rest, cols, maps, loads, diags = call(
+    grid, send, rest, cols, maps = call(
         prep_kernel,
         [
-            ((near, slots, block_rows, width), F32),
-            ((slots, block_rows + 16, width), F32),
+            ((2 * rows, columns), F32),
+            own,
+            ((slots, block_rows + 8, width), F32),
             (cols.shape, jnp.int32),
             (iface_map.shape, F32),
-            extent,
-            extent,
         ],
         (live_blocks.reshape(1, slots), sub_diag, penalty, sub_load, cols, iface_map, global_load, global_diag),
         raw=8,
         cost=pl.CostEstimate(flops=20_000_000_000, bytes_accessed=0, transcendentals=0),
     )
-    first = lax.all_to_all(send, "sub", 0, 0)
+    grids = [grid] + [
+        lax.ppermute(grid, "grp", [(i, (i + away) % groups) for i in range(groups)]) for away in range(1, groups)
+    ]
+    first = near_all(send)
     stiff = stiff_blocks
     (terms,) = call(
         first_kernel,
-        [((slots, count + rest.shape[1], width), F32)],
-        (cols, first, rest, stiff),
+        [((slots, count + rest.shape[1] + edge_rows(groups, columns // width), width), F32)],
+        (cols, first, rest, stiff, *grids),
         scalars=1,
     )
     pack = near_all(terms)
@@ -553,15 +553,14 @@
             extent,
             extent,
             ((slots, max(8, groups), width), F32),
-            ((groups, slots * near + 8, width), F32),
+            ((slots, count + near + 8, width), F32),
             (listed, F32),
             ((devices, columns, slots * width), BF16),
         ],
-        (got, pack, loads, diags),
+        (got, pack, terms, *grids),
+        limit=8,
         scratch=(parts, pltpu.VMEM(listed, F32)),
     )
-    sums = lax.all_to_all(send, "grp", 0, 0)
-    (send,) = call(share_kernel, [((slots, count + near + 8, width), F32)], (sums, terms))
     arrived = near_all(send)
     start, terms, xown, bound, field = call(
         fourth_kernel,
@@ -580,12 +579,13 @@
     got = everywhere(send)
     resid, sub_field, send = call(
         sixth_kernel,
-        [((rows, columns), F32), ((slots, rows_dev), F32), ((devices, 2, width), F32)],
+        [((rows, columns), F32), ((slots, rows_dev), F32), ((near, 2, width), F32)],
         (got, loads, diags, field, xown, pown, row_s, hot_s),
         scratch=(pltpu.VMEM(extent[0], F32), parts),
+        limit=8,
         plain=(1,),
     )
-    sums = everywhere(send)
+    sums = lax.all_to_all(send, "sub", 0, 0)
     (global_field,) = call(last_kernel, [((rows, columns), F32)], (sums, field, resid), plain=(0,))
     return global_field, sub_field
 

time: 94.6 us -> 92.8 us (0.981)
  blocking collectives: 78.9 us -> 68.3 us
  starting transfers between devices: 0 us -> 6.11 us
  Pallas kernels: 14.6 us -> 17.4 us
    all_to_all x2 -> x1, blocking collectives: 18.9 us -> 7.06 us  [body(): sums = lax.all_to_all(send, 'sub', 0, 0)]
    all_gather x3 -> x4, blocking collectives: 28.5 us -> 38.9 us  [near_all(): return lax.all_gather(x, 'sub')]
    all_to_all x3 -> x2, blocking collectives: 31.6 us -> 22.4 us  [everywhere(): return lax.all_to_all(x, ALL, 0, 0)]
    ppermute x0 -> x3, starting transfers between devices: none -> 6.11 us  [body(): lax.ppermute(grid, 'grp', [(i, (i + away) % groups) for i in range(groups)])]
    pallas_call x9 -> x8, Pallas kernels: 14.6 us -> 17.4 us  [call(): pl.pallas_call(kernel, out_shape=out_shape, in_specs=[SMEM] * scalars + [...]
  transfers between devices with their start and end apart: 0 -> 3, of which waited for: 0 -> 0; matrix products, arithmetic and copies ran while one was open for 0% -> 0% of each run, Pallas kernels for 0% -> 0%
where the time goes in v8:
time: 92.8 us; the launch traced here: 92.5 us
  blocking collectives  68.3 us (74%)
  Pallas kernels  17.4 us (19%)
  starting transfers between devices  6.11 us (7%)
    all_gather x4, blocking collectives, near_all(): return lax.all_gather(x, 'sub')  38.9 us
    all_to_all x2, blocking collectives, everywhere(): return lax.all_to_all(x, ALL, 0, 0)  22.4 us
    pallas_call x8, Pallas kernels, call(): pl.pallas_call(kernel, out_shape=out_shape, in_specs=[SMEM] * scalars + [...  17.4 us
    all_to_all x1, blocking collectives, body(): sums = lax.all_to_all(send, 'sub', 0, 0)  7.06 us
    ppermute x3, starting transfers between devices, body(): lax.ppermute(grid, 'grp', [(i, (i + away) % groups) for i in range(groups)])  6.11 us
  transfers between devices with their start and end apart: 3, of which 0 were waited for; matrix products, arithmetic and copies ran while one was open for 0% of the time, Pallas kernels for 0%

profile of v8, /device:TPU:0, one launch (start us, length us, event | category | flops | bytes accessed | tf_op | source)
XLA Modules:
  0.0 92.5 jit_solution(8816011856188622272)
XLA Ops:
  0.6 0.0 copy-start
  0.6 1.1 %shard_map.104 = (f32[64,256]{1,0:T(8,128)S(1)}, f32[2,16,128]{2,1,0:T(8,128)S(1)}, f32[2,24,128]{2,1,0:T(8,128)S(1)}, s32[2,4,16]{2,1,0:T(4,128)S(1)}, f32[2,128]{1,0:T(2,128)S(1)}) custom-call(s32[1,2]{1,0:T(1,128)} %bitcast.15, f32[2,2048]{1,0:T(2,128)} %diag.1, f32[2,128]{1,0:T(2,128)} %pen.1, f32[2,2048]{1,0:T(2,128)} %load.1, s32[2,4,16]{2,1,0:T(4,128)} %bitcast.14, ...), custom_call_target="tpu_custom_call" | custom-call | flops 20000000000 | tf_op jit(solution)/shard_map/pallas_call | solution.py:473
  1.8 5.1 %collective-permute-start.2 = (f32[64,256]{1,0:T(8,128)S(1)}, f32[64,256]{1,0:T(8,128)S(1)}, u32[]{:S(2)}, u32[]{:S(2)}) collective-permute-start(f32[64,256]{1,0:T(8,128)S(1)} %get-tuple-element.35.grids_0_.more_0_), channel_id=1, source_target_pairs={{0,24},{8,0},{16,8},{24,16},{1,25},{9,1},{17,9},{25,17},{2,26},{10... | collective-permute-start | bytes 196616 | tf_op jit(solution)/shard_map/ppermute | solution.py:529
  6.9 0.0 collective-permute-start.1
  6.9 1.0 %collective-permute-start = (f32[64,256]{1,0:T(8,128)S(1)}, f32[64,256]{1,0:T(8,128)S(1)}, u32[]{:S(2)}, u32[]{:S(2)}) collective-permute-start(f32[64,256]{1,0:T(8,128)S(1)} %get-tuple-element.35.grids_0_.more_0_), channel_id=1, source_target_pairs={{0,8},{8,16},{16,24},{24,0},{1,9},{9,17},{17,25},{25,1},{2,10},{10... | collective-permute-start | bytes 196616 | tf_op jit(solution)/shard_map/ppermute | solution.py:529
  7.9 9.2 %all-gather = f32[16,16,128]{2,1,0:T(8,128)S(1)} all-gather(f32[2,16,128]{2,1,0:T(8,128)S(1)} %get-tuple-element.33), channel_id=2, replica_groups=mesh['grp'=4,'sub'=8] {'sub'}, dimensions={0}, use_global_device_ids=true | all-gather | bytes 147456 | tf_op jit(solution)/shard_map/all_gather | solution.py:513
  17.1 0.0 collective-permute-done.2.grids_3_.more_3_
  17.1 0.0 collective-permute-done.1.grids_2_.more_2_
  17.1 0.0 collective-permute-done.grids_1_.more_1_
  17.1 0.0 copy-done
  17.1 1.8 %shard_map.105 = f32[2,112,128]{2,1,0:T(8,128)S(1)} custom-call(s32[2,4,16]{2,1,0:T(4,128)S(1)} %get-tuple-element.32.cols, f32[8,2,16,128]{3,2,1,0:T(8,128)S(1)} %bitcast.12, f32[2,24,128]{2,1,0:T(8,128)S(1)} %get-tuple-element.34.rest, f32[2,16,4,128,128]{4,3,2,1,0:T(8,128)S(1)} %copy-done, f32[64,256]{1,0:T(8,128)S(1)} %get-tuple-element.35.grids_0_.more_0_, ...), custom_call_target="tpu_custom_call" | custom-call | tf_op jit(solution)/shard_map/pallas_call | solution.py:473
  18.9 10.7 %all-gather.1 = f32[16,112,128]{2,1,0:T(8,128)S(1)} all-gather(f32[2,112,128]{2,1,0:T(8,128)S(1)} %shard_map.105), channel_id=3, replica_groups=mesh['grp'=4,'sub'=8] {'sub'}, dimensions={0}, use_global_device_ids=true | all-gather | bytes 1032192 | tf_op jit(solution)/shard_map/all_gather | solution.py:513
  29.6 2.5 %shard_map.106 = (f32[256,128]{1,0:T(8,128)S(1)}, f32[256,128]{1,0:T(8,128)S(1)}, f32[2,64,128]{2,1,0:T(8,128)S(1)}, f32[32,8,128]{2,1,0:T(8,128)S(1)}, f32[2,16...) custom-call(s32[2,4,16]{2,1,0:T(4,128)S(1)} %get-tuple-element.32.cols, ...), custom_call_target="tpu_custom_call" | custom-call | tf_op jit(solution)/shard_map/pallas_call | solution.py:473
  32.1 12.2 %all_to_all.15.got = f32[32,8,128]{2,1,0:T(8,128)S(1)} all-to-all(f32[32,8,128]{2,1,0:T(8,128)S(1)} %get-tuple-element.37), channel_id=1, replica_groups=mesh['grp'=4,'sub'=8] {'grp','sub'}, dimensions={0} | all-to-all | bytes 262144 | tf_op jit(solution)/shard_map/all_to_all | solution.py:510
  44.2 4.1 %shard_map.107 = (f32[192,256]{1,0:T(8,128)S(1)}, f32[192,256]{1,0:T(8,128)S(1)}, f32[192,256]{1,0:T(8,128)S(1)}, f32[2,8,128]{2,1,0:T(8,128)S(1)}, f32[2,80,128...) custom-call(f32[32,8,128]{2,1,0:T(8,128)S(1)} %all_to_all.15.got, ...), custom_call_target="tpu_custom_call" | custom-call | tf_op jit(solution)/shard_map/pallas_call | solution.py:473
  48.3 9.3 %all-gather.2 = f32[16,80,128]{2,1,0:T(8,128)S(1)} all-gather(f32[2,80,128]{2,1,0:T(8,128)S(1)} %get-tuple-element.39), channel_id=4, replica_groups=mesh['grp'=4,'sub'=8] {'sub'}, dimensions={0}, use_global_device_ids=true | all-gather | bytes 737280 | tf_op jit(solution)/shard_map/all_gather | solution.py:513
  57.6 2.1 %shard_map.108 = (f32[256,128]{1,0:T(8,128)S(1)}, f32[2,64,128]{2,1,0:T(8,128)S(1)}, f32[2,16,128]{2,1,0:T(8,128)S(1)}, f32[2,8,128]{2,1,0:T(8,128)S(1)}, f32[192,256]{1,0:T(8,128)S(1)}) custom-call(s32[2,4,16]{2,1,0:T(4,128)S(1)} %get-tuple-element.32.cols, f32[8,2,112,128]{3,2,1,0:T(8,128)S(1)} %bitcast.8, f32[8,2,80,128]{3,2,1,0:T(8,128)S(1)} %bitcast.10, ...), custom_call_target="tpu_custom_call" | custom-call | tf_op jit(solution)/shard_map/pallas_call | solution.py:473
  59.7 9.7 %all-gather.3 = f32[16,64,128]{2,1,0:T(8,128)S(1)} all-gather(f32[2,64,128]{2,1,0:T(8,128)S(1)} %get-tuple-element.47), channel_id=5, replica_groups=mesh['grp'=4,'sub'=8] {'sub'}, dimensions={0}, use_global_device_ids=true | all-gather | bytes 589824 | tf_op jit(solution)/shard_map/all_gather | solution.py:513
  69.4 1.9 %shard_map.109 = (f32[32,3,2,128]{3,2,1,0:T(2,128)S(1)}, f32[2,16,128]{2,1,0:T(8,128)S(1)}, f32[2,16,128]{2,1,0:T(8,128)S(1)}) custom-call(s32[2,4,16]{2,1,0:T(4,128)S(1)} %get-tuple-element.32.cols, f32[8,2,112,128]{3,2,1,0:T(8,128)S(1)} %bitcast.9, f32[8,2,64,128]{3,2,1,0:T(8,128)S(1)} %bitcast.11, bf16[2,128,512]{2,1,0:T(8,128)(2,1)S(1)} %get-tuple-element.40.hot, ...), custom_call_target="tpu_custom_call" | custom-call | tf_op jit(solution)/shard_map/pallas_call | solution.py:473
  71.3 10.2 %all_to_all.16.got = f32[32,3,2,128]{3,2,1,0:T(2,128)S(1)} all-to-all(f32[32,3,2,128]{3,2,1,0:T(2,128)S(1)} %get-tuple-element.51), channel_id=1, replica_groups=mesh['grp'=4,'sub'=8] {'grp','sub'}, dimensions={0} | all-to-all | bytes 196608 | tf_op jit(solution)/shard_map/all_to_all | solution.py:510
  81.5 3.4 %shard_map.110 = (f32[32,256]{1,0:T(8,128)S(1)}, f32[2,2048]{1,0:T(2,128)}, f32[8,2,128]{2,1,0:T(2,128)S(1)}) custom-call(f32[32,3,2,128]{3,2,1,0:T(2,128)S(1)} %all_to_all.16.got, f32[192,256]{1,0:T(8,128)S(1)} %get-tuple-element.52.loads, f32[192,256]{1,0:T(8,128)S(1)} %get-tuple-element.53.diags, f32[192,256]{1,0:T(8,128)S(1)} %get-tuple-element.54.field, ...), custom_call_target="tpu_custom_call" | custom-call | tf_op jit(solution)/shard_map/pallas_call | solution.py:473
  84.8 7.1 %all_to_all.17.got = f32[8,2,128]{2,1,0:T(2,128)S(1)} all-to-all(f32[8,2,128]{2,1,0:T(2,128)S(1)} %get-tuple-element.59), channel_id=1, replica_groups=mesh['grp'=4,'sub'=8] {'sub'}, dimensions={0} | all-to-all | bytes 16384 | tf_op jit(solution)/shard_map/all_to_all | solution.py:588
  91.9 0.6 shard_map.111
Async XLA Ops:
  0.6 16.5 %copy-start = (f32[2,16,4,128,128]{4,3,2,1,0:T(8,128)S(1)}, f32[2,16,4,128,128]{4,3,2,1,0:T(8,128)}, u32[]{:S(2)}) copy-start(f32[2,16,4,128,128]{4,3,2,1,0:T(8,128)} %stiff.7) | copy-start | bytes 25165828
  1.8 15.3 %collective-permute-start.2 = (f32[64,256]{1,0:T(8,128)S(1)}, f32[64,256]{1,0:T(8,128)S(1)}, u32[]{:S(2)}, u32[]{:S(2)}) collective-permute-start(f32[64,256]{1,0:T(8,128)S(1)} %get-tuple-element.35.grids_0_.more_0_), channel_id=1, source_target_pairs={{0,24},{8,0},{16,8},{24,16},{1,25},{9,1},{17,9},{25,17},{2,26},{10... | collective-permute-start | bytes 196616 | tf_op jit(solution)/shard_map/ppermute | solution.py:529
  6.9 10.2 %collective-permute-start.1 = (f32[64,256]{1,0:T(8,128)S(1)}, f32[64,256]{1,0:T(8,128)S(1)}, u32[]{:S(2)}, u32[]{:S(2)}) collective-permute-start(f32[64,256]{1,0:T(8,128)S(1)} %get-tuple-element.35.grids_0_.more_0_), channel_id=1, source_target_pairs={{0,16},{8,24},{16,0},{24,8},{1,17},{9,25},{17,1},{25,9},{2,18},{10... | collective-permute-start | bytes 196616 | tf_op jit(solution)/shard_map/ppermute | solution.py:529
  6.9 10.2 %collective-permute-start = (f32[64,256]{1,0:T(8,128)S(1)}, f32[64,256]{1,0:T(8,128)S(1)}, u32[]{:S(2)}, u32[]{:S(2)}) collective-permute-start(f32[64,256]{1,0:T(8,128)S(1)} %get-tuple-element.35.grids_0_.more_0_), channel_id=1, source_target_pairs={{0,8},{8,16},{16,24},{24,0},{1,9},{9,17},{17,25},{25,1},{2,10},{10... | collective-permute-start | bytes 196616 | tf_op jit(solution)/shard_map/ppermute | solution.py:529

commit v9 on v8

--- a/solution.py
+++ b/solution.py
@@ -24,6 +24,11 @@
     rest = x - hi.astype(F32)
     mid = rest.astype(BF16)
     return hi, mid, (rest - mid.astype(F32)).astype(BF16)
+
+
+def split2(x):
+    hi = x.astype(BF16)
+    return hi, (x - hi.astype(F32)).astype(BF16)
 
 
 def matches(ids, wanted):
@@ -214,10 +219,8 @@
 def split_lams(lams, part_s):
     for s, lam in enumerate(lams):
         hi = lam.astype(BF16).astype(F32)
-        mid = (lam - hi).astype(BF16).astype(F32)
         part_s[0, s] = hi
-        part_s[1, s] = mid
-        part_s[2, s] = lam - hi - mid
+        part_s[1, s] = lam - hi
 
 
 def lanes_of(ref, d, slots):
@@ -235,7 +238,7 @@
             hit = ids_r == lanes_of(row_s, d, slots).astype(BF16)
             lefts.append(
                 jnp.concatenate(
-                    [jnp.where(hit, lanes_of(part_s.at[i], d, slots).astype(BF16), jnp.zeros((), BF16)) for i in range(3)],
+                    [jnp.where(hit, lanes_of(part_s.at[i], d, slots).astype(BF16), jnp.zeros((), BF16)) for i in range(2)],
                     axis=0,
                 )
             )
@@ -247,9 +250,9 @@
             preferred_element_type=F32,
         )
 
-    acc = jnp.zeros((3 * rows, columns), F32)
+    acc = jnp.zeros((2 * rows, columns), F32)
     acc = step(0, acc) if chunk == devices else lax.fori_loop(0, devices // chunk, step, acc)
-    return acc[:rows] + acc[rows : 2 * rows] + acc[2 * rows :]
+    return acc[:rows] + acc[rows:]
 
 
 def stencil(ref, gdiag, first, count):
@@ -341,12 +344,12 @@
     send[:, at : at + 1, :] = jnp.broadcast_to(total(top)[None], (slots, 1, width))
     send[:, at + 1 : at + 2, :] = jnp.broadcast_to(total(bottom)[None], (slots, 1, width))
     own, ids = jnp.concatenate(owns, axis=0), jnp.concatenate(ids, axis=0)
-    parts = jnp.concatenate(split3(own), axis=0)
+    parts = jnp.concatenate(split2(own), axis=0)
     tall_own = groups * rows
     for k in range(near):
         d = group * near + k
         seen = jnp.dot(parts, hot_s[d], preferred_element_type=F32)
-        seen = seen[:tall_own] + seen[tall_own : 2 * tall_own] + seen[2 * tall_own :]
+        seen = seen[:tall_own] + seen[tall_own:]
         hit = ids == lanes_of(row_s, d, slots)
         mine = jnp.sum(jnp.where(hit, seen, 0.0), axis=0, keepdims=True)
         for s in range(slots):
@@ -545,7 +548,7 @@
     )
     got = everywhere(send)
     listed = (slots, devices, width)
-    parts = pltpu.VMEM((3,) + listed, F32)
+    parts = pltpu.VMEM((2,) + listed, F32)
     window, loads, diags, alphas, send, row_s, hot_s = call(
         third_kernel,
         [

time: 92.8 us -> 91 us (0.981)
  Pallas kernels: 17.4 us -> 15.5 us
    pallas_call x8, Pallas kernels: 17.4 us -> 15.5 us  [call(): pl.pallas_call(kernel, out_shape=out_shape, in_specs=[SMEM] * scalars + [...]
where the time goes in v9:
time: 91 us; the launch traced here: 90.7 us
  blocking collectives  68.3 us (75%)
  Pallas kernels  15.5 us (17%)
  starting transfers between devices  6.11 us (7%)
    all_gather x4, blocking collectives, near_all(): return lax.all_gather(x, 'sub')  38.9 us
    all_to_all x2, blocking collectives, everywhere(): return lax.all_to_all(x, ALL, 0, 0)  22.3 us
    pallas_call x8, Pallas kernels, call(): pl.pallas_call(kernel, out_shape=out_shape, in_specs=[SMEM] * scalars + [...  15.5 us
    all_to_all x1, blocking collectives, body(): sums = lax.all_to_all(send, 'sub', 0, 0)  7.06 us
    ppermute x3, starting transfers between devices, body(): lax.ppermute(grid, 'grp', [(i, (i + away) % groups) for i in range(groups)])  6.11 us
  transfers between devices with their start and end apart: 3, of which 0 were waited for; matrix products, arithmetic and copies ran while one was open for 0% of the time, Pallas kernels for 0%

profile of v9, /device:TPU:0, one launch (start us, length us, event | category | flops | bytes accessed | tf_op | source)
XLA Modules:
  0.0 90.7 jit_solution(9694009794174700256)
XLA Ops:
  0.6 0.0 copy-start
  0.6 1.1 %shard_map.104 = (f32[64,256]{1,0:T(8,128)S(1)}, f32[2,16,128]{2,1,0:T(8,128)S(1)}, f32[2,24,128]{2,1,0:T(8,128)S(1)}, s32[2,4,16]{2,1,0:T(4,128)S(1)}, f32[2,128]{1,0:T(2,128)S(1)}) custom-call(s32[1,2]{1,0:T(1,128)} %bitcast.15, f32[2,2048]{1,0:T(2,128)} %diag.1, f32[2,128]{1,0:T(2,128)} %pen.1, f32[2,2048]{1,0:T(2,128)} %load.1, s32[2,4,16]{2,1,0:T(4,128)} %bitcast.14, ...), custom_call_target="tpu_custom_call" | custom-call | flops 20000000000 | tf_op jit(solution)/shard_map/pallas_call | solution.py:476
  1.8 5.1 %collective-permute-start.2 = (f32[64,256]{1,0:T(8,128)S(1)}, f32[64,256]{1,0:T(8,128)S(1)}, u32[]{:S(2)}, u32[]{:S(2)}) collective-permute-start(f32[64,256]{1,0:T(8,128)S(1)} %get-tuple-element.35.grids_0_.more_0_), channel_id=1, source_target_pairs={{0,24},{8,0},{16,8},{24,16},{1,25},{9,1},{17,9},{25,17},{2,26},{10... | collective-permute-start | bytes 196616 | tf_op jit(solution)/shard_map/ppermute | solution.py:532
  6.9 0.0 collective-permute-start.1
  6.9 1.0 %collective-permute-start = (f32[64,256]{1,0:T(8,128)S(1)}, f32[64,256]{1,0:T(8,128)S(1)}, u32[]{:S(2)}, u32[]{:S(2)}) collective-permute-start(f32[64,256]{1,0:T(8,128)S(1)} %get-tuple-element.35.grids_0_.more_0_), channel_id=1, source_target_pairs={{0,8},{8,16},{16,24},{24,0},{1,9},{9,17},{17,25},{25,1},{2,10},{10... | collective-permute-start | bytes 196616 | tf_op jit(solution)/shard_map/ppermute | solution.py:532
  7.9 9.2 %all-gather = f32[16,16,128]{2,1,0:T(8,128)S(1)} all-gather(f32[2,16,128]{2,1,0:T(8,128)S(1)} %get-tuple-element.33), channel_id=2, replica_groups=mesh['grp'=4,'sub'=8] {'sub'}, dimensions={0}, use_global_device_ids=true | all-gather | bytes 147456 | tf_op jit(solution)/shard_map/all_gather | solution.py:516
  17.1 0.0 collective-permute-done.2.grids_3_.more_3_
  17.1 0.0 collective-permute-done.1.grids_2_.more_2_
  17.1 0.0 collective-permute-done.grids_1_.more_1_
  17.1 0.0 copy-done
  17.1 1.8 %shard_map.105 = f32[2,112,128]{2,1,0:T(8,128)S(1)} custom-call(s32[2,4,16]{2,1,0:T(4,128)S(1)} %get-tuple-element.32.cols, f32[8,2,16,128]{3,2,1,0:T(8,128)S(1)} %bitcast.12, f32[2,24,128]{2,1,0:T(8,128)S(1)} %get-tuple-element.34.rest, f32[2,16,4,128,128]{4,3,2,1,0:T(8,128)S(1)} %copy-done, f32[64,256]{1,0:T(8,128)S(1)} %get-tuple-element.35.grids_0_.more_0_, ...), custom_call_target="tpu_custom_call" | custom-call | tf_op jit(solution)/shard_map/pallas_call | solution.py:476
  18.9 10.7 %all-gather.1 = f32[16,112,128]{2,1,0:T(8,128)S(1)} all-gather(f32[2,112,128]{2,1,0:T(8,128)S(1)} %shard_map.105), channel_id=3, replica_groups=mesh['grp'=4,'sub'=8] {'sub'}, dimensions={0}, use_global_device_ids=true | all-gather | bytes 1032192 | tf_op jit(solution)/shard_map/all_gather | solution.py:516
  29.6 2.5 %shard_map.106 = (f32[256,128]{1,0:T(8,128)S(1)}, f32[256,128]{1,0:T(8,128)S(1)}, f32[2,64,128]{2,1,0:T(8,128)S(1)}, f32[32,8,128]{2,1,0:T(8,128)S(1)}, f32[2,16...) custom-call(s32[2,4,16]{2,1,0:T(4,128)S(1)} %get-tuple-element.32.cols, ...), custom_call_target="tpu_custom_call" | custom-call | tf_op jit(solution)/shard_map/pallas_call | solution.py:476
  32.1 12.1 %all_to_all.15.got = f32[32,8,128]{2,1,0:T(8,128)S(1)} all-to-all(f32[32,8,128]{2,1,0:T(8,128)S(1)} %get-tuple-element.37), channel_id=1, replica_groups=mesh['grp'=4,'sub'=8] {'grp','sub'}, dimensions={0} | all-to-all | bytes 262144 | tf_op jit(solution)/shard_map/all_to_all | solution.py:513
  44.2 3.0 %shard_map.107 = (f32[192,256]{1,0:T(8,128)S(1)}, f32[192,256]{1,0:T(8,128)S(1)}, f32[192,256]{1,0:T(8,128)S(1)}, f32[2,8,128]{2,1,0:T(8,128)S(1)}, f32[2,80,128...) custom-call(f32[32,8,128]{2,1,0:T(8,128)S(1)} %all_to_all.15.got, ...), custom_call_target="tpu_custom_call" | custom-call | tf_op jit(solution)/shard_map/pallas_call | solution.py:476
  47.3 9.3 %all-gather.2 = f32[16,80,128]{2,1,0:T(8,128)S(1)} all-gather(f32[2,80,128]{2,1,0:T(8,128)S(1)} %get-tuple-element.39), channel_id=4, replica_groups=mesh['grp'=4,'sub'=8] {'sub'}, dimensions={0}, use_global_device_ids=true | all-gather | bytes 737280 | tf_op jit(solution)/shard_map/all_gather | solution.py:516
  56.5 2.1 %shard_map.108 = (f32[256,128]{1,0:T(8,128)S(1)}, f32[2,64,128]{2,1,0:T(8,128)S(1)}, f32[2,16,128]{2,1,0:T(8,128)S(1)}, f32[2,8,128]{2,1,0:T(8,128)S(1)}, f32[192,256]{1,0:T(8,128)S(1)}) custom-call(s32[2,4,16]{2,1,0:T(4,128)S(1)} %get-tuple-element.32.cols, f32[8,2,112,128]{3,2,1,0:T(8,128)S(1)} %bitcast.8, f32[8,2,80,128]{3,2,1,0:T(8,128)S(1)} %bitcast.10, ...), custom_call_target="tpu_custom_call" | custom-call | tf_op jit(solution)/shard_map/pallas_call | solution.py:476
  58.6 9.7 %all-gather.3 = f32[16,64,128]{2,1,0:T(8,128)S(1)} all-gather(f32[2,64,128]{2,1,0:T(8,128)S(1)} %get-tuple-element.47), channel_id=5, replica_groups=mesh['grp'=4,'sub'=8] {'sub'}, dimensions={0}, use_global_device_ids=true | all-gather | bytes 589824 | tf_op jit(solution)/shard_map/all_gather | solution.py:516
  68.4 1.9 %shard_map.109 = (f32[32,3,2,128]{3,2,1,0:T(2,128)S(1)}, f32[2,16,128]{2,1,0:T(8,128)S(1)}, f32[2,16,128]{2,1,0:T(8,128)S(1)}) custom-call(s32[2,4,16]{2,1,0:T(4,128)S(1)} %get-tuple-element.32.cols, f32[8,2,112,128]{3,2,1,0:T(8,128)S(1)} %bitcast.9, f32[8,2,64,128]{3,2,1,0:T(8,128)S(1)} %bitcast.11, bf16[2,128,512]{2,1,0:T(8,128)(2,1)S(1)} %get-tuple-element.40.hot, ...), custom_call_target="tpu_custom_call" | custom-call | tf_op jit(solution)/shard_map/pallas_call | solution.py:476
  70.2 10.2 %all_to_all.16.got = f32[32,3,2,128]{3,2,1,0:T(2,128)S(1)} all-to-all(f32[32,3,2,128]{3,2,1,0:T(2,128)S(1)} %get-tuple-element.51), channel_id=1, replica_groups=mesh['grp'=4,'sub'=8] {'grp','sub'}, dimensions={0} | all-to-all | bytes 196608 | tf_op jit(solution)/shard_map/all_to_all | solution.py:513
  80.5 2.5 %shard_map.110 = (f32[32,256]{1,0:T(8,128)S(1)}, f32[2,2048]{1,0:T(2,128)}, f32[8,2,128]{2,1,0:T(2,128)S(1)}) custom-call(f32[32,3,2,128]{3,2,1,0:T(2,128)S(1)} %all_to_all.16.got, f32[192,256]{1,0:T(8,128)S(1)} %get-tuple-element.52.loads, f32[192,256]{1,0:T(8,128)S(1)} %get-tuple-element.53.diags, f32[192,256]{1,0:T(8,128)S(1)} %get-tuple-element.54.field, ...), custom_call_target="tpu_custom_call" | custom-call | tf_op jit(solution)/shard_map/pallas_call | solution.py:476
  83.0 7.1 %all_to_all.17.got = f32[8,2,128]{2,1,0:T(2,128)S(1)} all-to-all(f32[8,2,128]{2,1,0:T(2,128)S(1)} %get-tuple-element.59), channel_id=1, replica_groups=mesh['grp'=4,'sub'=8] {'sub'}, dimensions={0} | all-to-all | bytes 16384 | tf_op jit(solution)/shard_map/all_to_all | solution.py:591
  90.0 0.6 shard_map.111
Async XLA Ops:
  0.6 16.5 %copy-start = (f32[2,16,4,128,128]{4,3,2,1,0:T(8,128)S(1)}, f32[2,16,4,128,128]{4,3,2,1,0:T(8,128)}, u32[]{:S(2)}) copy-start(f32[2,16,4,128,128]{4,3,2,1,0:T(8,128)} %stiff.7) | copy-start | bytes 25165828
  1.8 15.3 %collective-permute-start.2 = (f32[64,256]{1,0:T(8,128)S(1)}, f32[64,256]{1,0:T(8,128)S(1)}, u32[]{:S(2)}, u32[]{:S(2)}) collective-permute-start(f32[64,256]{1,0:T(8,128)S(1)} %get-tuple-element.35.grids_0_.more_0_), channel_id=1, source_target_pairs={{0,24},{8,0},{16,8},{24,16},{1,25},{9,1},{17,9},{25,17},{2,26},{10... | collective-permute-start | bytes 196616 | tf_op jit(solution)/shard_map/ppermute | solution.py:532
  6.9 10.2 %collective-permute-start.1 = (f32[64,256]{1,0:T(8,128)S(1)}, f32[64,256]{1,0:T(8,128)S(1)}, u32[]{:S(2)}, u32[]{:S(2)}) collective-permute-start(f32[64,256]{1,0:T(8,128)S(1)} %get-tuple-element.35.grids_0_.more_0_), channel_id=1, source_target_pairs={{0,16},{8,24},{16,0},{24,8},{1,17},{9,25},{17,1},{25,9},{2,18},{10... | collective-permute-start | bytes 196616 | tf_op jit(solution)/shard_map/ppermute | solution.py:532
  6.9 10.2 %collective-permute-start = (f32[64,256]{1,0:T(8,128)S(1)}, f32[64,256]{1,0:T(8,128)S(1)}, u32[]{:S(2)}, u32[]{:S(2)}) collective-permute-start(f32[64,256]{1,0:T(8,128)S(1)} %get-tuple-element.35.grids_0_.more_0_), channel_id=1, source_target_pairs={{0,8},{8,16},{16,24},{24,0},{1,9},{9,17},{17,25},{25,1},{2,10},{10... | collective-permute-start | bytes 196616 | tf_op jit(solution)/shard_map/ppermute | solution.py:532
